TPU v7x, 32 devices: a whole 2x2x4 slice. The times are simulated.
32 devices in a mesh: tm: 8 (over z, x), space: 4 (over y, core).
Axes of the slice: x: 2, y: 2, z: 4, core: 2. Of those that a mesh axis runs over, the one named last changes fastest.
Arguments:
- video: bfloat16 [16, 32, 32, 384], P('tm', 'space'), may hold values from -6 to 6
- conv_weight: bfloat16 [3, 3, 3, 384, 384], replicated, may hold values from -0.0625 to 0.0625
- embed_weight: bfloat16 [384, 1152], replicated, may hold values from -0.3125 to 0.3125
- q_weight: bfloat16 [1152, 1152], replicated, may hold values from -0.1875 to 0.1875
- k_weight: bfloat16 [1152, 1152], replicated, may hold values from -0.1875 to 0.1875
- v_weight: bfloat16 [1152, 1152], replicated, may hold values from -0.1875 to 0.1875
- initial_state: float32 [16, 72, 72], P('space'), may hold values from -1536 to 1536
- probe_in: int32 [16, 32, 32, 1152], P('tm', 'space'), may hold values from -1 to 1, as said below
- probe_out: int32 [16, 32, 32, 1152], P('tm', None, None, 'space'), may hold values from -1 to 1, as said below
Outputs:
- flow: bfloat16 [16, 32, 32, 1152], P('tm', None, None, 'space')
- tangent: bfloat16 [16, 32, 32, 1152], P('tm', None, None, 'space')
- adjoint: bfloat16 [16, 32, 32, 1152], P('tm', 'space')
- state_cotangent: float32 [64, 16, 72, 72], P('tm', 'space')
Inputs may be any that keep to these rules, and one draw needn't show every extreme that they name: `probe_in`: every entry is -1 or +1. `probe_out`: every entry is -1 or +1.
All inputs are finite; a program needn't handle non-finite values.
Results may differ from a plain program's by a relative error of at most 0.012.
Values may be sent and summed in bfloat16 or wider, within the bound.
No kernel may reach another device: no remote copies, remote signals or barrier semaphores. Data moves between devices by JAX's collectives and lax.ppermute only.
A program may use at most 128 MiB of HBM per device.

v0:
```python
import functools

import jax
import jax.numpy as jnp
from jax import lax
from jax.experimental import pallas as pl
from jax.experimental.pallas import tpu as pltpu
from jax.sharding import PartitionSpec as P


D = 1152
HEADS = 16
SPAN = 256
HEAD = D // HEADS
PAIR = 2 * HEAD
F32 = jnp.float32
BF16 = jnp.bfloat16
VMEM_BYTES = 14 * 1024 * 1024


def call(body, outs, args, scratch=(), flops=0, moved=0, far=0):
    vmem = pl.BlockSpec(memory_space=pltpu.VMEM)
    anywhere = pl.BlockSpec(memory_space=pltpu.HBM)
    args = [pltpu.with_memory_space_constraint(a, pltpu.HBM) for a in args[:far]] + list(args[far:])
    return pl.pallas_call(
        body,
        in_specs=[anywhere] * far + [vmem] * (len(args) - far),
        out_specs=[vmem] * len(outs),
        out_shape=outs,
        scratch_shapes=list(scratch),
        compiler_params=pltpu.CompilerParams(vmem_limit_bytes=VMEM_BYTES),
        cost_estimate=pl.CostEstimate(flops=flops, bytes_accessed=moved, transcendentals=0),
    )(*args)


def struct(shape, dtype):
    return jax.ShapeDtypeStruct(shape, dtype)


def dot(a, b):
    return jnp.dot(a, b, preferred_element_type=F32)


def dot_nt(a, b):
    return lax.dot_general(a, b, (((1,), (1,)), ((), ())), preferred_element_type=F32)


def dot_tn(a, b):
    return lax.dot_general(a, b, (((0,), (0,)), ((), ())), preferred_element_type=F32)


def same_head():
    row = lax.broadcasted_iota(jnp.int32, (PAIR, PAIR), 0) < HEAD
    col = lax.broadcasted_iota(jnp.int32, (PAIR, PAIR), 1) < HEAD
    return row == col


def spread(packed):
    both = jnp.concatenate([packed, packed], 0)
    return jnp.where(same_head(), both, 0.0).astype(BF16)


def packed_of(square):
    col = lax.broadcasted_iota(jnp.int32, (HEAD, PAIR), 1) < HEAD
    return jnp.where(col, square[:HEAD], square[HEAD:])


def project(x, w):
    return dot(x, w).T.astype(BF16)


def mine():
    return lax.axis_index("space")


def hand_out(held, outs):
    for k, out_ref in enumerate(outs):
        out_ref[...] = held[mine() ^ k]


def take_in(parts, held):
    for k, part_ref in enumerate(parts):
        held[mine() ^ k] = part_ref[...]


def exchange(parts):
    size = lax.axis_size("space")
    got = [parts[0]]
    for k in range(1, size):
        got.append(lax.ppermute(parts[k], "space", [(i, i ^ k) for i in range(size)]))
    return got


def project_groups(x, w_ref, held):
    held[...] = project(x, w_ref[...]).reshape(held.shape)


def probe_body(x_hbm, w_hbm, taps_hbm, *rest):
    *outs, x_out, w_ref, taps_ref, x_ref, held, sems = rest
    copies = [
        pltpu.make_async_copy(source, target, sems.at[i])
        for i, (source, target) in enumerate(
            ((x_hbm, x_ref), (w_hbm, w_ref), (taps_hbm, taps_ref))
        )
    ]
    copies[0].start()
    copies[1].start()
    copies[0].wait()
    x_out[...] = x_ref[...].astype(F32).astype(BF16)
    copies[1].wait()
    copies[2].start()
    project_groups(x_out[...], w_ref, held)
    hand_out(held, outs)
    copies[2].wait()


def query_body(x_ref, w_ref, *rest):
    *outs, held = rest
    project_groups(x_ref[...], w_ref, held)
    hand_out(held, outs)


def probe_pair_body(x_ref, k_ref, v_ref, out_ref):
    out_ref[0] = project(x_ref[...], k_ref[...])
    out_ref[1] = project(x_ref[...], v_ref[...])


def flip_body(po_ref, tie_ref, out_ref):
    frames, tiles = po_ref.shape[:2]

    def flip(i, _):
        f, s = i // tiles, i % tiles
        out_ref[f, s] = po_ref[f, s].astype(F32).T.astype(BF16)
        return 0

    lax.fori_loop(0, frames * tiles, flip, 0)


def conv_body(outer, own_ref, up_ref, down_ref, w_ref, out_ref, wide):
    main, source, target = outer
    frames, tile_rows, columns, channels = own_ref.shape
    tokens = tile_rows * columns
    span = (tile_rows + 2) * columns
    column = lax.broadcasted_iota(jnp.int32, (span, channels), 0) % columns
    for f in range(frames):
        mid, top, bottom = (r[f].reshape(-1, channels) for r in (own_ref, up_ref, down_ref))
        x = jnp.concatenate([top, mid, bottom], 0).astype(F32)
        left = jnp.where(column == 0, 0.0, pltpu.roll(x, 1, 0))
        right = jnp.where(column == columns - 1, 0.0, pltpu.roll(x, span - 1, 0))
        for n, part in enumerate((left, x, right)):
            part = part.astype(BF16)
            for b in range(3):
                at = (3 * b + n) * channels
                wide[f * tokens : (f + 1) * tokens, at : at + channels] = part[
                    b * columns : b * columns + tokens
                ]
    total = dot(wide[...], w_ref[main])
    extra = dot(wide[source * tokens : (source + 1) * tokens, :], w_ref[1])
    for f in range(frames):
        part = total[f * tokens : (f + 1) * tokens]
        part = part + extra if f == target else part
        out_ref[f * tokens : (f + 1) * tokens, :] = part.astype(out_ref.dtype)


def state_body(near_ref, far_ref, embed_ref, dots, k_ref, v_ref, latent, both, *rest):
    *outs, state_ref = rest
    groups = state_ref.shape[1]
    u = near_ref[...] + far_ref[...].astype(F32)
    active = (u / (1.0 + jnp.exp(-u))).astype(BF16)
    latent[...] = dot(active, embed_ref[...]).astype(BF16)
    both[0] = project(latent[...], k_ref[...])
    both[1] = project(latent[...], v_ref[...])
    share = state_ref.shape[3] // 2

    def group(g, _):
        for half in range(share // PAIR):
            rows = pl.ds(pl.multiple_of(g * share + half * PAIR, 16), PAIR)
            blocks = []
            for f in range(2):
                at = slice(f * SPAN, (f + 1) * SPAN)
                kt, vt = both[0, rows, at], both[1, rows, at]
                state = dot_nt(vt, kt)
                moved = dot_nt(vt, dots[0, rows, at]) + dot_nt(dots[1, rows, at], kt)
                blocks.append((packed_of(state), packed_of(moved)))
            for kind in range(2):
                to = kind * share + half * PAIR
                first, second = blocks[0][kind], blocks[1][kind]
                state_ref[0, g, :, to : to + PAIR] = (first + second).astype(BF16)
                state_ref[1, g, :, to : to + PAIR] = first.astype(BF16)
        return 0

    lax.fori_loop(0, groups, group, 0)
    hand_out(state_ref.at[0], outs[:groups])
    hand_out(state_ref.at[1], outs[groups:])


def total_body(*refs):
    *parts, out_ref, sent_ref = refs
    total = sum(part[...].astype(F32) for part in parts)
    out_ref[...] = total
    sent_ref[...] = total.astype(BF16)


def prefixes(start, sums, firsts, at, held, out_ref):
    groups = len(sums)
    for k in range(groups):
        first = firsts[k][:, at].astype(F32)
        held[0, mine() ^ k] = first
        held[1, mine() ^ k] = sums[k][:, at].astype(F32) - first
    for f in range(2):
        for s in range(groups):
            start = start + held[f, s]
            out_ref[f, s] = start.astype(BF16)


def before_of(gots, forward):
    counts = lax.axis_index("tm") % 2 == (1 if forward else 0)
    first = jnp.where(counts, gots[0][...].astype(F32), 0.0)
    return first + sum(got[...].astype(F32) for got in gots[1:])


def flow_body(groups, count, *refs):
    q_parts, refs = refs[:groups], refs[groups:]
    sums, firsts, refs = refs[:groups], refs[groups : 2 * groups], refs[2 * groups :]
    gots, refs = refs[:count], refs[count:]
    init_ref, po_ref, *refs = refs
    qbar_outs, refs = refs[:groups], refs[groups:]
    q_ref, unit_ref, scale_ref, suffix_ref, sent_ref, prefix_ref, held, s_ref, carry, qbar_ref = refs
    share = q_ref.shape[1]
    frames = prefix_ref.shape[0]
    take_in(q_parts, q_ref)
    for h in range(init_ref.shape[0]):
        held[:, h * HEAD : (h + 1) * HEAD] = init_ref[h]
    before = before_of(gots, True)[:, :share]
    for p in range(share // PAIR):
        at = slice(p * PAIR, (p + 1) * PAIR)
        packed = held[:, at]
        square = jnp.where(same_head(), jnp.concatenate([packed, packed], 0), 0.0)
        held[:, at] = packed_of(square.T) + before[:, at]
    prefixes(held[...], sums, firsts, slice(0, share), s_ref, prefix_ref)
    carry[...] = jnp.zeros_like(carry)

    def frame(n, _):
        f = frames - 1 - n
        tokens = pl.ds(pl.multiple_of(f * SPAN, SPAN), SPAN)
        for s in reversed(range(groups)):
            for p in range(share // PAIR):
                at = slice(p * PAIR, (p + 1) * PAIR)
                query = q_ref[s, at, tokens]
                prefix = spread(prefix_ref[f, s, :, at].astype(F32))
                mixed = dot(prefix, query)
                bars = []
                for h in range(2):
                    rows = slice(p * PAIR + h * HEAD, p * PAIR + (h + 1) * HEAD)
                    part = mixed[h * HEAD : (h + 1) * HEAD]
                    scale = lax.rsqrt(jnp.sum(part * part, 0, keepdims=True) * (1.0 / HEAD) + 1e-6)
                    unit = part * scale
                    cotangent = po_ref[f, s, rows, :].astype(F32)
                    across = jnp.sum(unit * cotangent, 0, keepdims=True) * (1.0 / HEAD)
                    bars.append((cotangent - unit * across) * scale)
                    unit_ref[f, s, rows, :] = unit.astype(BF16)
                    scale_ref[f, s, 2 * p + h : 2 * p + h + 1, :] = scale
                mixed_bar = jnp.concatenate(bars, 0).astype(BF16)
                carry[:, at] += packed_of(dot_nt(query, mixed_bar))
                suffix_ref[s, f, :, at] = carry[:, at]
                qbar_ref[s, at, tokens] = dot_tn(prefix, mixed_bar).astype(BF16)
        return 0

    lax.fori_loop(0, frames, frame, 0)
    sent_ref[...] = carry[...].astype(BF16)
    hand_out(qbar_ref, qbar_outs)


def tangent_body(groups, count, *refs):
    qd_parts, refs = refs[:groups], refs[groups:]
    sums, firsts, refs = refs[:groups], refs[groups : 2 * groups], refs[2 * groups :]
    gots, refs = refs[:count], refs[count:]
    q_ref, prefix_ref, unit_ref, scale_ref, flow_ref, out_ref, qd_ref, s_ref, dots = refs
    share = q_ref.shape[1]
    frames = prefix_ref.shape[0]
    take_in(qd_parts, qd_ref)
    before = before_of(gots, True)[:, share:]
    prefixes(before, sums, firsts, slice(share, 2 * share), s_ref, dots)

    def frame(f, _):
        tokens = pl.ds(pl.multiple_of(f * SPAN, SPAN), SPAN)
        for s in range(groups):
            outs = []
            for p in range(share // PAIR):
                at = slice(p * PAIR, (p + 1) * PAIR)
                moved = dot(spread(prefix_ref[f, s, :, at].astype(F32)), qd_ref[s, at, tokens])
                moved = moved + dot(spread(dots[f, s, :, at].astype(F32)), q_ref[s, at, tokens])
                for h in range(2):
                    rows = slice(p * PAIR + h * HEAD, p * PAIR + (h + 1) * HEAD)
                    part = moved[h * HEAD : (h + 1) * HEAD]
                    part = part * scale_ref[f, s, 2 * p + h : 2 * p + h + 1, :]
                    unit = unit_ref[f, s, rows, :].astype(F32)
                    along = jnp.sum(unit * part, 0, keepdims=True) * (1.0 / HEAD)
                    outs.append(part - unit * along)
            out_ref[f, s] = jnp.concatenate(outs, 0).T.astype(BF16)
            flow_ref[f, s] = unit_ref[f, s].astype(F32).T.astype(BF16)
        return 0

    lax.fori_loop(0, frames, frame, 0)


def back_body(count, suffix_ref, *refs):
    gots, refs = refs[:count], refs[count:]
    *outs, after_ref = refs
    after = before_of(gots, False)
    after_ref[...] = after
    for k, out_ref in enumerate(outs):
        out_ref[...] = (suffix_ref[mine() ^ k] + after).astype(BF16)


def cotangent_body(suffix_ref, after_ref, out_ref):
    tiles, frames = suffix_ref.shape[:2]
    for f in range(frames):
        for s in range(tiles):
            for h in range(out_ref.shape[1]):
                at = slice(h * HEAD, (h + 1) * HEAD)
                out_ref[f * tiles + s, h] = suffix_ref[s, f, :, at] + after_ref[:, at]


def adjoint_query_body(w_ref, *refs):
    *parts, out_ref, held = refs
    take_in(parts, held)
    out_ref[...] = dot(w_ref[...], held[...].reshape(-1, held.shape[2]))


def adjoint_body(groups, *refs):
    s_parts, refs = refs[:groups], refs[groups:]
    both, part_ref, k_ref, v_ref, out_ref, bars, state_ref = refs
    take_in(s_parts, state_ref)
    _, frames, _, share = state_ref.shape

    def group(g, _):
        for half in range(share // PAIR):
            rows = pl.ds(pl.multiple_of(g * share + half * PAIR, 16), PAIR)
            for f in range(frames):
                at = slice(f * SPAN, (f + 1) * SPAN)
                state = spread(state_ref[g, f, :, half * PAIR : (half + 1) * PAIR].astype(F32))
                bars[0, rows, at] = dot(state, both[1, rows, at]).astype(BF16)
                bars[1, rows, at] = dot_tn(state, both[0, rows, at]).astype(BF16)
        return 0

    lax.fori_loop(0, groups, group, 0)
    out = part_ref[...] + dot(k_ref[...], bars[0]) + dot(v_ref[...], bars[1])
    out_ref[...] = out.T.astype(BF16)


def scan_over(total, sent, axis, forward):
    size = lax.axis_size(axis)
    assert size % 2 == 0
    gots = [lax.ppermute(sent, axis, [(i, i ^ 1) for i in range(size)])]
    total = total + gots[0].astype(F32)
    by = 2
    while by < size:
        pairs = [(i, i + by) for i in range(size - by)]
        if not forward:
            pairs = [(j, i) for i, j in pairs]
        gots.append(lax.ppermute(total.astype(BF16), axis, pairs))
        total = total + gots[-1].astype(F32)
        by *= 2
    return gots


def on_device(
    video, conv_weight, embed_weight, q_weight, k_weight, v_weight, initial_state, probe_in, probe_out
):
    groups, tms = lax.axis_size("space"), lax.axis_size("tm")
    frames, tile_rows, columns, channels = video.shape
    assert tile_rows * columns == SPAN
    tokens = frames * SPAN
    share = D // groups
    heads = HEADS // groups

    first, last = video[:, :1], video[:, -1:]
    up = [(i, i + 1) for i in range(groups - 1)]
    down = [(j, i) for i, j in up]
    above = lax.ppermute(last, "space", up)
    below = lax.ppermute(first, "space", down)

    taps = conv_weight.reshape(3, 9 * channels, -1)
    weight_bytes = 2 * D * D

    def conv(outer, dtype):
        return call(
            functools.partial(conv_body, outer),
            [struct((tokens, taps.shape[2]), dtype)], (video, above, below, taps),
            scratch=[pltpu.VMEM((tokens, taps.shape[1]), BF16)],
            flops=27 * tokens * channels * channels, moved=taps.size + 6 * video.size,
        )[0]

    two_tall = (2, D, tokens)
    part = struct((share, tokens), BF16)
    grouped = (groups, share, tokens)
    held = pltpu.VMEM(grouped, BF16)

    *query_dot, direction, q_near, taps = call(
        probe_body,
        [part] * groups
        + [struct((tokens, D), BF16), struct(q_weight.shape, BF16), struct(taps.shape, BF16)],
        (probe_in.reshape(tokens, D), q_weight, taps), far=3,
        scratch=[pltpu.VMEM((tokens, D), jnp.int32), held, pltpu.SemaphoreType.DMA((3,))],
        flops=2 * tokens * D * D, moved=weight_bytes + 8 * tokens * D,
    )
    query_dot = exchange(query_dot)

    far = conv((0, 1, 0), BF16)
    far = lax.ppermute(far, "tm", [(t, t + 1) for t in range(tms - 1)])
    near = conv((2, 0, 1), F32)

    dots = call(
        probe_pair_body, [struct(two_tall, BF16)], (direction, k_weight, v_weight),
        flops=4 * tokens * D * D, moved=2 * weight_bytes + 6 * tokens * D,
    )[0]

    assert frames == 2
    state_part = struct((HEAD, 2 * share), BF16)
    latent, both, *states = call(
        state_body,
        [struct((tokens, D), BF16), struct(two_tall, BF16)] + [state_part] * (2 * groups),
        (near, far, embed_weight, dots, k_weight, v_weight),
        scratch=[pltpu.VMEM((2, groups) + state_part.shape, BF16)],
        flops=4 * tokens * D * D, moved=2 * weight_bytes + 14 * tokens * D,
    )
    sums, firsts = exchange(states[:groups]), states[groups:]

    query = call(
        query_body, [part] * groups, (latent, q_near), scratch=[held],
        flops=2 * tokens * D * D, moved=weight_bytes + 4 * tokens * D,
    )
    total, sent = call(
        total_body,
        [struct((HEAD, 2 * share), F32), struct((HEAD, 2 * share), BF16)], sums,
        moved=8 * HEAD * share * groups,
    )
    query = exchange(query)
    firsts = exchange(firsts)
    gots = scan_over(total, sent, "tm", True)

    shape_fs = (frames, groups, SPAN, share)
    flip_fs = (frames, groups, share, SPAN)
    cotangent = call(
        flip_body, [struct(flip_fs, BF16)], (probe_out.reshape(shape_fs), sent),
        moved=6 * tokens * D,
    )[0]

    prefix_shape = (frames, groups, HEAD, share)
    state_held = pltpu.VMEM(prefix_shape, F32)
    *query_bar, query, unit, scale, suffix, bar_sent, prefix = call(
        functools.partial(flow_body, groups, len(gots)),
        [part] * groups
        + [
            struct(grouped, BF16),
            struct(flip_fs, BF16),
            struct((frames, groups, heads, SPAN), F32),
            struct((groups, frames, HEAD, share), F32),
            struct((HEAD, share), BF16),
            struct(prefix_shape, BF16),
        ],
        (*query, *sums, *firsts, *gots, initial_state, cotangent),
        scratch=[pltpu.VMEM((HEAD, share), F32), state_held, pltpu.VMEM((HEAD, share), F32), held],
        flops=12 * tokens * D * PAIR, moved=10 * tokens * D,
    )
    query_bar = exchange(query_bar)
    bar_gots = scan_over(suffix[0, 0], bar_sent, "tm", False)

    flow, tangent = call(
        functools.partial(tangent_body, groups, len(gots)), [struct(shape_fs, BF16)] * 2,
        (*query_dot, *sums, *firsts, *gots, query, prefix, unit, scale),
        scratch=[held, state_held, pltpu.VMEM(prefix_shape, BF16)],
        flops=12 * tokens * D * PAIR, moved=10 * tokens * D,
    )

    *state_back, after = call(
        functools.partial(back_body, len(bar_gots)),
        [struct((frames, HEAD, share), BF16)] * groups + [struct((HEAD, share), F32)],
        (suffix, *bar_gots), moved=10 * frames * groups * HEAD * share,
    )
    state_back, flow, tangent = lax.optimization_barrier((state_back, flow, tangent))
    state_back = exchange(state_back)
    state_bar = call(
        cotangent_body, [struct((frames * groups, heads, HEAD, HEAD), F32)],
        (suffix, after), moved=10 * frames * groups * HEAD * share,
    )[0]
    query_part = call(
        adjoint_query_body, [struct((D, tokens), F32)], (q_near, *query_bar),
        scratch=[held], flops=2 * tokens * D * D, moved=weight_bytes + 6 * tokens * D,
    )[0]
    adjoint = call(
        functools.partial(adjoint_body, groups), [struct((tokens, D), BF16)],
        (*state_back, both, query_part, k_weight, v_weight),
        scratch=[pltpu.VMEM(two_tall, BF16), pltpu.VMEM((groups, frames, HEAD, share), BF16)],
        flops=4 * tokens * D * D, moved=2 * weight_bytes + 10 * tokens * D,
    )[0]
    out_shape = (frames, groups * tile_rows, columns, share)
    return (
        flow.reshape(out_shape),
        tangent.reshape(out_shape),
        adjoint.reshape(frames, tile_rows, columns, D),
        state_bar,
    )


def solution(mesh):
    in_specs = (
        P("tm", "space", None, None),
        P(),
        P(),
        P(),
        P(),
        P(),
        P("space", None, None),
        P("tm", "space", None, None),
        P("tm", None, None, "space"),
    )
    out_specs = (
        P("tm", None, None, "space"),
        P("tm", None, None, "space"),
        P("tm", "space", None, None),
        P("tm", "space", None, None),
    )
    return jax.shard_map(
        on_device, mesh=mesh, in_specs=in_specs, out_specs=out_specs, check_vma=False
    )
```

profile of v0, /device:TPU:0, one launch (start us, length us, event | category | flops | bytes accessed | tf_op | source)
XLA Modules:
  0.0 114.4 jit_solution(14325560924036365723)
XLA Ops:
  0.6 0.8 fusion.2
  1.5 1.3 %collective-permute-start.1 = (bf16[2,1,32,384]{3,2,1,0:T(8,128)(2,1)S(1)}, bf16[2,1,32,384]{3,2,1,0:T(8,128)(2,1)S(1)}, u32[]{:S(2)}, u32[]{:S(2)}) collective-permute-start(bf16[2,1,32,384]{3,2,1,0:T(8,128)(2,1)S(1)} %get-tuple-element.96), channel_id=1, source_target_pairs={{1,0},{2,1},{3,2},{5,4},{6,5},{7,6},{9,8},{10,9},{11,10},{13,12},{... | collective-permute-start | bytes 147464 | tf_op jit(solution)/shard_map/ppermute | solution.py:382
  2.8 3.0 %collective-permute-start = (bf16[2,1,32,384]{3,2,1,0:T(8,128)(2,1)S(1)}, bf16[2,1,32,384]{3,2,1,0:T(8,128)(2,1)S(1)}, u32[]{:S(2)}, u32[]{:S(2)}) collective-permute-start(bf16[2,1,32,384]{3,2,1,0:T(8,128)(2,1)S(1)} %get-tuple-element.97), channel_id=1, source_target_pairs={{0,1},{1,2},{2,3},{4,5},{5,6},{6,7},{8,9},{9,10},{10,11},{12,13},{... | collective-permute-start | bytes 147464 | tf_op jit(solution)/shard_map/ppermute | solution.py:381
  5.8 5.8 %shard_map.120 = (bf16[288,512]{1,0:T(8,128)(2,1)S(1)}, bf16[288,512]{1,0:T(8,128)(2,1)S(1)}, bf16[288,512]{1,0:T(8,128)(2,1)S(1)}, bf16[288,512]{1,0:T(8,128)(2...) custom-call(s32[512,1152]{1,0:T(8,128)} %bitcast.14, ...), custom_call_target="tpu_custom_call" | custom-call | flops 1358954496 | bytes 7372800 | tf_op jit(solution)/shard_map/pallas_call | solution.py:25
  11.7 3.0 %shard_map.122 = bf16[512,384]{1,0:T(8,128)(2,1)S(1)} custom-call(bf16[2,8,32,384]{3,2,1,0:T(8,128)(2,1)S(1)} %copy-done.3, bf16[2,1,32,384]{3,2,1,0:T(8,128)(2,1)S(1)} %collective-permute-done.up_ref, bf16[2,1,32,384]{3,2,1,0:T(8,128)(2,1)S(1)} %collective-permute-done.1.down_ref, bf16[3,3456,384]{2,1,0:T(8,128)(2,1)S(1)} %get-tuple-element.50.w_ref), custom_call_target="tpu_custom_call" | custom-call | flops 2038431744 | bytes 5160960 | tf_op jit(solution)/shard_map/pallas_call | solution.py:25
  14.7 5.1 %collective-permute-start.2 = (bf16[512,384]{1,0:T(8,128)(2,1)S(1)}, bf16[512,384]{1,0:T(8,128)(2,1)S(1)}, u32[]{:S(2)}, u32[]{:S(2)}) collective-permute-start(bf16[512,384]{1,0:T(8,128)(2,1)S(1)} %shard_map.122), channel_id=1, source_target_pairs={{0,4},{4,8},{8,12},{12,16},{16,20},{20,24},{24,28},{1,5},{5,9},{9,... | collective-permute-start | bytes 1179656 | tf_op jit(solution)/shard_map/ppermute | solution.py:411
  19.8 3.6 %shard_map.123.dots = bf16[2,1152,512]{2,1,0:T(8,128)(2,1)S(1)} custom-call(bf16[512,1152]{1,0:T(8,128)(2,1)S(1)} %get-tuple-element.51.x_ref, bf16[1152,1152]{1,0:T(8,128)(2,1)S(1)} %copy-done.1, bf16[1152,1152]{1,0:T(8,128)(2,1)S(1)} %copy-done.2), custom_call_target="tpu_custom_call" | custom-call | flops 2717908992 | bytes 8847360 | tf_op jit(solution)/shard_map/pallas_call | solution.py:25
  23.4 3.0 %shard_map.121.near_ref = f32[512,384]{1,0:T(8,128)S(1)} custom-call(bf16[2,8,32,384]{3,2,1,0:T(8,128)(2,1)S(1)} %copy-done.3, bf16[2,1,32,384]{3,2,1,0:T(8,128)(2,1)S(1)} %collective-permute-done.up_ref, bf16[2,1,32,384]{3,2,1,0:T(8,128)(2,1)S(1)} %collective-permute-done.1.down_ref, bf16[3,3456,384]{2,1,0:T(8,128)(2,1)S(1)} %get-tuple-element.50.w_ref), custom_call_target="tpu_custom_call" | custom-call | flops 2038431744 | bytes 5160960 | tf_op jit(solution)/shard_map/pallas_call | solution.py:25
  26.4 2.5 %collective-permute-done.2.far_ref = bf16[512,384]{1,0:T(8,128)(2,1)S(1)} collective-permute-done((bf16[512,384]{1,0:T(8,128)(2,1)S(1)}, bf16[512,384]{1,0:T(8,128)(2,1)S(1)}, u32[]{:S(2)}, u32[]{:S(2)}) %collective-permute-start.2) | collective-permute-done | bytes 393248 | tf_op jit(solution)/shard_map/ppermute | solution.py:411
  28.9 6.2 %shard_map.124 = (bf16[512,1152]{1,0:T(8,128)(2,1)S(1)}, bf16[2,1152,512]{2,1,0:T(8,128)(2,1)S(1)}, bf16[72,576]{1,0:T(8,128)(2,1)S(1)}, bf16[72,576]{1,0:T(8,12...) custom-call(f32[512,384]{1,0:T(8,128)S(1)} %shard_map.121.near_ref, ...), custom_call_target="tpu_custom_call" | custom-call | flops 2717908992 | bytes 13565952 | tf_op jit(solution)/shard_map/pallas_call | solution.py:25
  35.1 0.3 collective-permute-start.6
  35.5 1.6 %collective-permute-start.8 = (bf16[72,576]{1,0:T(8,128)(2,1)S(1)}, bf16[72,576]{1,0:T(8,128)(2,1)S(1)}, u32[]{:S(2)}, u32[]{:S(2)}) collective-permute-start(bf16[72,576]{1,0:T(8,128)(2,1)S(1)} %get-tuple-element.61), channel_id=1, source_target_pairs={{0,3},{1,2},{2,1},{3,0},{4,7},{5,6},{6,5},{7,4},{8,11},{9,10},{10,... | collective-permute-start | bytes 248840 | tf_op jit(solution)/shard_map/ppermute | solution.py:90
  37.1 4.0 %collective-permute-done.7.refs_2_.refs_6_ = bf16[72,576]{1,0:T(8,128)(2,1)S(1)} collective-permute-done((bf16[72,576]{1,0:T(8,128)(2,1)S(1)}, bf16[72,576]{1,0:T(8,128)(2,1)S(1)}, u32[]{:S(2)}, u32[]{:S(2)}) %collective-permute-start.7) | collective-permute-done | bytes 82976 | tf_op jit(solution)/shard_map/ppermute | solution.py:90
  41.0 0.5 collective-permute-done.8.refs_3_.refs_7_
  41.6 2.7 %collective-permute-start.12 = (bf16[72,576]{1,0:T(8,128)(2,1)S(1)}, bf16[72,576]{1,0:T(8,128)(2,1)S(1)}, u32[]{:S(2)}, u32[]{:S(2)}) collective-permute-start(bf16[72,576]{1,0:T(8,128)(2,1)S(1)} %get-tuple-element.66.tie_ref), channel_id=1, source_target_pairs={{0,4},{4,0},{8,12},{12,8},{16,20},{20,16},{24,28},{28,24},{1,5},{5... | collective-permute-start | bytes 248840 | tf_op jit(solution)/shard_map/ppermute | solution.py:355
  44.3 0.1 collective-permute-start.9
  44.4 0.5 collective-permute-start.10
  44.9 1.2 %collective-permute-start.11 = (bf16[72,576]{1,0:T(8,128)(2,1)S(1)}, bf16[72,576]{1,0:T(8,128)(2,1)S(1)}, u32[]{:S(2)}, u32[]{:S(2)}) collective-permute-start(bf16[72,576]{1,0:T(8,128)(2,1)S(1)} %get-tuple-element.65), channel_id=1, source_target_pairs={{0,3},{1,2},{2,1},{3,0},{4,7},{5,6},{6,5},{7,4},{8,11},{9,10},{10,... | collective-permute-start | bytes 248840 | tf_op jit(solution)/shard_map/ppermute | solution.py:90
  46.2 1.4 %collective-permute-done.12.refs_12_ = bf16[72,576]{1,0:T(8,128)(2,1)S(1)} collective-permute-done((bf16[72,576]{1,0:T(8,128)(2,1)S(1)}, bf16[72,576]{1,0:T(8,128)(2,1)S(1)}, u32[]{:S(2)}, u32[]{:S(2)}) %collective-permute-start.12) | collective-permute-done | bytes 82976 | tf_op jit(solution)/shard_map/ppermute | solution.py:355
  47.5 4.6 %collective-permute-start.13 = (bf16[72,576]{1,0:T(8,128)(2,1)S(1)}, bf16[72,576]{1,0:T(8,128)(2,1)S(1)}, u32[]{:S(2)}, u32[]{:S(2)}) collective-permute-start(bf16[72,576]{1,0:T(8,128)(2,1)S(1)} %fusion), channel_id=1, source_target_pairs={{0,8},{4,12},{8,16},{12,20},{16,24},{20,28},{1,9},{5,13},{9,17},{1... | collective-permute-start | bytes 248840 | tf_op jit(solution)/shard_map/ppermute | solution.py:362
  52.2 2.1 %shard_map.125 = (bf16[288,512]{1,0:T(8,128)(2,1)S(1)}, bf16[288,512]{1,0:T(8,128)(2,1)S(1)}, bf16[288,512]{1,0:T(8,128)(2,1)S(1)}, bf16[288,512]{1,0:T(8,128)(2,1)S(1)}) custom-call(bf16[512,1152]{1,0:T(8,128)(2,1)S(1)} %get-tuple-element.52.x_ref, bf16[1152,1152]{1,0:T(8,128)(2,1)S(1)} %get-tuple-element.53.w_ref), custom_call_target="tpu_custom_call" | custom-call | flops 1358954496 | bytes 5013504 | tf_op jit(solution)/shard_map/pallas_call | solution.py:25
  54.4 0.4 collective-permute-start.4
  54.8 1.4 %collective-permute-start.5 = (bf16[288,512]{1,0:T(8,128)(2,1)S(1)}, bf16[288,512]{1,0:T(8,128)(2,1)S(1)}, u32[]{:S(2)}, u32[]{:S(2)}) collective-permute-start(bf16[288,512]{1,0:T(8,128)(2,1)S(1)} %get-tuple-element.57), channel_id=1, source_target_pairs={{0,3},{1,2},{2,1},{3,0},{4,7},{5,6},{6,5},{7,4},{8,11},{9,10},{10,... | collective-permute-start | bytes 884744 | tf_op jit(solution)/shard_map/ppermute | solution.py:90
  56.3 4.7 %collective-permute-start.14 = (bf16[72,576]{1,0:T(8,128)(2,1)S(1)}, bf16[72,576]{1,0:T(8,128)(2,1)S(1)}, u32[]{:S(2)}, u32[]{:S(2)}) collective-permute-start(bf16[72,576]{1,0:T(8,128)(2,1)S(1)} %add_convert_fusion), channel_id=1, source_target_pairs={{0,16},{4,20},{8,24},{12,28},{1,17},{5,21},{9,25},{13,29},{2,18},{... | collective-permute-start | bytes 248840 | tf_op jit(solution)/shard_map/ppermute | solution.py:362
  61.0 1.1 shard_map.127.refs_16_
  62.2 2.2 %collective-permute-done.4.refs_2_ = bf16[288,512]{1,0:T(8,128)(2,1)S(1)} collective-permute-done((bf16[288,512]{1,0:T(8,128)(2,1)S(1)}, bf16[288,512]{1,0:T(8,128)(2,1)S(1)}, u32[]{:S(2)}, u32[]{:S(2)}) %collective-permute-start.4) | collective-permute-done | bytes 294944 | tf_op jit(solution)/shard_map/ppermute | solution.py:90
  64.3 5.2 %collective-permute-done.5.refs_3_ = bf16[288,512]{1,0:T(8,128)(2,1)S(1)} collective-permute-done((bf16[288,512]{1,0:T(8,128)(2,1)S(1)}, bf16[288,512]{1,0:T(8,128)(2,1)S(1)}, u32[]{:S(2)}, u32[]{:S(2)}) %collective-permute-start.5) | collective-permute-done | bytes 294944 | tf_op jit(solution)/shard_map/ppermute | solution.py:90
  69.6 5.6 %shard_map.128 = (bf16[288,512]{1,0:T(8,128)(2,1)S(1)}, bf16[288,512]{1,0:T(8,128)(2,1)S(1)}, bf16[288,512]{1,0:T(8,128)(2,1)S(1)}, bf16[288,512]{1,0:T(8,128)(2...) custom-call(bf16[288,512]{1,0:T(8,128)(2,1)S(1)} %get-tuple-element., ...), custom_call_target="tpu_custom_call" | custom-call | flops 1019215872 | bytes 5898240 | tf_op jit(solution)/shard_map/pallas_call | solution.py:25
  75.2 0.7 collective-permute-start.15
  75.9 0.4 collective-permute-start.19
  76.2 1.4 %collective-permute-start.20 = (bf16[288,512]{1,0:T(8,128)(2,1)S(1)}, bf16[288,512]{1,0:T(8,128)(2,1)S(1)}, u32[]{:S(2)}, u32[]{:S(2)}) collective-permute-start(bf16[288,512]{1,0:T(8,128)(2,1)S(1)} %get-tuple-element.77), channel_id=1, source_target_pairs={{0,3},{1,2},{2,1},{3,0},{4,7},{5,6},{6,5},{7,4},{8,11},{9,10},{10,... | collective-permute-start | bytes 884744 | tf_op jit(solution)/shard_map/ppermute | solution.py:90
  77.7 1.7 %collective-permute-done.15.refs_0_ = bf16[72,288]{1,0:T(8,128)(2,1)S(1)} collective-permute-done((bf16[72,288]{1,0:T(8,128)(2,1)S(1)}, bf16[72,288]{1,0:T(8,128)(2,1)S(1)}, u32[]{:S(2)}, u32[]{:S(2)}) %collective-permute-start.15) | collective-permute-done | bytes 41504 | tf_op jit(solution)/shard_map/ppermute | solution.py:355
  79.4 1.3 %collective-permute-start.16 = (bf16[72,288]{1,0:T(8,128)(2,1)S(1)}, bf16[72,288]{1,0:T(8,128)(2,1)S(1)}, u32[]{:S(2)}, u32[]{:S(2)}) collective-permute-start(bf16[72,288]{1,0:T(8,128)(2,1)S(1)} %fusion.1), channel_id=1, source_target_pairs={{8,0},{12,4},{16,8},{20,12},{24,16},{28,20},{9,1},{13,5},{17,9},{2... | collective-permute-start | bytes 124424 | tf_op jit(solution)/shard_map/ppermute | solution.py:362
  80.8 0.4 collective-permute-start.25
  81.2 4.2 %collective-permute-done.16.refs_1_ = bf16[72,288]{1,0:T(8,128)(2,1)S(1)} collective-permute-done((bf16[72,288]{1,0:T(8,128)(2,1)S(1)}, bf16[72,288]{1,0:T(8,128)(2,1)S(1)}, u32[]{:S(2)}, u32[]{:S(2)}) %collective-permute-start.16) | collective-permute-done | bytes 41504 | tf_op jit(solution)/shard_map/ppermute | solution.py:362
  85.5 0.3 collective-permute-done.19.refs_2_
  85.8 1.3 %collective-permute-start.17 = (bf16[72,288]{1,0:T(8,128)(2,1)S(1)}, bf16[72,288]{1,0:T(8,128)(2,1)S(1)}, u32[]{:S(2)}, u32[]{:S(2)}) collective-permute-start(bf16[72,288]{1,0:T(8,128)(2,1)S(1)} %add_convert_fusion.1), channel_id=1, source_target_pairs={{16,0},{20,4},{24,8},{28,12},{17,1},{21,5},{25,9},{29,13},{18,2},{... | collective-permute-start | bytes 124424 | tf_op jit(solution)/shard_map/ppermute | solution.py:362
  87.1 3.9 %collective-permute-done.20.refs_3_ = bf16[288,512]{1,0:T(8,128)(2,1)S(1)} collective-permute-done((bf16[288,512]{1,0:T(8,128)(2,1)S(1)}, bf16[288,512]{1,0:T(8,128)(2,1)S(1)}, u32[]{:S(2)}, u32[]{:S(2)}) %collective-permute-start.20) | collective-permute-done | bytes 294944 | tf_op jit(solution)/shard_map/ppermute | solution.py:90
  91.0 4.6 %shard_map.130 = (bf16[2,4,256,288]{3,2,1,0:T(8,128)(2,1)}, bf16[2,4,256,288]{3,2,1,0:T(8,128)(2,1)}) custom-call(bf16[288,512]{1,0:T(8,128)(2,1)S(1)} %get-tuple-element.74.refs_0_, bf16[288,512]{1,0:T(8,128)(2,1)S(1)} %collective-permute-done.18.refs_1_, bf16[288,512]{1,0:T(8,128)(2,1)S(1)} %collective-permute-done.19.refs_2_, ...), custom_call_target="tpu_custom_call" | custom-call | flops 1019215872 | bytes 5898240 | tf_op jit(solution)/shard_map/pallas_call | solution.py:25
  95.7 1.5 %shard_map.133 = f32[8,4,72,72]{3,2,1,0:T(8,128)} custom-call(f32[4,2,72,288]{3,2,1,0:T(8,128)S(1)} %get-tuple-element.68.suffix_ref, f32[72,288]{1,0:T(8,128)S(1)} %get-tuple-element.95.after_ref), custom_call_target="tpu_custom_call" | custom-call | bytes 1658880 | tf_op jit(solution)/shard_map/pallas_call | solution.py:25
  97.2 0.9 collective-permute-start.21
  98.1 0.4 collective-permute-start.22
  98.4 1.0 collective-permute-start.23
  99.4 4.2 %collective-permute-done.26.refs_3_ = bf16[288,512]{1,0:T(8,128)(2,1)S(1)} collective-permute-done((bf16[288,512]{1,0:T(8,128)(2,1)S(1)}, bf16[288,512]{1,0:T(8,128)(2,1)S(1)}, u32[]{:S(2)}, u32[]{:S(2)}) %collective-permute-start.26) | collective-permute-done | bytes 294944 | tf_op jit(solution)/shard_map/ppermute | solution.py:90
  103.6 1.8 %shard_map.131.refs_5_ = f32[1152,512]{1,0:T(8,128)S(1)} custom-call(bf16[1152,1152]{1,0:T(8,128)(2,1)S(1)} %get-tuple-element.53.w_ref, bf16[288,512]{1,0:T(8,128)(2,1)S(1)} %get-tuple-element.91.refs_0_, bf16[288,512]{1,0:T(8,128)(2,1)S(1)} %collective-permute-done.24.refs_1_, bf16[288,512]{1,0:T(8,128)(2,1)S(1)} %collective-permute-done.25.refs_2_, ...), custom_call_target="tpu_custom_call" | custom-call | flops 1358954496 | bytes 6193152 | tf_op jit(solution)/shard_map/pallas_call | solution.py:25
  105.4 1.7 %collective-permute-done.22.refs_2_ = bf16[2,72,288]{2,1,0:T(8,128)(2,1)S(1)} collective-permute-done((bf16[2,72,288]{2,1,0:T(8,128)(2,1)S(1)}, bf16[2,72,288]{2,1,0:T(8,128)(2,1)S(1)}, u32[]{:S(2)}, u32[]{:S(2)}) %collective-permute-start.22) | collective-permute-done | bytes 82976 | tf_op jit(solution)/shard_map/ppermute | solution.py:90
  107.1 1.3 %collective-permute-done.23.refs_3_ = bf16[2,72,288]{2,1,0:T(8,128)(2,1)S(1)} collective-permute-done((bf16[2,72,288]{2,1,0:T(8,128)(2,1)S(1)}, bf16[2,72,288]{2,1,0:T(8,128)(2,1)S(1)}, u32[]{:S(2)}, u32[]{:S(2)}) %collective-permute-start.23) | collective-permute-done | bytes 82976 | tf_op jit(solution)/shard_map/ppermute | solution.py:90
  108.4 6.0 %shard_map.132 = bf16[512,1152]{1,0:T(8,128)(2,1)} custom-call(bf16[2,72,288]{2,1,0:T(8,128)(2,1)S(1)} %get-tuple-element.86.refs_0_, bf16[2,72,288]{2,1,0:T(8,128)(2,1)S(1)} %collective-permute-done.21.refs_1_, bf16[2,72,288]{2,1,0:T(8,128)(2,1)S(1)} %collective-permute-done.22.refs_2_, bf16[2,72,288]{2,1,0:T(8,128)(2,1)S(1)} %collective-permute-done.23.refs_3_, ...), custom_call_target="tpu_custom_call" | custom-call | flops 2717908992 | bytes 11206656 | tf_op jit(solution)/shard_map/pallas_call | solution.py:25
  (37 shorter events, 0.5 us)
Async XLA Ops:
  1.5 10.2 %collective-permute-start.1 = (bf16[2,1,32,384]{3,2,1,0:T(8,128)(2,1)S(1)}, bf16[2,1,32,384]{3,2,1,0:T(8,128)(2,1)S(1)}, u32[]{:S(2)}, u32[]{:S(2)}) collective-permute-start(bf16[2,1,32,384]{3,2,1,0:T(8,128)(2,1)S(1)} %get-tuple-element.96), channel_id=1, source_target_pairs={{1,0},{2,1},{3,2},{5,4},{6,5},{7,6},{9,8},{10,9},{11,10},{13,12},{... | collective-permute-start | bytes 147464 | tf_op jit(solution)/shard_map/ppermute | solution.py:382
  2.8 8.9 %collective-permute-start = (bf16[2,1,32,384]{3,2,1,0:T(8,128)(2,1)S(1)}, bf16[2,1,32,384]{3,2,1,0:T(8,128)(2,1)S(1)}, u32[]{:S(2)}, u32[]{:S(2)}) collective-permute-start(bf16[2,1,32,384]{3,2,1,0:T(8,128)(2,1)S(1)} %get-tuple-element.97), channel_id=1, source_target_pairs={{0,1},{1,2},{2,3},{4,5},{5,6},{6,7},{8,9},{9,10},{10,11},{12,13},{... | collective-permute-start | bytes 147464 | tf_op jit(solution)/shard_map/ppermute | solution.py:381
  5.8 5.9 %copy-start.3 = (bf16[2,8,32,384]{3,2,1,0:T(8,128)(2,1)S(1)}, bf16[2,8,32,384]{3,2,1,0:T(8,128)(2,1)}, u32[]{:S(2)}) copy-start(bf16[2,8,32,384]{3,2,1,0:T(8,128)(2,1)} %own_ref.3) | copy-start | bytes 1179652
  11.7 8.1 %copy-start.1 = (bf16[1152,1152]{1,0:T(8,128)(2,1)S(1)}, bf16[1152,1152]{1,0:T(8,128)(2,1)}, u32[]{:S(2)}) copy-start(bf16[1152,1152]{1,0:T(8,128)(2,1)} %refs_6_.1) | copy-start | bytes 7962628
  11.7 8.1 %copy-start.2 = (bf16[1152,1152]{1,0:T(8,128)(2,1)S(1)}, bf16[1152,1152]{1,0:T(8,128)(2,1)}, u32[]{:S(2)}) copy-start(bf16[1152,1152]{1,0:T(8,128)(2,1)} %refs_7_.1) | copy-start | bytes 7962628
  14.7 14.2 %collective-permute-start.2 = (bf16[512,384]{1,0:T(8,128)(2,1)S(1)}, bf16[512,384]{1,0:T(8,128)(2,1)S(1)}, u32[]{:S(2)}, u32[]{:S(2)}) collective-permute-start(bf16[512,384]{1,0:T(8,128)(2,1)S(1)} %shard_map.122), channel_id=1, source_target_pairs={{0,4},{4,8},{8,12},{12,16},{16,20},{20,24},{24,28},{1,5},{5,9},{9,... | collective-permute-start | bytes 1179656 | tf_op jit(solution)/shard_map/ppermute | solution.py:411
  23.4 5.5 %copy-start.4 = (bf16[384,1152]{1,0:T(8,128)(2,1)S(1)}, bf16[384,1152]{1,0:T(8,128)(2,1)}, u32[]{:S(2)}) copy-start(bf16[384,1152]{1,0:T(8,128)(2,1)} %embed_ref.1) | copy-start | bytes 2654212
  35.1 1.9 %collective-permute-start.6 = (bf16[72,576]{1,0:T(8,128)(2,1)S(1)}, bf16[72,576]{1,0:T(8,128)(2,1)S(1)}, u32[]{:S(2)}, u32[]{:S(2)}) collective-permute-start(bf16[72,576]{1,0:T(8,128)(2,1)S(1)} %get-tuple-element.59), channel_id=1, source_target_pairs={{0,1},{1,0},{2,3},{3,2},{4,5},{5,4},{6,7},{7,6},{8,9},{9,8},{10,11... | collective-permute-start | bytes 248840 | tf_op jit(solution)/shard_map/ppermute | solution.py:90
  35.5 5.5 %collective-permute-start.7 = (bf16[72,576]{1,0:T(8,128)(2,1)S(1)}, bf16[72,576]{1,0:T(8,128)(2,1)S(1)}, u32[]{:S(2)}, u32[]{:S(2)}) collective-permute-start(bf16[72,576]{1,0:T(8,128)(2,1)S(1)} %get-tuple-element.60), channel_id=1, source_target_pairs={{0,2},{1,3},{2,0},{3,1},{4,6},{5,7},{6,4},{7,5},{8,10},{9,11},{10,... | collective-permute-start | bytes 248840 | tf_op jit(solution)/shard_map/ppermute | solution.py:90
  35.5 6.0 %collective-permute-start.8 = (bf16[72,576]{1,0:T(8,128)(2,1)S(1)}, bf16[72,576]{1,0:T(8,128)(2,1)S(1)}, u32[]{:S(2)}, u32[]{:S(2)}) collective-permute-start(bf16[72,576]{1,0:T(8,128)(2,1)S(1)} %get-tuple-element.61), channel_id=1, source_target_pairs={{0,3},{1,2},{2,1},{3,0},{4,7},{5,6},{6,5},{7,4},{8,11},{9,10},{10,... | collective-permute-start | bytes 248840 | tf_op jit(solution)/shard_map/ppermute | solution.py:90
  41.6 5.9 %collective-permute-start.12 = (bf16[72,576]{1,0:T(8,128)(2,1)S(1)}, bf16[72,576]{1,0:T(8,128)(2,1)S(1)}, u32[]{:S(2)}, u32[]{:S(2)}) collective-permute-start(bf16[72,576]{1,0:T(8,128)(2,1)S(1)} %get-tuple-element.66.tie_ref), channel_id=1, source_target_pairs={{0,4},{4,0},{8,12},{12,8},{16,20},{20,16},{24,28},{28,24},{1,5},{5... | collective-permute-start | bytes 248840 | tf_op jit(solution)/shard_map/ppermute | solution.py:355
  44.3 10.1 %collective-permute-start.9 = (bf16[72,576]{1,0:T(8,128)(2,1)S(1)}, bf16[72,576]{1,0:T(8,128)(2,1)S(1)}, u32[]{:S(2)}, u32[]{:S(2)}) collective-permute-start(bf16[72,576]{1,0:T(8,128)(2,1)S(1)} %get-tuple-element.63), channel_id=1, source_target_pairs={{0,1},{1,0},{2,3},{3,2},{4,5},{5,4},{6,7},{7,6},{8,9},{9,8},{10,11... | collective-permute-start | bytes 248840 | tf_op jit(solution)/shard_map/ppermute | solution.py:90
  44.4 11.9 %collective-permute-start.10 = (bf16[72,576]{1,0:T(8,128)(2,1)S(1)}, bf16[72,576]{1,0:T(8,128)(2,1)S(1)}, u32[]{:S(2)}, u32[]{:S(2)}) collective-permute-start(bf16[72,576]{1,0:T(8,128)(2,1)S(1)} %get-tuple-element.64), channel_id=1, source_target_pairs={{0,2},{1,3},{2,0},{3,1},{4,6},{5,7},{6,4},{7,5},{8,10},{9,11},{10,... | collective-permute-start | bytes 248840 | tf_op jit(solution)/shard_map/ppermute | solution.py:90
  44.9 17.2 %collective-permute-start.11 = (bf16[72,576]{1,0:T(8,128)(2,1)S(1)}, bf16[72,576]{1,0:T(8,128)(2,1)S(1)}, u32[]{:S(2)}, u32[]{:S(2)}) collective-permute-start(bf16[72,576]{1,0:T(8,128)(2,1)S(1)} %get-tuple-element.65), channel_id=1, source_target_pairs={{0,3},{1,2},{2,1},{3,0},{4,7},{5,6},{6,5},{7,4},{8,11},{9,10},{10,... | collective-permute-start | bytes 248840 | tf_op jit(solution)/shard_map/ppermute | solution.py:90
  47.5 7.2 %collective-permute-start.13 = (bf16[72,576]{1,0:T(8,128)(2,1)S(1)}, bf16[72,576]{1,0:T(8,128)(2,1)S(1)}, u32[]{:S(2)}, u32[]{:S(2)}) collective-permute-start(bf16[72,576]{1,0:T(8,128)(2,1)S(1)} %fusion), channel_id=1, source_target_pairs={{0,8},{4,12},{8,16},{12,20},{16,24},{20,28},{1,9},{5,13},{9,17},{1... | collective-permute-start | bytes 248840 | tf_op jit(solution)/shard_map/ppermute | solution.py:362
  52.2 8.8 %copy-start = (s32[2,32,32,288]{3,2,1,0:T(8,128)S(1)}, s32[2,32,32,288]{3,2,1,0:T(8,128)}, u32[]{:S(2)}) copy-start(s32[2,32,32,288]{3,2,1,0:T(8,128)} %param.17) | copy-start | bytes 7077892
  54.3 7.9 %collective-permute-start.3 = (bf16[288,512]{1,0:T(8,128)(2,1)S(1)}, bf16[288,512]{1,0:T(8,128)(2,1)S(1)}, u32[]{:S(2)}, u32[]{:S(2)}) collective-permute-start(bf16[288,512]{1,0:T(8,128)(2,1)S(1)} %get-tuple-element.55), channel_id=1, source_target_pairs={{0,1},{1,0},{2,3},{3,2},{4,5},{5,4},{6,7},{7,6},{8,9},{9,8},{10,11... | collective-permute-start | bytes 884744 | tf_op jit(solution)/shard_map/ppermute | solution.py:90
  54.4 9.9 %collective-permute-start.4 = (bf16[288,512]{1,0:T(8,128)(2,1)S(1)}, bf16[288,512]{1,0:T(8,128)(2,1)S(1)}, u32[]{:S(2)}, u32[]{:S(2)}) collective-permute-start(bf16[288,512]{1,0:T(8,128)(2,1)S(1)} %get-tuple-element.56), channel_id=1, source_target_pairs={{0,2},{1,3},{2,0},{3,1},{4,6},{5,7},{6,4},{7,5},{8,10},{9,11},{10,... | collective-permute-start | bytes 884744 | tf_op jit(solution)/shard_map/ppermute | solution.py:90
  54.8 14.8 %copy-start.5 = (f32[4,72,72]{2,1,0:T(8,128)S(1)}, f32[4,72,72]{2,1,0:T(8,128)}, u32[]{:S(2)}) copy-start(f32[4,72,72]{2,1,0:T(8,128)} %refs_15_.1) | copy-start | bytes 248836
  54.8 14.8 %collective-permute-start.5 = (bf16[288,512]{1,0:T(8,128)(2,1)S(1)}, bf16[288,512]{1,0:T(8,128)(2,1)S(1)}, u32[]{:S(2)}, u32[]{:S(2)}) collective-permute-start(bf16[288,512]{1,0:T(8,128)(2,1)S(1)} %get-tuple-element.57), channel_id=1, source_target_pairs={{0,3},{1,2},{2,1},{3,0},{4,7},{5,6},{6,5},{7,4},{8,11},{9,10},{10,... | collective-permute-start | bytes 884744 | tf_op jit(solution)/shard_map/ppermute | solution.py:90
  56.3 13.3 %collective-permute-start.14 = (bf16[72,576]{1,0:T(8,128)(2,1)S(1)}, bf16[72,576]{1,0:T(8,128)(2,1)S(1)}, u32[]{:S(2)}, u32[]{:S(2)}) collective-permute-start(bf16[72,576]{1,0:T(8,128)(2,1)S(1)} %add_convert_fusion), channel_id=1, source_target_pairs={{0,16},{4,20},{8,24},{12,28},{1,17},{5,21},{9,25},{13,29},{2,18},{... | collective-permute-start | bytes 248840 | tf_op jit(solution)/shard_map/ppermute | solution.py:362
  75.2 4.2 %collective-permute-start.15 = (bf16[72,288]{1,0:T(8,128)(2,1)S(1)}, bf16[72,288]{1,0:T(8,128)(2,1)S(1)}, u32[]{:S(2)}, u32[]{:S(2)}) collective-permute-start(bf16[72,288]{1,0:T(8,128)(2,1)S(1)} %get-tuple-element.69), channel_id=1, source_target_pairs={{0,4},{4,0},{8,12},{12,8},{16,20},{20,16},{24,28},{28,24},{1,5},{5... | collective-permute-start | bytes 124424 | tf_op jit(solution)/shard_map/ppermute | solution.py:355
  75.8 5.0 %collective-permute-start.18 = (bf16[288,512]{1,0:T(8,128)(2,1)S(1)}, bf16[288,512]{1,0:T(8,128)(2,1)S(1)}, u32[]{:S(2)}, u32[]{:S(2)}) collective-permute-start(bf16[288,512]{1,0:T(8,128)(2,1)S(1)} %get-tuple-element.75), channel_id=1, source_target_pairs={{0,1},{1,0},{2,3},{3,2},{4,5},{5,4},{6,7},{7,6},{8,9},{9,8},{10,11... | collective-permute-start | bytes 884744 | tf_op jit(solution)/shard_map/ppermute | solution.py:90
  75.9 9.9 %collective-permute-start.19 = (bf16[288,512]{1,0:T(8,128)(2,1)S(1)}, bf16[288,512]{1,0:T(8,128)(2,1)S(1)}, u32[]{:S(2)}, u32[]{:S(2)}) collective-permute-start(bf16[288,512]{1,0:T(8,128)(2,1)S(1)} %get-tuple-element.76), channel_id=1, source_target_pairs={{0,2},{1,3},{2,0},{3,1},{4,6},{5,7},{6,4},{7,5},{8,10},{9,11},{10,... | collective-permute-start | bytes 884744 | tf_op jit(solution)/shard_map/ppermute | solution.py:90
  76.2 14.8 %collective-permute-start.20 = (bf16[288,512]{1,0:T(8,128)(2,1)S(1)}, bf16[288,512]{1,0:T(8,128)(2,1)S(1)}, u32[]{:S(2)}, u32[]{:S(2)}) collective-permute-start(bf16[288,512]{1,0:T(8,128)(2,1)S(1)} %get-tuple-element.77), channel_id=1, source_target_pairs={{0,3},{1,2},{2,1},{3,0},{4,7},{5,6},{6,5},{7,4},{8,11},{9,10},{10,... | collective-permute-start | bytes 884744 | tf_op jit(solution)/shard_map/ppermute | solution.py:90
  79.4 6.0 %collective-permute-start.16 = (bf16[72,288]{1,0:T(8,128)(2,1)S(1)}, bf16[72,288]{1,0:T(8,128)(2,1)S(1)}, u32[]{:S(2)}, u32[]{:S(2)}) collective-permute-start(bf16[72,288]{1,0:T(8,128)(2,1)S(1)} %fusion.1), channel_id=1, source_target_pairs={{8,0},{12,4},{16,8},{20,12},{24,16},{28,20},{9,1},{13,5},{17,9},{2... | collective-permute-start | bytes 124424 | tf_op jit(solution)/shard_map/ppermute | solution.py:362
  80.7 17.7 %collective-permute-start.24 = (bf16[288,512]{1,0:T(8,128)(2,1)S(1)}, bf16[288,512]{1,0:T(8,128)(2,1)S(1)}, u32[]{:S(2)}, u32[]{:S(2)}) collective-permute-start(bf16[288,512]{1,0:T(8,128)(2,1)S(1)} %get-tuple-element.92), channel_id=1, source_target_pairs={{0,1},{1,0},{2,3},{3,2},{4,5},{5,4},{6,7},{7,6},{8,9},{9,8},{10,11... | collective-permute-start | bytes 884744 | tf_op jit(solution)/shard_map/ppermute | solution.py:90
  80.8 18.6 %collective-permute-start.25 = (bf16[288,512]{1,0:T(8,128)(2,1)S(1)}, bf16[288,512]{1,0:T(8,128)(2,1)S(1)}, u32[]{:S(2)}, u32[]{:S(2)}) collective-permute-start(bf16[288,512]{1,0:T(8,128)(2,1)S(1)} %get-tuple-element.93), channel_id=1, source_target_pairs={{0,2},{1,3},{2,0},{3,1},{4,6},{5,7},{6,4},{7,5},{8,10},{9,11},{10,... | collective-permute-start | bytes 884744 | tf_op jit(solution)/shard_map/ppermute | solution.py:90
  85.4 18.2 %collective-permute-start.26 = (bf16[288,512]{1,0:T(8,128)(2,1)S(1)}, bf16[288,512]{1,0:T(8,128)(2,1)S(1)}, u32[]{:S(2)}, u32[]{:S(2)}) collective-permute-start(bf16[288,512]{1,0:T(8,128)(2,1)S(1)} %get-tuple-element.94), channel_id=1, source_target_pairs={{0,3},{1,2},{2,1},{3,0},{4,7},{5,6},{6,5},{7,4},{8,11},{9,10},{10,... | collective-permute-start | bytes 884744 | tf_op jit(solution)/shard_map/ppermute | solution.py:90
  85.8 9.8 %collective-permute-start.17 = (bf16[72,288]{1,0:T(8,128)(2,1)S(1)}, bf16[72,288]{1,0:T(8,128)(2,1)S(1)}, u32[]{:S(2)}, u32[]{:S(2)}) collective-permute-start(bf16[72,288]{1,0:T(8,128)(2,1)S(1)} %add_convert_fusion.1), channel_id=1, source_target_pairs={{16,0},{20,4},{24,8},{28,12},{17,1},{21,5},{25,9},{29,13},{18,2},{... | collective-permute-start | bytes 124424 | tf_op jit(solution)/shard_map/ppermute | solution.py:362
  97.2 8.3 %collective-permute-start.21 = (bf16[2,72,288]{2,1,0:T(8,128)(2,1)S(1)}, bf16[2,72,288]{2,1,0:T(8,128)(2,1)S(1)}, u32[]{:S(2)}, u32[]{:S(2)}) collective-permute-start(bf16[2,72,288]{2,1,0:T(8,128)(2,1)S(1)} %get-tuple-element.87), channel_id=1, source_target_pairs={{0,1},{1,0},{2,3},{3,2},{4,5},{5,4},{6,7},{7,6},{8,9},{9,8},{10,11... | collective-permute-start | bytes 248840 | tf_op jit(solution)/shard_map/ppermute | solution.py:90
  98.1 9.0 %collective-permute-start.22 = (bf16[2,72,288]{2,1,0:T(8,128)(2,1)S(1)}, bf16[2,72,288]{2,1,0:T(8,128)(2,1)S(1)}, u32[]{:S(2)}, u32[]{:S(2)}) collective-permute-start(bf16[2,72,288]{2,1,0:T(8,128)(2,1)S(1)} %get-tuple-element.88), channel_id=1, source_target_pairs={{0,2},{1,3},{2,0},{3,1},{4,6},{5,7},{6,4},{7,5},{8,10},{9,11},{10,... | collective-permute-start | bytes 248840 | tf_op jit(solution)/shard_map/ppermute | solution.py:90
  98.4 10.0 %collective-permute-start.23 = (bf16[2,72,288]{2,1,0:T(8,128)(2,1)S(1)}, bf16[2,72,288]{2,1,0:T(8,128)(2,1)S(1)}, u32[]{:S(2)}, u32[]{:S(2)}) collective-permute-start(bf16[2,72,288]{2,1,0:T(8,128)(2,1)S(1)} %get-tuple-element.89), channel_id=1, source_target_pairs={{0,3},{1,2},{2,1},{3,0},{4,7},{5,6},{6,5},{7,4},{8,11},{9,10},{10,... | collective-permute-start | bytes 248840 | tf_op jit(solution)/shard_map/ppermute | solution.py:90
where the time goes:
time: 115 us; the launch traced here: 114 us
  Pallas kernels  44.4 us (39%)
  starting transfers between devices  35 us (30%)
  waiting for transfers between devices  33.1 us (29%)
    pallas_call x14, Pallas kernels, call(): pl.pallas_call(body, in_specs=[anywhere] * far + [vmem] * (len(args) - fa...  44.4 us
    ppermute x18, waiting for transfers between devices, exchange(): lax.ppermute(parts[k], 'space', [(i, i ^ k) for i in range(size)])  23.3 us
    ppermute x4, starting transfers between devices, scan_over(): gots.append(lax.ppermute(total.astype(BF16), axis, pairs))  11.9 us
    ppermute x18, starting transfers between devices, exchange(): lax.ppermute(parts[k], 'space', [(i, i ^ k) for i in range(size)])  10.3 us
    ppermute x1, starting transfers between devices, on_device(): far = lax.ppermute(far, 'tm', [(t, t + 1) for t in range(tms - 1)])  5.08 us
    ppermute x4, waiting for transfers between devices, scan_over(): gots.append(lax.ppermute(total.astype(BF16), axis, pairs))  4.25 us
    ppermute x2, starting transfers between devices, scan_over(): gots = [lax.ppermute(sent, axis, [(i, i ^ 1) for i in range(size)])]  3.37 us
    ppermute x2, waiting for transfers between devices, scan_over(): gots = [lax.ppermute(sent, axis, [(i, i ^ 1) for i in range(size)])]  3.07 us
  transfers between devices with their start and end apart: 27, of which 13 were waited for; matrix products, arithmetic and copies ran while one was open for 0% of the time, Pallas kernels for 21%

commit v1 on v0

--- a/solution.py
+++ b/solution.py
@@ -100,7 +100,7 @@
     copies = [
         pltpu.make_async_copy(source, target, sems.at[i])
         for i, (source, target) in enumerate(
-            ((x_hbm, x_ref), (w_hbm, w_ref), (taps_hbm, taps_ref))
+            ((x_hbm, x_ref), (w_hbm, w_ref), (taps_hbm.at[pl.ds(0, 2)], taps_ref))
         )
     ]
     copies[0].start()
@@ -120,9 +120,12 @@
     hand_out(held, outs)
 
 
-def probe_pair_body(x_ref, k_ref, v_ref, out_ref):
+def probe_pair_body(taps_hbm, x_ref, k_ref, v_ref, out_ref, taps_ref, sem):
+    copy = pltpu.make_async_copy(taps_hbm.at[2], taps_ref, sem)
+    copy.start()
     out_ref[0] = project(x_ref[...], k_ref[...])
     out_ref[1] = project(x_ref[...], v_ref[...])
+    copy.wait()
 
 
 def flip_body(po_ref, tie_ref, out_ref):
@@ -136,8 +139,7 @@
     lax.fori_loop(0, frames * tiles, flip, 0)
 
 
-def conv_body(outer, own_ref, up_ref, down_ref, w_ref, out_ref, wide):
-    main, source, target = outer
+def conv_body(source, target, own_ref, up_ref, down_ref, main_ref, mid_ref, out_ref, wide):
     frames, tile_rows, columns, channels = own_ref.shape
     tokens = tile_rows * columns
     span = (tile_rows + 2) * columns
@@ -154,8 +156,8 @@
                 wide[f * tokens : (f + 1) * tokens, at : at + channels] = part[
                     b * columns : b * columns + tokens
                 ]
-    total = dot(wide[...], w_ref[main])
-    extra = dot(wide[source * tokens : (source + 1) * tokens, :], w_ref[1])
+    total = dot(wide[...], main_ref[...] if len(main_ref.shape) == 2 else main_ref[0])
+    extra = dot(wide[source * tokens : (source + 1) * tokens, :], mid_ref[1])
     for f in range(frames):
         part = total[f * tokens : (f + 1) * tokens]
         part = part + extra if f == target else part
@@ -354,14 +356,18 @@
     assert size % 2 == 0
     gots = [lax.ppermute(sent, axis, [(i, i ^ 1) for i in range(size)])]
     total = total + gots[0].astype(F32)
-    by = 2
-    while by < size:
+    shifts = [2 * k for k in range(1, size // 2)]
+    if len(shifts) > 3:
+        shifts = [2 << k for k in range(len(shifts).bit_length())]
+    paired = total.astype(BF16)
+    for by in shifts:
         pairs = [(i, i + by) for i in range(size - by)]
         if not forward:
             pairs = [(j, i) for i, j in pairs]
-        gots.append(lax.ppermute(total.astype(BF16), axis, pairs))
-        total = total + gots[-1].astype(F32)
-        by *= 2
+        gots.append(lax.ppermute(paired, axis, pairs))
+        if size > 8:
+            total = total + gots[-1].astype(F32)
+            paired = total.astype(BF16)
     return gots
 
 
@@ -384,10 +390,10 @@
     taps = conv_weight.reshape(3, 9 * channels, -1)
     weight_bytes = 2 * D * D
 
-    def conv(outer, dtype):
+    def conv(source, target, main, dtype):
         return call(
-            functools.partial(conv_body, outer),
-            [struct((tokens, taps.shape[2]), dtype)], (video, above, below, taps),
+            functools.partial(conv_body, source, target),
+            [struct((tokens, taps.shape[2]), dtype)], (video, above, below, main, two_taps),
             scratch=[pltpu.VMEM((tokens, taps.shape[1]), BF16)],
             flops=27 * tokens * channels * channels, moved=taps.size + 6 * video.size,
         )[0]
@@ -397,24 +403,24 @@
     grouped = (groups, share, tokens)
     held = pltpu.VMEM(grouped, BF16)
 
-    *query_dot, direction, q_near, taps = call(
+    *query_dot, direction, q_near, two_taps = call(
         probe_body,
         [part] * groups
-        + [struct((tokens, D), BF16), struct(q_weight.shape, BF16), struct(taps.shape, BF16)],
+        + [struct((tokens, D), BF16), struct(q_weight.shape, BF16), struct((2,) + taps.shape[1:], BF16)],
         (probe_in.reshape(tokens, D), q_weight, taps), far=3,
         scratch=[pltpu.VMEM((tokens, D), jnp.int32), held, pltpu.SemaphoreType.DMA((3,))],
         flops=2 * tokens * D * D, moved=weight_bytes + 8 * tokens * D,
     )
     query_dot = exchange(query_dot)
 
-    far = conv((0, 1, 0), BF16)
+    far = conv(1, 0, two_taps, BF16)
     far = lax.ppermute(far, "tm", [(t, t + 1) for t in range(tms - 1)])
-    near = conv((2, 0, 1), F32)
-
-    dots = call(
-        probe_pair_body, [struct(two_tall, BF16)], (direction, k_weight, v_weight),
+    dots, last_tap = call(
+        probe_pair_body, [struct(two_tall, BF16), struct(taps.shape[1:], BF16)],
+        (taps, direction, k_weight, v_weight), far=1, scratch=[pltpu.SemaphoreType.DMA],
         flops=4 * tokens * D * D, moved=2 * weight_bytes + 6 * tokens * D,
-    )[0]
+    )
+    near = conv(0, 1, last_tap, F32)
 
     assert frames == 2
     state_part = struct((HEAD, 2 * share), BF16)

time: 115 us -> 123 us (1.070)
  starting transfers between devices: 35 us -> 45.3 us
    ppermute x4 -> x6, starting transfers between devices: 11.9 us -> 18.4 us  [scan_over(): gots.append(lax.ppermute(paired, axis, pairs))]
    ppermute x18, starting transfers between devices: 10.3 us -> 14.8 us  [exchange(): lax.ppermute(parts[k], 'space', [(i, i ^ k) for i in range(size)])]
    ppermute x2, waiting for transfers between devices: 3.07 us -> 0.56 us  [scan_over(): gots = [lax.ppermute(sent, axis, [(i, i ^ 1) for i in range(size)])]]
    ppermute x18, waiting for transfers between devices: 23.3 us -> 25.6 us  [exchange(): lax.ppermute(parts[k], 'space', [(i, i ^ k) for i in range(size)])]
    ppermute x1, waiting for transfers between devices: 2.48 us -> 1.17 us  [on_device(): far = lax.ppermute(far, 'tm', [(t, t + 1) for t in range(tms - 1)])]
    ppermute x4 -> x6, waiting for transfers between devices: 4.25 us -> 4.85 us  [scan_over(): gots.append(lax.ppermute(paired, axis, pairs))]
  transfers between devices with their start and end apart: 27 -> 29, of which waited for: 13 -> 11; matrix products, arithmetic and copies ran while one was open for 0% -> 0% of each run, Pallas kernels for 21% -> 23%
where the time goes in v1:
time: 123 us
  starting transfers between devices  45.3 us (37%)
  Pallas kernels  43.6 us (35%)
  waiting for transfers between devices  32.2 us (26%)
    pallas_call x14, Pallas kernels, call(): pl.pallas_call(body, in_specs=[anywhere] * far + [vmem] * (len(args) - fa...  43.6 us
    ppermute x18, waiting for transfers between devices, exchange(): lax.ppermute(parts[k], 'space', [(i, i ^ k) for i in range(size)])  25.6 us
    ppermute x6, starting transfers between devices, scan_over(): gots.append(lax.ppermute(paired, axis, pairs))  18.4 us
    ppermute x18, starting transfers between devices, exchange(): lax.ppermute(parts[k], 'space', [(i, i ^ k) for i in range(size)])  14.8 us
    ppermute x6, waiting for transfers between devices, scan_over(): gots.append(lax.ppermute(paired, axis, pairs))  4.85 us
    ppermute x1, starting transfers between devices, on_device(): far = lax.ppermute(far, 'tm', [(t, t + 1) for t in range(tms - 1)])  4.42 us
    ppermute x2, starting transfers between devices, scan_over(): gots = [lax.ppermute(sent, axis, [(i, i ^ 1) for i in range(size)])]  4.06 us
  transfers between devices with their start and end apart: 29, of which 11 were waited for; matrix products, arithmetic and copies ran while one was open for 0% of the time, Pallas kernels for 23%

profile of v1, /device:TPU:0, one launch (start us, length us, event | category | flops | bytes accessed | tf_op | source)
XLA Modules:
  0.0 123.0 jit_solution(2642401977045134394)
XLA Ops:
  0.6 0.8 fusion.1
  1.5 2.4 %collective-permute-start = (bf16[2,1,32,384]{3,2,1,0:T(8,128)(2,1)S(1)}, bf16[2,1,32,384]{3,2,1,0:T(8,128)(2,1)S(1)}, u32[]{:S(2)}, u32[]{:S(2)}) collective-permute-start(bf16[2,1,32,384]{3,2,1,0:T(8,128)(2,1)S(1)} %get-tuple-element.101), channel_id=1, source_target_pairs={{0,1},{1,2},{2,3},{4,5},{5,6},{6,7},{8,9},{9,10},{10,11},{12,13},{... | collective-permute-start | bytes 147464 | tf_op jit(solution)/shard_map/ppermute | solution.py:387
  3.9 1.3 %collective-permute-start.1 = (bf16[2,1,32,384]{3,2,1,0:T(8,128)(2,1)S(1)}, bf16[2,1,32,384]{3,2,1,0:T(8,128)(2,1)S(1)}, u32[]{:S(2)}, u32[]{:S(2)}) collective-permute-start(bf16[2,1,32,384]{3,2,1,0:T(8,128)(2,1)S(1)} %get-tuple-element.100), channel_id=1, source_target_pairs={{1,0},{2,1},{3,2},{5,4},{6,5},{7,6},{9,8},{10,9},{11,10},{13,12},{... | collective-permute-start | bytes 147464 | tf_op jit(solution)/shard_map/ppermute | solution.py:388
  5.2 5.1 %shard_map.120 = (bf16[288,512]{1,0:T(8,128)(2,1)S(1)}, bf16[288,512]{1,0:T(8,128)(2,1)S(1)}, bf16[288,512]{1,0:T(8,128)(2,1)S(1)}, bf16[288,512]{1,0:T(8,128)(2...) custom-call(s32[512,1152]{1,0:T(8,128)} %bitcast.13, ...), custom_call_target="tpu_custom_call" | custom-call | flops 1358954496 | bytes 7372800 | tf_op jit(solution)/shard_map/pallas_call | solution.py:25
  10.3 3.0 %shard_map.123 = bf16[512,384]{1,0:T(8,128)(2,1)S(1)} custom-call(bf16[2,8,32,384]{3,2,1,0:T(8,128)(2,1)S(1)} %copy-done.3, bf16[2,1,32,384]{3,2,1,0:T(8,128)(2,1)S(1)} %collective-permute-done.up_ref, bf16[2,1,32,384]{3,2,1,0:T(8,128)(2,1)S(1)} %collective-permute-done.1.down_ref, bf16[2,3456,384]{2,1,0:T(8,128)(2,1)S(1)} %get-tuple-element.54.mid_ref.main_ref, ...), custom_call_target="tpu_custom_call" | custom-call | flops 2038431744 | bytes 5160960 | tf_op jit(solution)/shard_map/pallas_call | solution.py:25
  13.3 4.4 %collective-permute-start.2 = (bf16[512,384]{1,0:T(8,128)(2,1)S(1)}, bf16[512,384]{1,0:T(8,128)(2,1)S(1)}, u32[]{:S(2)}, u32[]{:S(2)}) collective-permute-start(bf16[512,384]{1,0:T(8,128)(2,1)S(1)} %shard_map.123), channel_id=1, source_target_pairs={{0,4},{4,8},{8,12},{12,16},{16,20},{20,24},{24,28},{1,5},{5,9},{9,... | collective-permute-start | bytes 1179656 | tf_op jit(solution)/shard_map/ppermute | solution.py:417
  17.7 3.6 %shard_map.121 = (bf16[2,1152,512]{2,1,0:T(8,128)(2,1)S(1)}, bf16[3456,384]{1,0:T(8,128)(2,1)S(1)}) custom-call(bf16[3,3456,384]{2,1,0:T(8,128)(2,1)} %bitcast.12, bf16[512,1152]{1,0:T(8,128)(2,1)S(1)} %get-tuple-element.52.x_ref, bf16[1152,1152]{1,0:T(8,128)(2,1)S(1)} %copy-done, bf16[1152,1152]{1,0:T(8,128)(2,1)S(1)} %copy-done.1), custom_call_target="tpu_custom_call" | custom-call | flops 2717908992 | bytes 8847360 | tf_op jit(solution)/shard_map/pallas_call | solution.py:25
  21.4 3.0 %shard_map.122.near_ref = f32[512,384]{1,0:T(8,128)S(1)} custom-call(bf16[2,8,32,384]{3,2,1,0:T(8,128)(2,1)S(1)} %copy-done.3, bf16[2,1,32,384]{3,2,1,0:T(8,128)(2,1)S(1)} %collective-permute-done.up_ref, bf16[2,1,32,384]{3,2,1,0:T(8,128)(2,1)S(1)} %collective-permute-done.1.down_ref, bf16[3456,384]{1,0:T(8,128)(2,1)S(1)} %get-tuple-element.53.main_ref, ...), custom_call_target="tpu_custom_call" | custom-call | flops 2038431744 | bytes 5160960 | tf_op jit(solution)/shard_map/pallas_call | solution.py:25
  24.4 1.2 collective-permute-done.2.far_ref
  25.6 6.3 %shard_map.124 = (bf16[512,1152]{1,0:T(8,128)(2,1)S(1)}, bf16[2,1152,512]{2,1,0:T(8,128)(2,1)S(1)}, bf16[72,576]{1,0:T(8,128)(2,1)S(1)}, bf16[72,576]{1,0:T(8,12...) custom-call(f32[512,384]{1,0:T(8,128)S(1)} %shard_map.122.near_ref, ...), custom_call_target="tpu_custom_call" | custom-call | flops 2717908992 | bytes 13565952 | tf_op jit(solution)/shard_map/pallas_call | solution.py:25
  31.8 1.6 %collective-permute-start.6 = (bf16[72,576]{1,0:T(8,128)(2,1)S(1)}, bf16[72,576]{1,0:T(8,128)(2,1)S(1)}, u32[]{:S(2)}, u32[]{:S(2)}) collective-permute-start(bf16[72,576]{1,0:T(8,128)(2,1)S(1)} %get-tuple-element.63), channel_id=1, source_target_pairs={{0,1},{1,0},{2,3},{3,2},{4,5},{5,4},{6,7},{7,6},{8,9},{9,8},{10,11... | collective-permute-start | bytes 248840 | tf_op jit(solution)/shard_map/ppermute | solution.py:90
  33.5 1.8 %collective-permute-start.7 = (bf16[72,576]{1,0:T(8,128)(2,1)S(1)}, bf16[72,576]{1,0:T(8,128)(2,1)S(1)}, u32[]{:S(2)}, u32[]{:S(2)}) collective-permute-start(bf16[72,576]{1,0:T(8,128)(2,1)S(1)} %get-tuple-element.64), channel_id=1, source_target_pairs={{0,2},{1,3},{2,0},{3,1},{4,6},{5,7},{6,4},{7,5},{8,10},{9,11},{10,... | collective-permute-start | bytes 248840 | tf_op jit(solution)/shard_map/ppermute | solution.py:90
  35.3 1.7 %collective-permute-start.10 = (bf16[72,576]{1,0:T(8,128)(2,1)S(1)}, bf16[72,576]{1,0:T(8,128)(2,1)S(1)}, u32[]{:S(2)}, u32[]{:S(2)}) collective-permute-start(bf16[72,576]{1,0:T(8,128)(2,1)S(1)} %get-tuple-element.68), channel_id=1, source_target_pairs={{0,2},{1,3},{2,0},{3,1},{4,6},{5,7},{6,4},{7,5},{8,10},{9,11},{10,... | collective-permute-start | bytes 248840 | tf_op jit(solution)/shard_map/ppermute | solution.py:90
  37.1 1.7 %collective-permute-done.7.refs_2_.refs_6_ = bf16[72,576]{1,0:T(8,128)(2,1)S(1)} collective-permute-done((bf16[72,576]{1,0:T(8,128)(2,1)S(1)}, bf16[72,576]{1,0:T(8,128)(2,1)S(1)}, u32[]{:S(2)}, u32[]{:S(2)}) %collective-permute-start.7) | collective-permute-done | bytes 82976 | tf_op jit(solution)/shard_map/ppermute | solution.py:90
  38.8 1.5 %collective-permute-done.8.refs_3_.refs_7_ = bf16[72,576]{1,0:T(8,128)(2,1)S(1)} collective-permute-done((bf16[72,576]{1,0:T(8,128)(2,1)S(1)}, bf16[72,576]{1,0:T(8,128)(2,1)S(1)}, u32[]{:S(2)}, u32[]{:S(2)}) %collective-permute-start.8) | collective-permute-done | bytes 82976 | tf_op jit(solution)/shard_map/ppermute | solution.py:90
  40.4 2.5 %collective-permute-start.12 = (bf16[72,576]{1,0:T(8,128)(2,1)S(1)}, bf16[72,576]{1,0:T(8,128)(2,1)S(1)}, u32[]{:S(2)}, u32[]{:S(2)}) collective-permute-start(bf16[72,576]{1,0:T(8,128)(2,1)S(1)} %get-tuple-element.70.tie_ref), channel_id=1, source_target_pairs={{0,4},{4,0},{8,12},{12,8},{16,20},{20,16},{24,28},{28,24},{1,5},{5... | collective-permute-start | bytes 248840 | tf_op jit(solution)/shard_map/ppermute | solution.py:357
  42.9 2.1 %shard_map.125 = (bf16[288,512]{1,0:T(8,128)(2,1)S(1)}, bf16[288,512]{1,0:T(8,128)(2,1)S(1)}, bf16[288,512]{1,0:T(8,128)(2,1)S(1)}, bf16[288,512]{1,0:T(8,128)(2,1)S(1)}) custom-call(bf16[512,1152]{1,0:T(8,128)(2,1)S(1)} %get-tuple-element.56.x_ref, bf16[1152,1152]{1,0:T(8,128)(2,1)S(1)} %get-tuple-element.57.w_ref), custom_call_target="tpu_custom_call" | custom-call | flops 1358954496 | bytes 5013504 | tf_op jit(solution)/shard_map/pallas_call | solution.py:25
  45.0 0.1 collective-permute-start.3
  45.1 2.0 %collective-permute-start.4 = (bf16[288,512]{1,0:T(8,128)(2,1)S(1)}, bf16[288,512]{1,0:T(8,128)(2,1)S(1)}, u32[]{:S(2)}, u32[]{:S(2)}) collective-permute-start(bf16[288,512]{1,0:T(8,128)(2,1)S(1)} %get-tuple-element.60), channel_id=1, source_target_pairs={{0,2},{1,3},{2,0},{3,1},{4,6},{5,7},{6,4},{7,5},{8,10},{9,11},{10,... | collective-permute-start | bytes 884744 | tf_op jit(solution)/shard_map/ppermute | solution.py:90
  47.1 1.7 %collective-permute-start.11 = (bf16[72,576]{1,0:T(8,128)(2,1)S(1)}, bf16[72,576]{1,0:T(8,128)(2,1)S(1)}, u32[]{:S(2)}, u32[]{:S(2)}) collective-permute-start(bf16[72,576]{1,0:T(8,128)(2,1)S(1)} %get-tuple-element.69), channel_id=1, source_target_pairs={{0,3},{1,2},{2,1},{3,0},{4,7},{5,6},{6,5},{7,4},{8,11},{9,10},{10,... | collective-permute-start | bytes 248840 | tf_op jit(solution)/shard_map/ppermute | solution.py:90
  48.9 13.4 %collective-permute-done.11.refs_11_ = bf16[72,576]{1,0:T(8,128)(2,1)S(1)} collective-permute-done((bf16[72,576]{1,0:T(8,128)(2,1)S(1)}, bf16[72,576]{1,0:T(8,128)(2,1)S(1)}, u32[]{:S(2)}, u32[]{:S(2)}) %collective-permute-start.11) | collective-permute-done | bytes 82976 | tf_op jit(solution)/shard_map/ppermute | solution.py:90
  62.3 3.5 %collective-permute-start.13 = (bf16[72,576]{1,0:T(8,128)(2,1)S(1)}, bf16[72,576]{1,0:T(8,128)(2,1)S(1)}, u32[]{:S(2)}, u32[]{:S(2)}) collective-permute-start(bf16[72,576]{1,0:T(8,128)(2,1)S(1)} %add_convert_fusion), channel_id=1, source_target_pairs={{0,8},{4,12},{8,16},{12,20},{16,24},{20,28},{1,9},{5,13},{9,17},{1... | collective-permute-start | bytes 248840 | tf_op jit(solution)/shard_map/ppermute | solution.py:367
  65.7 4.5 %collective-permute-start.14 = (bf16[72,576]{1,0:T(8,128)(2,1)S(1)}, bf16[72,576]{1,0:T(8,128)(2,1)S(1)}, u32[]{:S(2)}, u32[]{:S(2)}) collective-permute-start(bf16[72,576]{1,0:T(8,128)(2,1)S(1)} %add_convert_fusion), channel_id=1, source_target_pairs={{0,16},{4,20},{8,24},{12,28},{1,17},{5,21},{9,25},{13,29},{2,18},{... | collective-permute-start | bytes 248840 | tf_op jit(solution)/shard_map/ppermute | solution.py:367
  70.3 0.1 collective-permute-start.20
  70.3 2.1 %collective-permute-done.14.refs_14_ = bf16[72,576]{1,0:T(8,128)(2,1)S(1)} collective-permute-done((bf16[72,576]{1,0:T(8,128)(2,1)S(1)}, bf16[72,576]{1,0:T(8,128)(2,1)S(1)}, u32[]{:S(2)}, u32[]{:S(2)}) %collective-permute-start.14) | collective-permute-done | bytes 82976 | tf_op jit(solution)/shard_map/ppermute | solution.py:367
  72.4 6.5 %collective-permute-start.15 = (bf16[72,576]{1,0:T(8,128)(2,1)S(1)}, bf16[72,576]{1,0:T(8,128)(2,1)S(1)}, u32[]{:S(2)}, u32[]{:S(2)}) collective-permute-start(bf16[72,576]{1,0:T(8,128)(2,1)S(1)} %add_convert_fusion), channel_id=1, source_target_pairs={{0,24},{4,28},{1,25},{5,29},{2,26},{6,30},{3,27},{7,31}} | collective-permute-start | bytes 248840 | tf_op jit(solution)/shard_map/ppermute | solution.py:367
  79.0 1.1 shard_map.127.refs_17_
  80.1 0.8 collective-permute-done.15.refs_15_
  80.9 1.6 %collective-permute-start.21 = (bf16[288,512]{1,0:T(8,128)(2,1)S(1)}, bf16[288,512]{1,0:T(8,128)(2,1)S(1)}, u32[]{:S(2)}, u32[]{:S(2)}) collective-permute-start(bf16[288,512]{1,0:T(8,128)(2,1)S(1)} %get-tuple-element.80), channel_id=1, source_target_pairs={{0,2},{1,3},{2,0},{3,1},{4,6},{5,7},{6,4},{7,5},{8,10},{9,11},{10,... | collective-permute-start | bytes 884744 | tf_op jit(solution)/shard_map/ppermute | solution.py:90
  82.5 5.6 %shard_map.128 = (bf16[288,512]{1,0:T(8,128)(2,1)S(1)}, bf16[288,512]{1,0:T(8,128)(2,1)S(1)}, bf16[288,512]{1,0:T(8,128)(2,1)S(1)}, bf16[288,512]{1,0:T(8,128)(2...) custom-call(bf16[288,512]{1,0:T(8,128)(2,1)S(1)} %get-tuple-element., ...), custom_call_target="tpu_custom_call" | custom-call | flops 1019215872 | bytes 5898240 | tf_op jit(solution)/shard_map/pallas_call | solution.py:25
  88.1 1.5 %collective-permute-start.16 = (bf16[72,288]{1,0:T(8,128)(2,1)S(1)}, bf16[72,288]{1,0:T(8,128)(2,1)S(1)}, u32[]{:S(2)}, u32[]{:S(2)}) collective-permute-start(bf16[72,288]{1,0:T(8,128)(2,1)S(1)} %get-tuple-element.73), channel_id=1, source_target_pairs={{0,4},{4,0},{8,12},{12,8},{16,20},{20,16},{24,28},{28,24},{1,5},{5... | collective-permute-start | bytes 124424 | tf_op jit(solution)/shard_map/ppermute | solution.py:357
  89.6 0.5 collective-permute-start.26
  90.2 1.6 %collective-permute-start.27 = (bf16[288,512]{1,0:T(8,128)(2,1)S(1)}, bf16[288,512]{1,0:T(8,128)(2,1)S(1)}, u32[]{:S(2)}, u32[]{:S(2)}) collective-permute-start(bf16[288,512]{1,0:T(8,128)(2,1)S(1)} %get-tuple-element.97), channel_id=1, source_target_pairs={{0,2},{1,3},{2,0},{3,1},{4,6},{5,7},{6,4},{7,5},{8,10},{9,11},{10,... | collective-permute-start | bytes 884744 | tf_op jit(solution)/shard_map/ppermute | solution.py:90
  91.8 0.6 collective-permute-done.16.refs_0_
  92.3 1.3 %collective-permute-start.17 = (bf16[72,288]{1,0:T(8,128)(2,1)S(1)}, bf16[72,288]{1,0:T(8,128)(2,1)S(1)}, u32[]{:S(2)}, u32[]{:S(2)}) collective-permute-start(bf16[72,288]{1,0:T(8,128)(2,1)S(1)} %fusion), channel_id=1, source_target_pairs={{8,0},{12,4},{16,8},{20,12},{24,16},{28,20},{9,1},{13,5},{17,9},{2... | collective-permute-start | bytes 124424 | tf_op jit(solution)/shard_map/ppermute | solution.py:367
  93.6 5.3 %collective-permute-done.22.refs_3_ = bf16[288,512]{1,0:T(8,128)(2,1)S(1)} collective-permute-done((bf16[288,512]{1,0:T(8,128)(2,1)S(1)}, bf16[288,512]{1,0:T(8,128)(2,1)S(1)}, u32[]{:S(2)}, u32[]{:S(2)}) %collective-permute-start.22) | collective-permute-done | bytes 294944 | tf_op jit(solution)/shard_map/ppermute | solution.py:90
  98.9 1.3 %collective-permute-start.18 = (bf16[72,288]{1,0:T(8,128)(2,1)S(1)}, bf16[72,288]{1,0:T(8,128)(2,1)S(1)}, u32[]{:S(2)}, u32[]{:S(2)}) collective-permute-start(bf16[72,288]{1,0:T(8,128)(2,1)S(1)} %fusion), channel_id=1, source_target_pairs={{16,0},{20,4},{24,8},{28,12},{17,1},{21,5},{25,9},{29,13},{18,2},{... | collective-permute-start | bytes 124424 | tf_op jit(solution)/shard_map/ppermute | solution.py:367
  100.2 1.3 %collective-permute-start.19 = (bf16[72,288]{1,0:T(8,128)(2,1)S(1)}, bf16[72,288]{1,0:T(8,128)(2,1)S(1)}, u32[]{:S(2)}, u32[]{:S(2)}) collective-permute-start(bf16[72,288]{1,0:T(8,128)(2,1)S(1)} %fusion), channel_id=1, source_target_pairs={{24,0},{28,4},{25,1},{29,5},{26,2},{30,6},{27,3},{31,7}} | collective-permute-start | bytes 124424 | tf_op jit(solution)/shard_map/ppermute | solution.py:367
  101.5 4.6 %shard_map.130 = (bf16[2,4,256,288]{3,2,1,0:T(8,128)(2,1)}, bf16[2,4,256,288]{3,2,1,0:T(8,128)(2,1)}) custom-call(bf16[288,512]{1,0:T(8,128)(2,1)S(1)} %get-tuple-element.78.refs_0_, bf16[288,512]{1,0:T(8,128)(2,1)S(1)} %collective-permute-done.20.refs_1_, bf16[288,512]{1,0:T(8,128)(2,1)S(1)} %collective-permute-done.21.refs_2_, ...), custom_call_target="tpu_custom_call" | custom-call | flops 1019215872 | bytes 5898240 | tf_op jit(solution)/shard_map/pallas_call | solution.py:25
  106.1 2.0 %collective-permute-done.19.refs_3_ = bf16[72,288]{1,0:T(8,128)(2,1)S(1)} collective-permute-done((bf16[72,288]{1,0:T(8,128)(2,1)S(1)}, bf16[72,288]{1,0:T(8,128)(2,1)S(1)}, u32[]{:S(2)}, u32[]{:S(2)}) %collective-permute-start.19) | collective-permute-done | bytes 41504 | tf_op jit(solution)/shard_map/ppermute | solution.py:367
  108.1 0.1 shard_map.129
  108.2 1.5 %shard_map.133 = f32[8,4,72,72]{3,2,1,0:T(8,128)} custom-call(f32[4,2,72,288]{3,2,1,0:T(8,128)S(1)} %get-tuple-element.72.suffix_ref, f32[72,288]{1,0:T(8,128)S(1)} %get-tuple-element.99.after_ref), custom_call_target="tpu_custom_call" | custom-call | bytes 1658880 | tf_op jit(solution)/shard_map/pallas_call | solution.py:25
  109.6 0.4 collective-permute-start.24
  110.1 1.4 %collective-permute-start.25 = (bf16[2,72,288]{2,1,0:T(8,128)(2,1)S(1)}, bf16[2,72,288]{2,1,0:T(8,128)(2,1)S(1)}, u32[]{:S(2)}, u32[]{:S(2)}) collective-permute-start(bf16[2,72,288]{2,1,0:T(8,128)(2,1)S(1)} %get-tuple-element.93), channel_id=1, source_target_pairs={{0,3},{1,2},{2,1},{3,0},{4,7},{5,6},{6,5},{7,4},{8,11},{9,10},{10,... | collective-permute-start | bytes 248840 | tf_op jit(solution)/shard_map/ppermute | solution.py:90
  111.5 1.8 %shard_map.131.refs_5_ = f32[1152,512]{1,0:T(8,128)S(1)} custom-call(bf16[1152,1152]{1,0:T(8,128)(2,1)S(1)} %get-tuple-element.57.w_ref, bf16[288,512]{1,0:T(8,128)(2,1)S(1)} %get-tuple-element.95.refs_0_, bf16[288,512]{1,0:T(8,128)(2,1)S(1)} %collective-permute-done.26.refs_1_, bf16[288,512]{1,0:T(8,128)(2,1)S(1)} %collective-permute-done.27.refs_2_, ...), custom_call_target="tpu_custom_call" | custom-call | flops 1358954496 | bytes 6193152 | tf_op jit(solution)/shard_map/pallas_call | solution.py:25
  113.3 2.3 %collective-permute-done.24.refs_2_ = bf16[2,72,288]{2,1,0:T(8,128)(2,1)S(1)} collective-permute-done((bf16[2,72,288]{2,1,0:T(8,128)(2,1)S(1)}, bf16[2,72,288]{2,1,0:T(8,128)(2,1)S(1)}, u32[]{:S(2)}, u32[]{:S(2)}) %collective-permute-start.24) | collective-permute-done | bytes 82976 | tf_op jit(solution)/shard_map/ppermute | solution.py:90
  115.6 1.4 %collective-permute-done.25.refs_3_ = bf16[2,72,288]{2,1,0:T(8,128)(2,1)S(1)} collective-permute-done((bf16[2,72,288]{2,1,0:T(8,128)(2,1)S(1)}, bf16[2,72,288]{2,1,0:T(8,128)(2,1)S(1)}, u32[]{:S(2)}, u32[]{:S(2)}) %collective-permute-start.25) | collective-permute-done | bytes 82976 | tf_op jit(solution)/shard_map/ppermute | solution.py:90
  117.0 6.0 %shard_map.132 = bf16[512,1152]{1,0:T(8,128)(2,1)} custom-call(bf16[2,72,288]{2,1,0:T(8,128)(2,1)S(1)} %get-tuple-element.90.refs_0_, bf16[2,72,288]{2,1,0:T(8,128)(2,1)S(1)} %collective-permute-done.23.refs_1_, bf16[2,72,288]{2,1,0:T(8,128)(2,1)S(1)} %collective-permute-done.24.refs_2_, bf16[2,72,288]{2,1,0:T(8,128)(2,1)S(1)} %collective-permute-done.25.refs_3_, ...), custom_call_target="tpu_custom_call" | custom-call | flops 2717908992 | bytes 11206656 | tf_op jit(solution)/shard_map/pallas_call | solution.py:25
  (39 shorter events, 0.2 us)
Async XLA Ops:
  1.5 8.8 %collective-permute-start = (bf16[2,1,32,384]{3,2,1,0:T(8,128)(2,1)S(1)}, bf16[2,1,32,384]{3,2,1,0:T(8,128)(2,1)S(1)}, u32[]{:S(2)}, u32[]{:S(2)}) collective-permute-start(bf16[2,1,32,384]{3,2,1,0:T(8,128)(2,1)S(1)} %get-tuple-element.101), channel_id=1, source_target_pairs={{0,1},{1,2},{2,3},{4,5},{5,6},{6,7},{8,9},{9,10},{10,11},{12,13},{... | collective-permute-start | bytes 147464 | tf_op jit(solution)/shard_map/ppermute | solution.py:387
  3.9 6.4 %collective-permute-start.1 = (bf16[2,1,32,384]{3,2,1,0:T(8,128)(2,1)S(1)}, bf16[2,1,32,384]{3,2,1,0:T(8,128)(2,1)S(1)}, u32[]{:S(2)}, u32[]{:S(2)}) collective-permute-start(bf16[2,1,32,384]{3,2,1,0:T(8,128)(2,1)S(1)} %get-tuple-element.100), channel_id=1, source_target_pairs={{1,0},{2,1},{3,2},{5,4},{6,5},{7,6},{9,8},{10,9},{11,10},{13,12},{... | collective-permute-start | bytes 147464 | tf_op jit(solution)/shard_map/ppermute | solution.py:388
  5.2 5.1 %copy-start.3 = (bf16[2,8,32,384]{3,2,1,0:T(8,128)(2,1)S(1)}, bf16[2,8,32,384]{3,2,1,0:T(8,128)(2,1)}, u32[]{:S(2)}) copy-start(bf16[2,8,32,384]{3,2,1,0:T(8,128)(2,1)} %own_ref.3) | copy-start | bytes 1179652
  10.3 7.4 %copy-start = (bf16[1152,1152]{1,0:T(8,128)(2,1)S(1)}, bf16[1152,1152]{1,0:T(8,128)(2,1)}, u32[]{:S(2)}) copy-start(bf16[1152,1152]{1,0:T(8,128)(2,1)} %refs_6_.1) | copy-start | bytes 7962628
  10.3 7.4 %copy-start.1 = (bf16[1152,1152]{1,0:T(8,128)(2,1)S(1)}, bf16[1152,1152]{1,0:T(8,128)(2,1)}, u32[]{:S(2)}) copy-start(bf16[1152,1152]{1,0:T(8,128)(2,1)} %refs_7_.1) | copy-start | bytes 7962628
  13.3 12.2 %collective-permute-start.2 = (bf16[512,384]{1,0:T(8,128)(2,1)S(1)}, bf16[512,384]{1,0:T(8,128)(2,1)S(1)}, u32[]{:S(2)}, u32[]{:S(2)}) collective-permute-start(bf16[512,384]{1,0:T(8,128)(2,1)S(1)} %shard_map.123), channel_id=1, source_target_pairs={{0,4},{4,8},{8,12},{12,16},{16,20},{20,24},{24,28},{1,5},{5,9},{9,... | collective-permute-start | bytes 1179656 | tf_op jit(solution)/shard_map/ppermute | solution.py:417
  21.4 4.2 %copy-start.4 = (bf16[384,1152]{1,0:T(8,128)(2,1)S(1)}, bf16[384,1152]{1,0:T(8,128)(2,1)}, u32[]{:S(2)}) copy-start(bf16[384,1152]{1,0:T(8,128)(2,1)} %embed_ref.1) | copy-start | bytes 2654212
  31.8 5.3 %collective-permute-start.6 = (bf16[72,576]{1,0:T(8,128)(2,1)S(1)}, bf16[72,576]{1,0:T(8,128)(2,1)S(1)}, u32[]{:S(2)}, u32[]{:S(2)}) collective-permute-start(bf16[72,576]{1,0:T(8,128)(2,1)S(1)} %get-tuple-element.63), channel_id=1, source_target_pairs={{0,1},{1,0},{2,3},{3,2},{4,5},{5,4},{6,7},{7,6},{8,9},{9,8},{10,11... | collective-permute-start | bytes 248840 | tf_op jit(solution)/shard_map/ppermute | solution.py:90
  33.5 5.3 %collective-permute-start.7 = (bf16[72,576]{1,0:T(8,128)(2,1)S(1)}, bf16[72,576]{1,0:T(8,128)(2,1)S(1)}, u32[]{:S(2)}, u32[]{:S(2)}) collective-permute-start(bf16[72,576]{1,0:T(8,128)(2,1)S(1)} %get-tuple-element.64), channel_id=1, source_target_pairs={{0,2},{1,3},{2,0},{3,1},{4,6},{5,7},{6,4},{7,5},{8,10},{9,11},{10,... | collective-permute-start | bytes 248840 | tf_op jit(solution)/shard_map/ppermute | solution.py:90
  35.3 5.0 %collective-permute-start.8 = (bf16[72,576]{1,0:T(8,128)(2,1)S(1)}, bf16[72,576]{1,0:T(8,128)(2,1)S(1)}, u32[]{:S(2)}, u32[]{:S(2)}) collective-permute-start(bf16[72,576]{1,0:T(8,128)(2,1)S(1)} %get-tuple-element.65), channel_id=1, source_target_pairs={{0,3},{1,2},{2,1},{3,0},{4,7},{5,6},{6,5},{7,4},{8,11},{9,10},{10,... | collective-permute-start | bytes 248840 | tf_op jit(solution)/shard_map/ppermute | solution.py:90
  35.3 11.8 %collective-permute-start.10 = (bf16[72,576]{1,0:T(8,128)(2,1)S(1)}, bf16[72,576]{1,0:T(8,128)(2,1)S(1)}, u32[]{:S(2)}, u32[]{:S(2)}) collective-permute-start(bf16[72,576]{1,0:T(8,128)(2,1)S(1)} %get-tuple-element.68), channel_id=1, source_target_pairs={{0,2},{1,3},{2,0},{3,1},{4,6},{5,7},{6,4},{7,5},{8,10},{9,11},{10,... | collective-permute-start | bytes 248840 | tf_op jit(solution)/shard_map/ppermute | solution.py:90
  40.4 8.5 %collective-permute-start.12 = (bf16[72,576]{1,0:T(8,128)(2,1)S(1)}, bf16[72,576]{1,0:T(8,128)(2,1)S(1)}, u32[]{:S(2)}, u32[]{:S(2)}) collective-permute-start(bf16[72,576]{1,0:T(8,128)(2,1)S(1)} %get-tuple-element.70.tie_ref), channel_id=1, source_target_pairs={{0,4},{4,0},{8,12},{12,8},{16,20},{20,16},{24,28},{28,24},{1,5},{5... | collective-permute-start | bytes 248840 | tf_op jit(solution)/shard_map/ppermute | solution.py:357
  42.9 36.1 %copy-start.2 = (s32[2,32,32,288]{3,2,1,0:T(8,128)S(1)}, s32[2,32,32,288]{3,2,1,0:T(8,128)}, u32[]{:S(2)}) copy-start(s32[2,32,32,288]{3,2,1,0:T(8,128)} %param.17) | copy-start | bytes 7077892
  45.0 37.5 %collective-permute-start.3 = (bf16[288,512]{1,0:T(8,128)(2,1)S(1)}, bf16[288,512]{1,0:T(8,128)(2,1)S(1)}, u32[]{:S(2)}, u32[]{:S(2)}) collective-permute-start(bf16[288,512]{1,0:T(8,128)(2,1)S(1)} %get-tuple-element.59), channel_id=1, source_target_pairs={{0,1},{1,0},{2,3},{3,2},{4,5},{5,4},{6,7},{7,6},{8,9},{9,8},{10,11... | collective-permute-start | bytes 884744 | tf_op jit(solution)/shard_map/ppermute | solution.py:90
  45.1 37.4 %collective-permute-start.4 = (bf16[288,512]{1,0:T(8,128)(2,1)S(1)}, bf16[288,512]{1,0:T(8,128)(2,1)S(1)}, u32[]{:S(2)}, u32[]{:S(2)}) collective-permute-start(bf16[288,512]{1,0:T(8,128)(2,1)S(1)} %get-tuple-element.60), channel_id=1, source_target_pairs={{0,2},{1,3},{2,0},{3,1},{4,6},{5,7},{6,4},{7,5},{8,10},{9,11},{10,... | collective-permute-start | bytes 884744 | tf_op jit(solution)/shard_map/ppermute | solution.py:90
  47.1 35.4 %collective-permute-start.5 = (bf16[288,512]{1,0:T(8,128)(2,1)S(1)}, bf16[288,512]{1,0:T(8,128)(2,1)S(1)}, u32[]{:S(2)}, u32[]{:S(2)}) collective-permute-start(bf16[288,512]{1,0:T(8,128)(2,1)S(1)} %get-tuple-element.61), channel_id=1, source_target_pairs={{0,3},{1,2},{2,1},{3,0},{4,7},{5,6},{6,5},{7,4},{8,11},{9,10},{10,... | collective-permute-start | bytes 884744 | tf_op jit(solution)/shard_map/ppermute | solution.py:90
  47.1 15.1 %collective-permute-start.11 = (bf16[72,576]{1,0:T(8,128)(2,1)S(1)}, bf16[72,576]{1,0:T(8,128)(2,1)S(1)}, u32[]{:S(2)}, u32[]{:S(2)}) collective-permute-start(bf16[72,576]{1,0:T(8,128)(2,1)S(1)} %get-tuple-element.69), channel_id=1, source_target_pairs={{0,3},{1,2},{2,1},{3,0},{4,7},{5,6},{6,5},{7,4},{8,11},{9,10},{10,... | collective-permute-start | bytes 248840 | tf_op jit(solution)/shard_map/ppermute | solution.py:90
  48.9 16.9 %collective-permute-start.9 = (bf16[72,576]{1,0:T(8,128)(2,1)S(1)}, bf16[72,576]{1,0:T(8,128)(2,1)S(1)}, u32[]{:S(2)}, u32[]{:S(2)}) collective-permute-start(bf16[72,576]{1,0:T(8,128)(2,1)S(1)} %get-tuple-element.67), channel_id=1, source_target_pairs={{0,1},{1,0},{2,3},{3,2},{4,5},{5,4},{6,7},{7,6},{8,9},{9,8},{10,11... | collective-permute-start | bytes 248840 | tf_op jit(solution)/shard_map/ppermute | solution.py:90
  48.9 33.6 %copy-start.5 = (f32[4,72,72]{2,1,0:T(8,128)S(1)}, f32[4,72,72]{2,1,0:T(8,128)}, u32[]{:S(2)}) copy-start(f32[4,72,72]{2,1,0:T(8,128)} %refs_16_.1) | copy-start | bytes 248836
  62.3 8.0 %collective-permute-start.13 = (bf16[72,576]{1,0:T(8,128)(2,1)S(1)}, bf16[72,576]{1,0:T(8,128)(2,1)S(1)}, u32[]{:S(2)}, u32[]{:S(2)}) collective-permute-start(bf16[72,576]{1,0:T(8,128)(2,1)S(1)} %add_convert_fusion), channel_id=1, source_target_pairs={{0,8},{4,12},{8,16},{12,20},{16,24},{20,28},{1,9},{5,13},{9,17},{1... | collective-permute-start | bytes 248840 | tf_op jit(solution)/shard_map/ppermute | solution.py:367
  65.7 6.7 %collective-permute-start.14 = (bf16[72,576]{1,0:T(8,128)(2,1)S(1)}, bf16[72,576]{1,0:T(8,128)(2,1)S(1)}, u32[]{:S(2)}, u32[]{:S(2)}) collective-permute-start(bf16[72,576]{1,0:T(8,128)(2,1)S(1)} %add_convert_fusion), channel_id=1, source_target_pairs={{0,16},{4,20},{8,24},{12,28},{1,17},{5,21},{9,25},{13,29},{2,18},{... | collective-permute-start | bytes 248840 | tf_op jit(solution)/shard_map/ppermute | solution.py:367
  70.3 19.9 %collective-permute-start.20 = (bf16[288,512]{1,0:T(8,128)(2,1)S(1)}, bf16[288,512]{1,0:T(8,128)(2,1)S(1)}, u32[]{:S(2)}, u32[]{:S(2)}) collective-permute-start(bf16[288,512]{1,0:T(8,128)(2,1)S(1)} %get-tuple-element.79), channel_id=1, source_target_pairs={{0,1},{1,0},{2,3},{3,2},{4,5},{5,4},{6,7},{7,6},{8,9},{9,8},{10,11... | collective-permute-start | bytes 884744 | tf_op jit(solution)/shard_map/ppermute | solution.py:90
  72.4 8.4 %collective-permute-start.15 = (bf16[72,576]{1,0:T(8,128)(2,1)S(1)}, bf16[72,576]{1,0:T(8,128)(2,1)S(1)}, u32[]{:S(2)}, u32[]{:S(2)}) collective-permute-start(bf16[72,576]{1,0:T(8,128)(2,1)S(1)} %add_convert_fusion), channel_id=1, source_target_pairs={{0,24},{4,28},{1,25},{5,29},{2,26},{6,30},{3,27},{7,31}} | collective-permute-start | bytes 248840 | tf_op jit(solution)/shard_map/ppermute | solution.py:367
  80.9 11.4 %collective-permute-start.21 = (bf16[288,512]{1,0:T(8,128)(2,1)S(1)}, bf16[288,512]{1,0:T(8,128)(2,1)S(1)}, u32[]{:S(2)}, u32[]{:S(2)}) collective-permute-start(bf16[288,512]{1,0:T(8,128)(2,1)S(1)} %get-tuple-element.80), channel_id=1, source_target_pairs={{0,2},{1,3},{2,0},{3,1},{4,6},{5,7},{6,4},{7,5},{8,10},{9,11},{10,... | collective-permute-start | bytes 884744 | tf_op jit(solution)/shard_map/ppermute | solution.py:90
  88.1 4.2 %collective-permute-start.16 = (bf16[72,288]{1,0:T(8,128)(2,1)S(1)}, bf16[72,288]{1,0:T(8,128)(2,1)S(1)}, u32[]{:S(2)}, u32[]{:S(2)}) collective-permute-start(bf16[72,288]{1,0:T(8,128)(2,1)S(1)} %get-tuple-element.73), channel_id=1, source_target_pairs={{0,4},{4,0},{8,12},{12,8},{16,20},{20,16},{24,28},{28,24},{1,5},{5... | collective-permute-start | bytes 124424 | tf_op jit(solution)/shard_map/ppermute | solution.py:357
  89.6 9.3 %collective-permute-start.22 = (bf16[288,512]{1,0:T(8,128)(2,1)S(1)}, bf16[288,512]{1,0:T(8,128)(2,1)S(1)}, u32[]{:S(2)}, u32[]{:S(2)}) collective-permute-start(bf16[288,512]{1,0:T(8,128)(2,1)S(1)} %get-tuple-element.81), channel_id=1, source_target_pairs={{0,3},{1,2},{2,1},{3,0},{4,7},{5,6},{6,5},{7,4},{8,11},{9,10},{10,... | collective-permute-start | bytes 884744 | tf_op jit(solution)/shard_map/ppermute | solution.py:90
  89.6 20.4 %collective-permute-start.26 = (bf16[288,512]{1,0:T(8,128)(2,1)S(1)}, bf16[288,512]{1,0:T(8,128)(2,1)S(1)}, u32[]{:S(2)}, u32[]{:S(2)}) collective-permute-start(bf16[288,512]{1,0:T(8,128)(2,1)S(1)} %get-tuple-element.96), channel_id=1, source_target_pairs={{0,1},{1,0},{2,3},{3,2},{4,5},{5,4},{6,7},{7,6},{8,9},{9,8},{10,11... | collective-permute-start | bytes 884744 | tf_op jit(solution)/shard_map/ppermute | solution.py:90
  90.2 21.3 %collective-permute-start.27 = (bf16[288,512]{1,0:T(8,128)(2,1)S(1)}, bf16[288,512]{1,0:T(8,128)(2,1)S(1)}, u32[]{:S(2)}, u32[]{:S(2)}) collective-permute-start(bf16[288,512]{1,0:T(8,128)(2,1)S(1)} %get-tuple-element.97), channel_id=1, source_target_pairs={{0,2},{1,3},{2,0},{3,1},{4,6},{5,7},{6,4},{7,5},{8,10},{9,11},{10,... | collective-permute-start | bytes 884744 | tf_op jit(solution)/shard_map/ppermute | solution.py:90
  92.3 19.2 %collective-permute-start.28 = (bf16[288,512]{1,0:T(8,128)(2,1)S(1)}, bf16[288,512]{1,0:T(8,128)(2,1)S(1)}, u32[]{:S(2)}, u32[]{:S(2)}) collective-permute-start(bf16[288,512]{1,0:T(8,128)(2,1)S(1)} %get-tuple-element.98), channel_id=1, source_target_pairs={{0,3},{1,2},{2,1},{3,0},{4,7},{5,6},{6,5},{7,4},{8,11},{9,10},{10,... | collective-permute-start | bytes 884744 | tf_op jit(solution)/shard_map/ppermute | solution.py:90
  92.3 7.9 %collective-permute-start.17 = (bf16[72,288]{1,0:T(8,128)(2,1)S(1)}, bf16[72,288]{1,0:T(8,128)(2,1)S(1)}, u32[]{:S(2)}, u32[]{:S(2)}) collective-permute-start(bf16[72,288]{1,0:T(8,128)(2,1)S(1)} %fusion), channel_id=1, source_target_pairs={{8,0},{12,4},{16,8},{20,12},{24,16},{28,20},{9,1},{13,5},{17,9},{2... | collective-permute-start | bytes 124424 | tf_op jit(solution)/shard_map/ppermute | solution.py:367
  98.9 7.2 %collective-permute-start.18 = (bf16[72,288]{1,0:T(8,128)(2,1)S(1)}, bf16[72,288]{1,0:T(8,128)(2,1)S(1)}, u32[]{:S(2)}, u32[]{:S(2)}) collective-permute-start(bf16[72,288]{1,0:T(8,128)(2,1)S(1)} %fusion), channel_id=1, source_target_pairs={{16,0},{20,4},{24,8},{28,12},{17,1},{21,5},{25,9},{29,13},{18,2},{... | collective-permute-start | bytes 124424 | tf_op jit(solution)/shard_map/ppermute | solution.py:367
  100.2 7.8 %collective-permute-start.19 = (bf16[72,288]{1,0:T(8,128)(2,1)S(1)}, bf16[72,288]{1,0:T(8,128)(2,1)S(1)}, u32[]{:S(2)}, u32[]{:S(2)}) collective-permute-start(bf16[72,288]{1,0:T(8,128)(2,1)S(1)} %fusion), channel_id=1, source_target_pairs={{24,0},{28,4},{25,1},{29,5},{26,2},{30,6},{27,3},{31,7}} | collective-permute-start | bytes 124424 | tf_op jit(solution)/shard_map/ppermute | solution.py:367
  109.6 3.7 %collective-permute-start.23 = (bf16[2,72,288]{2,1,0:T(8,128)(2,1)S(1)}, bf16[2,72,288]{2,1,0:T(8,128)(2,1)S(1)}, u32[]{:S(2)}, u32[]{:S(2)}) collective-permute-start(bf16[2,72,288]{2,1,0:T(8,128)(2,1)S(1)} %get-tuple-element.91), channel_id=1, source_target_pairs={{0,1},{1,0},{2,3},{3,2},{4,5},{5,4},{6,7},{7,6},{8,9},{9,8},{10,11... | collective-permute-start | bytes 248840 | tf_op jit(solution)/shard_map/ppermute | solution.py:90
  109.6 5.9 %collective-permute-start.24 = (bf16[2,72,288]{2,1,0:T(8,128)(2,1)S(1)}, bf16[2,72,288]{2,1,0:T(8,128)(2,1)S(1)}, u32[]{:S(2)}, u32[]{:S(2)}) collective-permute-start(bf16[2,72,288]{2,1,0:T(8,128)(2,1)S(1)} %get-tuple-element.92), channel_id=1, source_target_pairs={{0,2},{1,3},{2,0},{3,1},{4,6},{5,7},{6,4},{7,5},{8,10},{9,11},{10,... | collective-permute-start | bytes 248840 | tf_op jit(solution)/shard_map/ppermute | solution.py:90
  110.1 6.9 %collective-permute-start.25 = (bf16[2,72,288]{2,1,0:T(8,128)(2,1)S(1)}, bf16[2,72,288]{2,1,0:T(8,128)(2,1)S(1)}, u32[]{:S(2)}, u32[]{:S(2)}) collective-permute-start(bf16[2,72,288]{2,1,0:T(8,128)(2,1)S(1)} %get-tuple-element.93), channel_id=1, source_target_pairs={{0,3},{1,2},{2,1},{3,0},{4,7},{5,6},{6,5},{7,4},{8,11},{9,10},{10,... | collective-permute-start | bytes 248840 | tf_op jit(solution)/shard_map/ppermute | solution.py:90

commit v2 on v1

--- a/solution.py
+++ b/solution.py
@@ -165,14 +165,14 @@
 
 
 def state_body(near_ref, far_ref, embed_ref, dots, k_ref, v_ref, latent, both, *rest):
-    *outs, state_ref = rest
-    groups = state_ref.shape[1]
+    *outs, state_ref, first_ref = rest
+    groups = state_ref.shape[0]
     u = near_ref[...] + far_ref[...].astype(F32)
     active = (u / (1.0 + jnp.exp(-u))).astype(BF16)
     latent[...] = dot(active, embed_ref[...]).astype(BF16)
     both[0] = project(latent[...], k_ref[...])
     both[1] = project(latent[...], v_ref[...])
-    share = state_ref.shape[3] // 2
+    share = state_ref.shape[2] // 2
 
     def group(g, _):
         for half in range(share // PAIR):
@@ -187,13 +187,15 @@
             for kind in range(2):
                 to = kind * share + half * PAIR
                 first, second = blocks[0][kind], blocks[1][kind]
-                state_ref[0, g, :, to : to + PAIR] = (first + second).astype(BF16)
-                state_ref[1, g, :, to : to + PAIR] = first.astype(BF16)
+                state_ref[g, :, to : to + PAIR] = (first + second).astype(BF16)
+                to = half * PAIR
+                first_ref[kind, g, :, to : to + PAIR] = first.astype(BF16)
         return 0
 
     lax.fori_loop(0, groups, group, 0)
-    hand_out(state_ref.at[0], outs[:groups])
-    hand_out(state_ref.at[1], outs[groups:])
+    hand_out(state_ref, outs[:groups])
+    hand_out(first_ref.at[0], outs[groups : 2 * groups])
+    hand_out(first_ref.at[1], outs[2 * groups :])
 
 
 def total_body(*refs):
@@ -206,7 +208,7 @@
 def prefixes(start, sums, firsts, at, held, out_ref):
     groups = len(sums)
     for k in range(groups):
-        first = firsts[k][:, at].astype(F32)
+        first = firsts[k][...].astype(F32)
         held[0, mine() ^ k] = first
         held[1, mine() ^ k] = sums[k][:, at].astype(F32) - first
     for f in range(2):
@@ -215,10 +217,19 @@
             out_ref[f, s] = start.astype(BF16)
 
 
+def partners(size):
+    assert size & (size - 1) == 0
+    return [1, 2, 4, 6][: max(size // 2, 1)] if size <= 8 else [1 << k for k in range(size.bit_length() - 1)]
+
+
 def before_of(gots, forward):
-    counts = lax.axis_index("tm") % 2 == (1 if forward else 0)
-    first = jnp.where(counts, gots[0][...].astype(F32), 0.0)
-    return first + sum(got[...].astype(F32) for got in gots[1:])
+    place = lax.axis_index("tm")
+    total = 0.0
+    for by, got in zip(partners(lax.axis_size("tm")), gots):
+        other = place ^ by
+        counts = other < place if forward else other > place
+        total = total + jnp.where(counts, got[...].astype(F32), 0.0)
+    return total
 
 
 def flow_body(groups, count, *refs):
@@ -227,10 +238,9 @@
     gots, refs = refs[:count], refs[count:]
     init_ref, po_ref, *refs = refs
     qbar_outs, refs = refs[:groups], refs[groups:]
-    q_ref, unit_ref, scale_ref, suffix_ref, sent_ref, prefix_ref, held, s_ref, carry, qbar_ref = refs
-    share = q_ref.shape[1]
+    unit_ref, scale_ref, suffix_ref, sent_ref, prefix_ref, held, s_ref, pbar_ref = refs
+    share = held.shape[1]
     frames = prefix_ref.shape[0]
-    take_in(q_parts, q_ref)
     for h in range(init_ref.shape[0]):
         held[:, h * HEAD : (h + 1) * HEAD] = init_ref[h]
     before = before_of(gots, True)[:, :share]
@@ -240,15 +250,14 @@
         square = jnp.where(same_head(), jnp.concatenate([packed, packed], 0), 0.0)
         held[:, at] = packed_of(square.T) + before[:, at]
     prefixes(held[...], sums, firsts, slice(0, share), s_ref, prefix_ref)
-    carry[...] = jnp.zeros_like(carry)
-
-    def frame(n, _):
-        f = frames - 1 - n
+
+    def frame(f, _):
         tokens = pl.ds(pl.multiple_of(f * SPAN, SPAN), SPAN)
-        for s in reversed(range(groups)):
+        for k in range(groups):
+            s = mine() ^ k
             for p in range(share // PAIR):
                 at = slice(p * PAIR, (p + 1) * PAIR)
-                query = q_ref[s, at, tokens]
+                query = q_parts[k][at, tokens]
                 prefix = spread(prefix_ref[f, s, :, at].astype(F32))
                 mixed = dot(prefix, query)
                 bars = []
@@ -263,35 +272,38 @@
                     unit_ref[f, s, rows, :] = unit.astype(BF16)
                     scale_ref[f, s, 2 * p + h : 2 * p + h + 1, :] = scale
                 mixed_bar = jnp.concatenate(bars, 0).astype(BF16)
-                carry[:, at] += packed_of(dot_nt(query, mixed_bar))
-                suffix_ref[s, f, :, at] = carry[:, at]
-                qbar_ref[s, at, tokens] = dot_tn(prefix, mixed_bar).astype(BF16)
+                pbar_ref[f, s, :, at] = packed_of(dot_nt(query, mixed_bar))
+                qbar_outs[k][at, tokens] = dot_tn(prefix, mixed_bar).astype(BF16)
         return 0
 
     lax.fori_loop(0, frames, frame, 0)
-    sent_ref[...] = carry[...].astype(BF16)
-    hand_out(qbar_ref, qbar_outs)
+    carry = jnp.zeros(held.shape, F32)
+    for f in reversed(range(frames)):
+        for s in reversed(range(groups)):
+            carry = carry + pbar_ref[f, s]
+            suffix_ref[s, f] = carry
+    sent_ref[...] = carry.astype(BF16)
 
 
 def tangent_body(groups, count, *refs):
-    qd_parts, refs = refs[:groups], refs[groups:]
+    qd_parts, q_parts, refs = refs[:groups], refs[groups : 2 * groups], refs[2 * groups :]
     sums, firsts, refs = refs[:groups], refs[groups : 2 * groups], refs[2 * groups :]
     gots, refs = refs[:count], refs[count:]
-    q_ref, prefix_ref, unit_ref, scale_ref, flow_ref, out_ref, qd_ref, s_ref, dots = refs
-    share = q_ref.shape[1]
+    prefix_ref, unit_ref, scale_ref, out_ref, s_ref, dots = refs
+    share = prefix_ref.shape[3]
     frames = prefix_ref.shape[0]
-    take_in(qd_parts, qd_ref)
     before = before_of(gots, True)[:, share:]
     prefixes(before, sums, firsts, slice(share, 2 * share), s_ref, dots)
 
     def frame(f, _):
         tokens = pl.ds(pl.multiple_of(f * SPAN, SPAN), SPAN)
-        for s in range(groups):
+        for k in range(groups):
+            s = mine() ^ k
             outs = []
             for p in range(share // PAIR):
                 at = slice(p * PAIR, (p + 1) * PAIR)
-                moved = dot(spread(prefix_ref[f, s, :, at].astype(F32)), qd_ref[s, at, tokens])
-                moved = moved + dot(spread(dots[f, s, :, at].astype(F32)), q_ref[s, at, tokens])
+                moved = dot(spread(prefix_ref[f, s, :, at].astype(F32)), qd_parts[k][at, tokens])
+                moved = moved + dot(spread(dots[f, s, :, at].astype(F32)), q_parts[k][at, tokens])
                 for h in range(2):
                     rows = slice(p * PAIR + h * HEAD, p * PAIR + (h + 1) * HEAD)
                     part = moved[h * HEAD : (h + 1) * HEAD]
@@ -300,10 +312,20 @@
                     along = jnp.sum(unit * part, 0, keepdims=True) * (1.0 / HEAD)
                     outs.append(part - unit * along)
             out_ref[f, s] = jnp.concatenate(outs, 0).T.astype(BF16)
-            flow_ref[f, s] = unit_ref[f, s].astype(F32).T.astype(BF16)
         return 0
 
     lax.fori_loop(0, frames, frame, 0)
+
+
+def unit_out_body(unit_ref, out_ref):
+    frames, groups = unit_ref.shape[:2]
+
+    def block(i, _):
+        f, s = i // groups, i % groups
+        out_ref[f, s] = unit_ref[f, s].astype(F32).T.astype(BF16)
+        return 0
+
+    lax.fori_loop(0, frames * groups, block, 0)
 
 
 def back_body(count, suffix_ref, *refs):
@@ -351,23 +373,14 @@
     out_ref[...] = out.T.astype(BF16)
 
 
-def scan_over(total, sent, axis, forward):
+def scan_over(total, sent, axis):
     size = lax.axis_size(axis)
-    assert size % 2 == 0
-    gots = [lax.ppermute(sent, axis, [(i, i ^ 1) for i in range(size)])]
-    total = total + gots[0].astype(F32)
-    shifts = [2 * k for k in range(1, size // 2)]
-    if len(shifts) > 3:
-        shifts = [2 << k for k in range(len(shifts).bit_length())]
-    paired = total.astype(BF16)
-    for by in shifts:
-        pairs = [(i, i + by) for i in range(size - by)]
-        if not forward:
-            pairs = [(j, i) for i, j in pairs]
-        gots.append(lax.ppermute(paired, axis, pairs))
-        if size > 8:
+    gots = []
+    for by in partners(size):
+        gots.append(lax.ppermute(sent, axis, [(i, i ^ by) for i in range(size)]))
+        if by == 1 or size > 8:
             total = total + gots[-1].astype(F32)
-            paired = total.astype(BF16)
+            sent = total.astype(BF16)
     return gots
 
 
@@ -426,12 +439,17 @@
     state_part = struct((HEAD, 2 * share), BF16)
     latent, both, *states = call(
         state_body,
-        [struct((tokens, D), BF16), struct(two_tall, BF16)] + [state_part] * (2 * groups),
+        [struct((tokens, D), BF16), struct(two_tall, BF16)] + [state_part] * groups
+        + [struct((HEAD, share), BF16)] * (2 * groups),
         (near, far, embed_weight, dots, k_weight, v_weight),
-        scratch=[pltpu.VMEM((2, groups) + state_part.shape, BF16)],
+        scratch=[
+            pltpu.VMEM((groups,) + state_part.shape, BF16),
+            pltpu.VMEM((2, groups, HEAD, share), BF16),
+        ],
         flops=4 * tokens * D * D, moved=2 * weight_bytes + 14 * tokens * D,
     )
-    sums, firsts = exchange(states[:groups]), states[groups:]
+    sums, firsts = exchange(states[:groups]), states[groups : 2 * groups]
+    first_dots = states[2 * groups :]
 
     query = call(
         query_body, [part] * groups, (latent, q_near), scratch=[held],
@@ -444,7 +462,8 @@
     )
     query = exchange(query)
     firsts = exchange(firsts)
-    gots = scan_over(total, sent, "tm", True)
+    first_dots = exchange(first_dots)
+    gots = scan_over(total, sent, "tm")
 
     shape_fs = (frames, groups, SPAN, share)
     flip_fs = (frames, groups, share, SPAN)
@@ -455,11 +474,10 @@
 
     prefix_shape = (frames, groups, HEAD, share)
     state_held = pltpu.VMEM(prefix_shape, F32)
-    *query_bar, query, unit, scale, suffix, bar_sent, prefix = call(
+    *query_bar, unit, scale, suffix, bar_sent, prefix = call(
         functools.partial(flow_body, groups, len(gots)),
         [part] * groups
         + [
-            struct(grouped, BF16),
             struct(flip_fs, BF16),
             struct((frames, groups, heads, SPAN), F32),
             struct((groups, frames, HEAD, share), F32),
@@ -467,25 +485,26 @@
             struct(prefix_shape, BF16),
         ],
         (*query, *sums, *firsts, *gots, initial_state, cotangent),
-        scratch=[pltpu.VMEM((HEAD, share), F32), state_held, pltpu.VMEM((HEAD, share), F32), held],
+        scratch=[pltpu.VMEM((HEAD, share), F32), state_held, state_held],
         flops=12 * tokens * D * PAIR, moved=10 * tokens * D,
     )
     query_bar = exchange(query_bar)
-    bar_gots = scan_over(suffix[0, 0], bar_sent, "tm", False)
-
-    flow, tangent = call(
-        functools.partial(tangent_body, groups, len(gots)), [struct(shape_fs, BF16)] * 2,
-        (*query_dot, *sums, *firsts, *gots, query, prefix, unit, scale),
-        scratch=[held, state_held, pltpu.VMEM(prefix_shape, BF16)],
+    bar_gots = scan_over(suffix[0, 0], bar_sent, "tm")
+
+    tangent = call(
+        functools.partial(tangent_body, groups, len(gots)), [struct(shape_fs, BF16)],
+        (*query_dot, *query, *sums, *first_dots, *gots, prefix, unit, scale),
+        scratch=[state_held, pltpu.VMEM(prefix_shape, BF16)],
         flops=12 * tokens * D * PAIR, moved=10 * tokens * D,
-    )
+    )[0]
+    flow = call(unit_out_body, [struct(shape_fs, BF16)], (unit,), moved=4 * tokens * D)[0]
 
     *state_back, after = call(
         functools.partial(back_body, len(bar_gots)),
         [struct((frames, HEAD, share), BF16)] * groups + [struct((HEAD, share), F32)],
         (suffix, *bar_gots), moved=10 * frames * groups * HEAD * share,
     )
-    state_back, flow, tangent = lax.optimization_barrier((state_back, flow, tangent))
+    state_back, tangent = lax.optimization_barrier((state_back, tangent))
     state_back = exchange(state_back)
     state_bar = call(
         cotangent_body, [struct((frames * groups, heads, HEAD, HEAD), F32)],

time: 123 us -> 120 us (0.976)
  starting transfers between devices: 45.3 us -> 38.4 us
  waiting for transfers between devices: 32.2 us -> 34.7 us
  Pallas kernels: 43.6 us -> 45.2 us
    ppermute x8, starting transfers between devices: 22.4 us -> 14.4 us  [scan_over(): gots.append(lax.ppermute(sent, axis, [(i, i ^ by) for i in range(size)]))]
    pallas_call x14 -> x15, Pallas kernels: 43.6 us -> 45.2 us  [call(): pl.pallas_call(body, in_specs=[anywhere] * far + [vmem] * (len(args) - fa...]
    ppermute x18 -> x21, waiting for transfers between devices: 25.6 us -> 27 us  [exchange(): lax.ppermute(parts[k], 'space', [(i, i ^ k) for i in range(size)])]
    ppermute x18 -> x21, starting transfers between devices: 14.8 us -> 15.9 us  [exchange(): lax.ppermute(parts[k], 'space', [(i, i ^ k) for i in range(size)])]
  transfers between devices with their start and end apart: 29 -> 32, of which waited for: 11 -> 10; matrix products, arithmetic and copies ran while one was open for 0% -> 0% of each run, Pallas kernels for 23% -> 25%
where the time goes in v2:
time: 120 us
  Pallas kernels  45.2 us (38%)
  starting transfers between devices  38.4 us (32%)
  waiting for transfers between devices  34.7 us (29%)
    pallas_call x15, Pallas kernels, call(): pl.pallas_call(body, in_specs=[anywhere] * far + [vmem] * (len(args) - fa...  45.2 us
    ppermute x21, waiting for transfers between devices, exchange(): lax.ppermute(parts[k], 'space', [(i, i ^ k) for i in range(size)])  27 us
    ppermute x21, starting transfers between devices, exchange(): lax.ppermute(parts[k], 'space', [(i, i ^ k) for i in range(size)])  15.9 us
    ppermute x8, starting transfers between devices, scan_over(): gots.append(lax.ppermute(sent, axis, [(i, i ^ by) for i in range(size)]))  14.4 us
    ppermute x8, waiting for transfers between devices, scan_over(): gots.append(lax.ppermute(sent, axis, [(i, i ^ by) for i in range(size)]))  6.47 us
    ppermute x1, starting transfers between devices, on_device(): far = lax.ppermute(far, 'tm', [(t, t + 1) for t in range(tms - 1)])  4.42 us
  transfers between devices with their start and end apart: 32, of which 10 were waited for; matrix products, arithmetic and copies ran while one was open for 0% of the time, Pallas kernels for 25%

profile of v2, /device:TPU:0, one launch (start us, length us, event | category | flops | bytes accessed | tf_op | source)
XLA Modules:
  0.0 120.1 jit_solution(8863829285375933357)
XLA Ops:
  0.6 0.8 fusion.1
  1.5 2.4 %collective-permute-start = (bf16[2,1,32,384]{3,2,1,0:T(8,128)(2,1)S(1)}, bf16[2,1,32,384]{3,2,1,0:T(8,128)(2,1)S(1)}, u32[]{:S(2)}, u32[]{:S(2)}) collective-permute-start(bf16[2,1,32,384]{3,2,1,0:T(8,128)(2,1)S(1)} %get-tuple-element.101), channel_id=1, source_target_pairs={{0,1},{1,2},{2,3},{4,5},{5,6},{6,7},{8,9},{9,10},{10,11},{12,13},{... | collective-permute-start | bytes 147464 | tf_op jit(solution)/shard_map/ppermute | solution.py:400
  3.9 1.3 %collective-permute-start.1 = (bf16[2,1,32,384]{3,2,1,0:T(8,128)(2,1)S(1)}, bf16[2,1,32,384]{3,2,1,0:T(8,128)(2,1)S(1)}, u32[]{:S(2)}, u32[]{:S(2)}) collective-permute-start(bf16[2,1,32,384]{3,2,1,0:T(8,128)(2,1)S(1)} %get-tuple-element.100), channel_id=1, source_target_pairs={{1,0},{2,1},{3,2},{5,4},{6,5},{7,6},{9,8},{10,9},{11,10},{13,12},{... | collective-permute-start | bytes 147464 | tf_op jit(solution)/shard_map/ppermute | solution.py:401
  5.2 5.1 %shard_map.120 = (bf16[288,512]{1,0:T(8,128)(2,1)S(1)}, bf16[288,512]{1,0:T(8,128)(2,1)S(1)}, bf16[288,512]{1,0:T(8,128)(2,1)S(1)}, bf16[288,512]{1,0:T(8,128)(2...) custom-call(s32[512,1152]{1,0:T(8,128)} %bitcast.13, ...), custom_call_target="tpu_custom_call" | custom-call | flops 1358954496 | bytes 7372800 | tf_op jit(solution)/shard_map/pallas_call | solution.py:25
  10.3 3.0 %shard_map.123 = bf16[512,384]{1,0:T(8,128)(2,1)S(1)} custom-call(bf16[2,8,32,384]{3,2,1,0:T(8,128)(2,1)S(1)} %copy-done.3, bf16[2,1,32,384]{3,2,1,0:T(8,128)(2,1)S(1)} %collective-permute-done.up_ref, bf16[2,1,32,384]{3,2,1,0:T(8,128)(2,1)S(1)} %collective-permute-done.1.down_ref, bf16[2,3456,384]{2,1,0:T(8,128)(2,1)S(1)} %get-tuple-element.54.mid_ref.main_ref, ...), custom_call_target="tpu_custom_call" | custom-call | flops 2038431744 | bytes 5160960 | tf_op jit(solution)/shard_map/pallas_call | solution.py:25
  13.3 4.4 %collective-permute-start.2 = (bf16[512,384]{1,0:T(8,128)(2,1)S(1)}, bf16[512,384]{1,0:T(8,128)(2,1)S(1)}, u32[]{:S(2)}, u32[]{:S(2)}) collective-permute-start(bf16[512,384]{1,0:T(8,128)(2,1)S(1)} %shard_map.123), channel_id=1, source_target_pairs={{0,4},{4,8},{8,12},{12,16},{16,20},{20,24},{24,28},{1,5},{5,9},{9,... | collective-permute-start | bytes 1179656 | tf_op jit(solution)/shard_map/ppermute | solution.py:430
  17.7 3.6 %shard_map.121 = (bf16[2,1152,512]{2,1,0:T(8,128)(2,1)S(1)}, bf16[3456,384]{1,0:T(8,128)(2,1)S(1)}) custom-call(bf16[3,3456,384]{2,1,0:T(8,128)(2,1)} %bitcast.12, bf16[512,1152]{1,0:T(8,128)(2,1)S(1)} %get-tuple-element.52.x_ref, bf16[1152,1152]{1,0:T(8,128)(2,1)S(1)} %copy-done, bf16[1152,1152]{1,0:T(8,128)(2,1)S(1)} %copy-done.1), custom_call_target="tpu_custom_call" | custom-call | flops 2717908992 | bytes 8847360 | tf_op jit(solution)/shard_map/pallas_call | solution.py:25
  21.4 3.0 %shard_map.122.near_ref = f32[512,384]{1,0:T(8,128)S(1)} custom-call(bf16[2,8,32,384]{3,2,1,0:T(8,128)(2,1)S(1)} %copy-done.3, bf16[2,1,32,384]{3,2,1,0:T(8,128)(2,1)S(1)} %collective-permute-done.up_ref, bf16[2,1,32,384]{3,2,1,0:T(8,128)(2,1)S(1)} %collective-permute-done.1.down_ref, bf16[3456,384]{1,0:T(8,128)(2,1)S(1)} %get-tuple-element.53.main_ref, ...), custom_call_target="tpu_custom_call" | custom-call | flops 2038431744 | bytes 5160960 | tf_op jit(solution)/shard_map/pallas_call | solution.py:25
  24.4 1.2 collective-permute-done.2.far_ref
  25.6 6.4 %shard_map.124 = (bf16[512,1152]{1,0:T(8,128)(2,1)S(1)}, bf16[2,1152,512]{2,1,0:T(8,128)(2,1)S(1)}, bf16[72,576]{1,0:T(8,128)(2,1)S(1)}, bf16[72,576]{1,0:T(8,12...) custom-call(f32[512,384]{1,0:T(8,128)S(1)} %shard_map.122.near_ref, ...), custom_call_target="tpu_custom_call" | custom-call | flops 2717908992 | bytes 13565952 | tf_op jit(solution)/shard_map/pallas_call | solution.py:25
  32.0 1.6 %collective-permute-start.6 = (bf16[72,576]{1,0:T(8,128)(2,1)S(1)}, bf16[72,576]{1,0:T(8,128)(2,1)S(1)}, u32[]{:S(2)}, u32[]{:S(2)}) collective-permute-start(bf16[72,576]{1,0:T(8,128)(2,1)S(1)} %get-tuple-element.63), channel_id=1, source_target_pairs={{0,1},{1,0},{2,3},{3,2},{4,5},{5,4},{6,7},{7,6},{8,9},{9,8},{10,11... | collective-permute-start | bytes 248840 | tf_op jit(solution)/shard_map/ppermute | solution.py:90
  33.6 1.8 %collective-permute-start.7 = (bf16[72,576]{1,0:T(8,128)(2,1)S(1)}, bf16[72,576]{1,0:T(8,128)(2,1)S(1)}, u32[]{:S(2)}, u32[]{:S(2)}) collective-permute-start(bf16[72,576]{1,0:T(8,128)(2,1)S(1)} %get-tuple-element.64), channel_id=1, source_target_pairs={{0,2},{1,3},{2,0},{3,1},{4,6},{5,7},{6,4},{7,5},{8,10},{9,11},{10,... | collective-permute-start | bytes 248840 | tf_op jit(solution)/shard_map/ppermute | solution.py:90
  35.5 3.5 %collective-permute-done.7.refs_2_.refs_6_.refs_10_ = bf16[72,576]{1,0:T(8,128)(2,1)S(1)} collective-permute-done((bf16[72,576]{1,0:T(8,128)(2,1)S(1)}, bf16[72,576]{1,0:T(8,128)(2,1)S(1)}, u32[]{:S(2)}, u32[]{:S(2)}) %collective-permute-start.7) | collective-permute-done | bytes 82976 | tf_op jit(solution)/shard_map/ppermute | solution.py:90
  39.0 1.4 %collective-permute-done.8.refs_3_.refs_7_.refs_11_ = bf16[72,576]{1,0:T(8,128)(2,1)S(1)} collective-permute-done((bf16[72,576]{1,0:T(8,128)(2,1)S(1)}, bf16[72,576]{1,0:T(8,128)(2,1)S(1)}, u32[]{:S(2)}, u32[]{:S(2)}) %collective-permute-start.8) | collective-permute-done | bytes 82976 | tf_op jit(solution)/shard_map/ppermute | solution.py:90
  40.5 2.6 %collective-permute-start.12 = (bf16[72,576]{1,0:T(8,128)(2,1)S(1)}, bf16[72,576]{1,0:T(8,128)(2,1)S(1)}, u32[]{:S(2)}, u32[]{:S(2)}) collective-permute-start(bf16[72,576]{1,0:T(8,128)(2,1)S(1)} %get-tuple-element.70.tie_ref), channel_id=1, source_target_pairs={{0,4},{4,0},{8,12},{12,8},{16,20},{20,16},{24,28},{28,24},{1,5},{5... | collective-permute-start | bytes 248840 | tf_op jit(solution)/shard_map/ppermute | solution.py:380
  43.0 2.1 %shard_map.125 = (bf16[288,512]{1,0:T(8,128)(2,1)S(1)}, bf16[288,512]{1,0:T(8,128)(2,1)S(1)}, bf16[288,512]{1,0:T(8,128)(2,1)S(1)}, bf16[288,512]{1,0:T(8,128)(2,1)S(1)}) custom-call(bf16[512,1152]{1,0:T(8,128)(2,1)S(1)} %get-tuple-element.56.x_ref, bf16[1152,1152]{1,0:T(8,128)(2,1)S(1)} %get-tuple-element.57.w_ref), custom_call_target="tpu_custom_call" | custom-call | flops 1358954496 | bytes 5013504 | tf_op jit(solution)/shard_map/pallas_call | solution.py:25
  45.2 1.5 %collective-permute-start.10 = (bf16[72,288]{1,0:T(8,128)(2,1)S(1)}, bf16[72,288]{1,0:T(8,128)(2,1)S(1)}, u32[]{:S(2)}, u32[]{:S(2)}) collective-permute-start(bf16[72,288]{1,0:T(8,128)(2,1)S(1)} %get-tuple-element.68), channel_id=1, source_target_pairs={{0,2},{1,3},{2,0},{3,1},{4,6},{5,7},{6,4},{7,5},{8,10},{9,11},{10,... | collective-permute-start | bytes 124424 | tf_op jit(solution)/shard_map/ppermute | solution.py:90
  46.7 0.3 collective-permute-start.11
  47.1 1.7 %collective-permute-start.13 = (bf16[72,576]{1,0:T(8,128)(2,1)S(1)}, bf16[72,576]{1,0:T(8,128)(2,1)S(1)}, u32[]{:S(2)}, u32[]{:S(2)}) collective-permute-start(bf16[72,576]{1,0:T(8,128)(2,1)S(1)} %add_convert_fusion), channel_id=1, source_target_pairs={{0,8},{4,12},{8,0},{12,4},{16,24},{20,28},{24,16},{28,20},{1,9},{5... | collective-permute-start | bytes 248840 | tf_op jit(solution)/shard_map/ppermute | solution.py:380
  48.8 1.7 %collective-permute-start.4 = (bf16[288,512]{1,0:T(8,128)(2,1)S(1)}, bf16[288,512]{1,0:T(8,128)(2,1)S(1)}, u32[]{:S(2)}, u32[]{:S(2)}) collective-permute-start(bf16[288,512]{1,0:T(8,128)(2,1)S(1)} %get-tuple-element.60), channel_id=1, source_target_pairs={{0,2},{1,3},{2,0},{3,1},{4,6},{5,7},{6,4},{7,5},{8,10},{9,11},{10,... | collective-permute-start | bytes 884744 | tf_op jit(solution)/shard_map/ppermute | solution.py:90
  50.6 1.0 collective-permute-start.9
  51.6 0.9 collective-permute-done.9.refs_9_
  52.5 2.6 %collective-permute-start.14 = (bf16[72,576]{1,0:T(8,128)(2,1)S(1)}, bf16[72,576]{1,0:T(8,128)(2,1)S(1)}, u32[]{:S(2)}, u32[]{:S(2)}) collective-permute-start(bf16[72,576]{1,0:T(8,128)(2,1)S(1)} %add_convert_fusion), channel_id=1, source_target_pairs={{0,16},{4,20},{8,24},{12,28},{16,0},{20,4},{24,8},{28,12},{1,17},{... | collective-permute-start | bytes 248840 | tf_op jit(solution)/shard_map/ppermute | solution.py:380
  55.1 1.3 %collective-permute-start.15 = (bf16[72,576]{1,0:T(8,128)(2,1)S(1)}, bf16[72,576]{1,0:T(8,128)(2,1)S(1)}, u32[]{:S(2)}, u32[]{:S(2)}) collective-permute-start(bf16[72,576]{1,0:T(8,128)(2,1)S(1)} %add_convert_fusion), channel_id=1, source_target_pairs={{0,24},{4,28},{8,16},{12,20},{16,8},{20,12},{24,0},{28,4},{1,25},{... | collective-permute-start | bytes 248840 | tf_op jit(solution)/shard_map/ppermute | solution.py:380
  56.4 6.4 %collective-permute-done.14.refs_14_.refs_18_ = bf16[72,576]{1,0:T(8,128)(2,1)S(1)} collective-permute-done((bf16[72,576]{1,0:T(8,128)(2,1)S(1)}, bf16[72,576]{1,0:T(8,128)(2,1)S(1)}, u32[]{:S(2)}, u32[]{:S(2)}) %collective-permute-start.14) | collective-permute-done | bytes 82976 | tf_op jit(solution)/shard_map/ppermute | solution.py:380
  62.9 1.1 collective-permute-start.21
  63.9 0.8 collective-permute-start.22
  64.7 1.1 shard_map.127.refs_17_
  65.9 5.4 %shard_map.128 = (bf16[288,512]{1,0:T(8,128)(2,1)S(1)}, bf16[288,512]{1,0:T(8,128)(2,1)S(1)}, bf16[288,512]{1,0:T(8,128)(2,1)S(1)}, bf16[288,512]{1,0:T(8,128)(2...) custom-call(bf16[288,512]{1,0:T(8,128)(2,1)S(1)} %get-tuple-element., ...), custom_call_target="tpu_custom_call" | custom-call | flops 1019215872 | bytes 5898240 | tf_op jit(solution)/shard_map/pallas_call | solution.py:25
  71.3 1.2 collective-permute-start.16
  72.5 0.9 collective-permute-start.24
  73.6 4.5 %collective-permute-done.22.refs_3_ = bf16[288,512]{1,0:T(8,128)(2,1)S(1)} collective-permute-done((bf16[288,512]{1,0:T(8,128)(2,1)S(1)}, bf16[288,512]{1,0:T(8,128)(2,1)S(1)}, u32[]{:S(2)}, u32[]{:S(2)}) %collective-permute-start.22) | collective-permute-done | bytes 294944 | tf_op jit(solution)/shard_map/ppermute | solution.py:90
  78.1 1.1 collective-permute-start.30
  79.2 1.0 collective-permute-start.31
  80.3 0.8 collective-permute-start.25
  81.0 1.1 collective-permute-start.17
  82.2 12.9 %collective-permute-done.25.refs_15_ = bf16[72,288]{1,0:T(8,128)(2,1)S(1)} collective-permute-done((bf16[72,288]{1,0:T(8,128)(2,1)S(1)}, bf16[72,288]{1,0:T(8,128)(2,1)S(1)}, u32[]{:S(2)}, u32[]{:S(2)}) %collective-permute-start.25) | collective-permute-done | bytes 41504 | tf_op jit(solution)/shard_map/ppermute | solution.py:90
  95.1 3.5 %collective-permute-start.18 = (bf16[72,288]{1,0:T(8,128)(2,1)S(1)}, bf16[72,288]{1,0:T(8,128)(2,1)S(1)}, u32[]{:S(2)}, u32[]{:S(2)}) collective-permute-start(bf16[72,288]{1,0:T(8,128)(2,1)S(1)} %fusion), channel_id=1, source_target_pairs={{0,16},{4,20},{8,24},{12,28},{16,0},{20,4},{24,8},{28,12},{1,17},{... | collective-permute-start | bytes 124424 | tf_op jit(solution)/shard_map/ppermute | solution.py:380
  98.6 0.4 collective-permute-start.19
  99.0 3.9 %shard_map.131 = bf16[2,4,256,288]{3,2,1,0:T(8,128)(2,1)} custom-call(bf16[288,512]{1,0:T(8,128)(2,1)S(1)} %get-tuple-element.79.refs_0_, bf16[288,512]{1,0:T(8,128)(2,1)S(1)} %collective-permute-done.20.refs_1_, bf16[288,512]{1,0:T(8,128)(2,1)S(1)} %collective-permute-done.21.refs_2_, bf16[288,512]{1,0:T(8,128)(2,1)S(1)} %collective-permute-done.22.refs_3_, ...), custom_call_target="tpu_custom_call" | custom-call | flops 1019215872 | bytes 5898240 | tf_op jit(solution)/shard_map/pallas_call | solution.py:25
  102.9 2.3 %shard_map.129 = bf16[2,4,256,288]{3,2,1,0:T(8,128)(2,1)} custom-call(bf16[2,4,288,256]{3,2,1,0:T(8,128)(2,1)S(1)} %get-tuple-element.72.unit_ref.refs_21_), custom_call_target="tpu_custom_call" | custom-call | bytes 2359296 | tf_op jit(solution)/shard_map/pallas_call | solution.py:25
  105.3 1.5 %shard_map.134 = f32[8,4,72,72]{3,2,1,0:T(8,128)} custom-call(f32[4,2,72,288]{3,2,1,0:T(8,128)S(1)} %get-tuple-element.73.suffix_ref, f32[72,288]{1,0:T(8,128)S(1)} %get-tuple-element.99.after_ref), custom_call_target="tpu_custom_call" | custom-call | bytes 1658880 | tf_op jit(solution)/shard_map/pallas_call | solution.py:25
  106.7 0.7 collective-permute-start.27
  107.5 1.1 collective-permute-start.28
  108.6 1.8 %shard_map.132.refs_5_ = f32[1152,512]{1,0:T(8,128)S(1)} custom-call(bf16[1152,1152]{1,0:T(8,128)(2,1)S(1)} %get-tuple-element.57.w_ref, bf16[288,512]{1,0:T(8,128)(2,1)S(1)} %get-tuple-element.95.refs_0_, bf16[288,512]{1,0:T(8,128)(2,1)S(1)} %collective-permute-done.29.refs_1_, bf16[288,512]{1,0:T(8,128)(2,1)S(1)} %collective-permute-done.30.refs_2_, ...), custom_call_target="tpu_custom_call" | custom-call | flops 1358954496 | bytes 6193152 | tf_op jit(solution)/shard_map/pallas_call | solution.py:25
  110.4 2.3 %collective-permute-done.27.refs_2_ = bf16[2,72,288]{2,1,0:T(8,128)(2,1)S(1)} collective-permute-done((bf16[2,72,288]{2,1,0:T(8,128)(2,1)S(1)}, bf16[2,72,288]{2,1,0:T(8,128)(2,1)S(1)}, u32[]{:S(2)}, u32[]{:S(2)}) %collective-permute-start.27) | collective-permute-done | bytes 82976 | tf_op jit(solution)/shard_map/ppermute | solution.py:90
  112.7 1.4 %collective-permute-done.28.refs_3_ = bf16[2,72,288]{2,1,0:T(8,128)(2,1)S(1)} collective-permute-done((bf16[2,72,288]{2,1,0:T(8,128)(2,1)S(1)}, bf16[2,72,288]{2,1,0:T(8,128)(2,1)S(1)}, u32[]{:S(2)}, u32[]{:S(2)}) %collective-permute-start.28) | collective-permute-done | bytes 82976 | tf_op jit(solution)/shard_map/ppermute | solution.py:90
  114.1 6.0 %shard_map.133 = bf16[512,1152]{1,0:T(8,128)(2,1)} custom-call(bf16[2,72,288]{2,1,0:T(8,128)(2,1)S(1)} %get-tuple-element.90.refs_0_, bf16[2,72,288]{2,1,0:T(8,128)(2,1)S(1)} %collective-permute-done.26.refs_1_, bf16[2,72,288]{2,1,0:T(8,128)(2,1)S(1)} %collective-permute-done.27.refs_2_, bf16[2,72,288]{2,1,0:T(8,128)(2,1)S(1)} %collective-permute-done.28.refs_3_, ...), custom_call_target="tpu_custom_call" | custom-call | flops 2717908992 | bytes 11206656 | tf_op jit(solution)/shard_map/pallas_call | solution.py:25
  (46 shorter events, 0.7 us)
Async XLA Ops:
  1.5 8.8 %collective-permute-start = (bf16[2,1,32,384]{3,2,1,0:T(8,128)(2,1)S(1)}, bf16[2,1,32,384]{3,2,1,0:T(8,128)(2,1)S(1)}, u32[]{:S(2)}, u32[]{:S(2)}) collective-permute-start(bf16[2,1,32,384]{3,2,1,0:T(8,128)(2,1)S(1)} %get-tuple-element.101), channel_id=1, source_target_pairs={{0,1},{1,2},{2,3},{4,5},{5,6},{6,7},{8,9},{9,10},{10,11},{12,13},{... | collective-permute-start | bytes 147464 | tf_op jit(solution)/shard_map/ppermute | solution.py:400
  3.9 6.4 %collective-permute-start.1 = (bf16[2,1,32,384]{3,2,1,0:T(8,128)(2,1)S(1)}, bf16[2,1,32,384]{3,2,1,0:T(8,128)(2,1)S(1)}, u32[]{:S(2)}, u32[]{:S(2)}) collective-permute-start(bf16[2,1,32,384]{3,2,1,0:T(8,128)(2,1)S(1)} %get-tuple-element.100), channel_id=1, source_target_pairs={{1,0},{2,1},{3,2},{5,4},{6,5},{7,6},{9,8},{10,9},{11,10},{13,12},{... | collective-permute-start | bytes 147464 | tf_op jit(solution)/shard_map/ppermute | solution.py:401
  5.2 5.1 %copy-start.3 = (bf16[2,8,32,384]{3,2,1,0:T(8,128)(2,1)S(1)}, bf16[2,8,32,384]{3,2,1,0:T(8,128)(2,1)}, u32[]{:S(2)}) copy-start(bf16[2,8,32,384]{3,2,1,0:T(8,128)(2,1)} %own_ref.3) | copy-start | bytes 1179652
  10.3 7.4 %copy-start = (bf16[1152,1152]{1,0:T(8,128)(2,1)S(1)}, bf16[1152,1152]{1,0:T(8,128)(2,1)}, u32[]{:S(2)}) copy-start(bf16[1152,1152]{1,0:T(8,128)(2,1)} %refs_6_.1) | copy-start | bytes 7962628
  10.3 7.4 %copy-start.1 = (bf16[1152,1152]{1,0:T(8,128)(2,1)S(1)}, bf16[1152,1152]{1,0:T(8,128)(2,1)}, u32[]{:S(2)}) copy-start(bf16[1152,1152]{1,0:T(8,128)(2,1)} %refs_7_.1) | copy-start | bytes 7962628
  13.3 12.2 %collective-permute-start.2 = (bf16[512,384]{1,0:T(8,128)(2,1)S(1)}, bf16[512,384]{1,0:T(8,128)(2,1)S(1)}, u32[]{:S(2)}, u32[]{:S(2)}) collective-permute-start(bf16[512,384]{1,0:T(8,128)(2,1)S(1)} %shard_map.123), channel_id=1, source_target_pairs={{0,4},{4,8},{8,12},{12,16},{16,20},{20,24},{24,28},{1,5},{5,9},{9,... | collective-permute-start | bytes 1179656 | tf_op jit(solution)/shard_map/ppermute | solution.py:430
  21.4 4.2 %copy-start.4 = (bf16[384,1152]{1,0:T(8,128)(2,1)S(1)}, bf16[384,1152]{1,0:T(8,128)(2,1)}, u32[]{:S(2)}) copy-start(bf16[384,1152]{1,0:T(8,128)(2,1)} %embed_ref.1) | copy-start | bytes 2654212
  32.0 3.5 %collective-permute-start.6 = (bf16[72,576]{1,0:T(8,128)(2,1)S(1)}, bf16[72,576]{1,0:T(8,128)(2,1)S(1)}, u32[]{:S(2)}, u32[]{:S(2)}) collective-permute-start(bf16[72,576]{1,0:T(8,128)(2,1)S(1)} %get-tuple-element.63), channel_id=1, source_target_pairs={{0,1},{1,0},{2,3},{3,2},{4,5},{5,4},{6,7},{7,6},{8,9},{9,8},{10,11... | collective-permute-start | bytes 248840 | tf_op jit(solution)/shard_map/ppermute | solution.py:90
  33.6 5.3 %collective-permute-start.7 = (bf16[72,576]{1,0:T(8,128)(2,1)S(1)}, bf16[72,576]{1,0:T(8,128)(2,1)S(1)}, u32[]{:S(2)}, u32[]{:S(2)}) collective-permute-start(bf16[72,576]{1,0:T(8,128)(2,1)S(1)} %get-tuple-element.64), channel_id=1, source_target_pairs={{0,2},{1,3},{2,0},{3,1},{4,6},{5,7},{6,4},{7,5},{8,10},{9,11},{10,... | collective-permute-start | bytes 248840 | tf_op jit(solution)/shard_map/ppermute | solution.py:90
  35.4 5.0 %collective-permute-start.8 = (bf16[72,576]{1,0:T(8,128)(2,1)S(1)}, bf16[72,576]{1,0:T(8,128)(2,1)S(1)}, u32[]{:S(2)}, u32[]{:S(2)}) collective-permute-start(bf16[72,576]{1,0:T(8,128)(2,1)S(1)} %get-tuple-element.65), channel_id=1, source_target_pairs={{0,3},{1,2},{2,1},{3,0},{4,7},{5,6},{6,5},{7,4},{8,11},{9,10},{10,... | collective-permute-start | bytes 248840 | tf_op jit(solution)/shard_map/ppermute | solution.py:90
  40.5 6.6 %collective-permute-start.12 = (bf16[72,576]{1,0:T(8,128)(2,1)S(1)}, bf16[72,576]{1,0:T(8,128)(2,1)S(1)}, u32[]{:S(2)}, u32[]{:S(2)}) collective-permute-start(bf16[72,576]{1,0:T(8,128)(2,1)S(1)} %get-tuple-element.70.tie_ref), channel_id=1, source_target_pairs={{0,4},{4,0},{8,12},{12,8},{16,20},{20,16},{24,28},{28,24},{1,5},{5... | collective-permute-start | bytes 248840 | tf_op jit(solution)/shard_map/ppermute | solution.py:380
  43.0 21.7 %copy-start.2 = (s32[2,32,32,288]{3,2,1,0:T(8,128)S(1)}, s32[2,32,32,288]{3,2,1,0:T(8,128)}, u32[]{:S(2)}) copy-start(s32[2,32,32,288]{3,2,1,0:T(8,128)} %param.17) | copy-start | bytes 7077892
  45.1 18.8 %collective-permute-start.3 = (bf16[288,512]{1,0:T(8,128)(2,1)S(1)}, bf16[288,512]{1,0:T(8,128)(2,1)S(1)}, u32[]{:S(2)}, u32[]{:S(2)}) collective-permute-start(bf16[288,512]{1,0:T(8,128)(2,1)S(1)} %get-tuple-element.59), channel_id=1, source_target_pairs={{0,1},{1,0},{2,3},{3,2},{4,5},{5,4},{6,7},{7,6},{8,9},{9,8},{10,11... | collective-permute-start | bytes 884744 | tf_op jit(solution)/shard_map/ppermute | solution.py:90
  45.2 5.3 %collective-permute-start.10 = (bf16[72,288]{1,0:T(8,128)(2,1)S(1)}, bf16[72,288]{1,0:T(8,128)(2,1)S(1)}, u32[]{:S(2)}, u32[]{:S(2)}) collective-permute-start(bf16[72,288]{1,0:T(8,128)(2,1)S(1)} %get-tuple-element.68), channel_id=1, source_target_pairs={{0,2},{1,3},{2,0},{3,1},{4,6},{5,7},{6,4},{7,5},{8,10},{9,11},{10,... | collective-permute-start | bytes 124424 | tf_op jit(solution)/shard_map/ppermute | solution.py:90
  46.7 3.9 %collective-permute-start.11 = (bf16[72,288]{1,0:T(8,128)(2,1)S(1)}, bf16[72,288]{1,0:T(8,128)(2,1)S(1)}, u32[]{:S(2)}, u32[]{:S(2)}) collective-permute-start(bf16[72,288]{1,0:T(8,128)(2,1)S(1)} %get-tuple-element.69), channel_id=1, source_target_pairs={{0,3},{1,2},{2,1},{3,0},{4,7},{5,6},{6,5},{7,4},{8,11},{9,10},{10,... | collective-permute-start | bytes 124424 | tf_op jit(solution)/shard_map/ppermute | solution.py:90
  47.0 18.8 %copy-start.5 = (f32[4,72,72]{2,1,0:T(8,128)S(1)}, f32[4,72,72]{2,1,0:T(8,128)}, u32[]{:S(2)}) copy-start(f32[4,72,72]{2,1,0:T(8,128)} %refs_16_.1) | copy-start | bytes 248836
  47.1 8.0 %collective-permute-start.13 = (bf16[72,576]{1,0:T(8,128)(2,1)S(1)}, bf16[72,576]{1,0:T(8,128)(2,1)S(1)}, u32[]{:S(2)}, u32[]{:S(2)}) collective-permute-start(bf16[72,576]{1,0:T(8,128)(2,1)S(1)} %add_convert_fusion), channel_id=1, source_target_pairs={{0,8},{4,12},{8,0},{12,4},{16,24},{20,28},{24,16},{28,20},{1,9},{5... | collective-permute-start | bytes 248840 | tf_op jit(solution)/shard_map/ppermute | solution.py:380
  48.8 17.1 %collective-permute-start.4 = (bf16[288,512]{1,0:T(8,128)(2,1)S(1)}, bf16[288,512]{1,0:T(8,128)(2,1)S(1)}, u32[]{:S(2)}, u32[]{:S(2)}) collective-permute-start(bf16[288,512]{1,0:T(8,128)(2,1)S(1)} %get-tuple-element.60), channel_id=1, source_target_pairs={{0,2},{1,3},{2,0},{3,1},{4,6},{5,7},{6,4},{7,5},{8,10},{9,11},{10,... | collective-permute-start | bytes 884744 | tf_op jit(solution)/shard_map/ppermute | solution.py:90
  50.5 15.4 %collective-permute-start.5 = (bf16[288,512]{1,0:T(8,128)(2,1)S(1)}, bf16[288,512]{1,0:T(8,128)(2,1)S(1)}, u32[]{:S(2)}, u32[]{:S(2)}) collective-permute-start(bf16[288,512]{1,0:T(8,128)(2,1)S(1)} %get-tuple-element.61), channel_id=1, source_target_pairs={{0,3},{1,2},{2,1},{3,0},{4,7},{5,6},{6,5},{7,4},{8,11},{9,10},{10,... | collective-permute-start | bytes 884744 | tf_op jit(solution)/shard_map/ppermute | solution.py:90
  50.6 1.9 %collective-permute-start.9 = (bf16[72,288]{1,0:T(8,128)(2,1)S(1)}, bf16[72,288]{1,0:T(8,128)(2,1)S(1)}, u32[]{:S(2)}, u32[]{:S(2)}) collective-permute-start(bf16[72,288]{1,0:T(8,128)(2,1)S(1)} %get-tuple-element.67), channel_id=1, source_target_pairs={{0,1},{1,0},{2,3},{3,2},{4,5},{5,4},{6,7},{7,6},{8,9},{9,8},{10,11... | collective-permute-start | bytes 124424 | tf_op jit(solution)/shard_map/ppermute | solution.py:90
  52.5 10.4 %collective-permute-start.14 = (bf16[72,576]{1,0:T(8,128)(2,1)S(1)}, bf16[72,576]{1,0:T(8,128)(2,1)S(1)}, u32[]{:S(2)}, u32[]{:S(2)}) collective-permute-start(bf16[72,576]{1,0:T(8,128)(2,1)S(1)} %add_convert_fusion), channel_id=1, source_target_pairs={{0,16},{4,20},{8,24},{12,28},{16,0},{20,4},{24,8},{28,12},{1,17},{... | collective-permute-start | bytes 248840 | tf_op jit(solution)/shard_map/ppermute | solution.py:380
  55.1 7.8 %collective-permute-start.15 = (bf16[72,576]{1,0:T(8,128)(2,1)S(1)}, bf16[72,576]{1,0:T(8,128)(2,1)S(1)}, u32[]{:S(2)}, u32[]{:S(2)}) collective-permute-start(bf16[72,576]{1,0:T(8,128)(2,1)S(1)} %add_convert_fusion), channel_id=1, source_target_pairs={{0,24},{4,28},{8,16},{12,20},{16,8},{20,12},{24,0},{28,4},{1,25},{... | collective-permute-start | bytes 248840 | tf_op jit(solution)/shard_map/ppermute | solution.py:380
  62.9 9.6 %collective-permute-start.20 = (bf16[288,512]{1,0:T(8,128)(2,1)S(1)}, bf16[288,512]{1,0:T(8,128)(2,1)S(1)}, u32[]{:S(2)}, u32[]{:S(2)}) collective-permute-start(bf16[288,512]{1,0:T(8,128)(2,1)S(1)} %get-tuple-element.80), channel_id=1, source_target_pairs={{0,1},{1,0},{2,3},{3,2},{4,5},{5,4},{6,7},{7,6},{8,9},{9,8},{10,11... | collective-permute-start | bytes 884744 | tf_op jit(solution)/shard_map/ppermute | solution.py:90
  62.9 10.5 %collective-permute-start.21 = (bf16[288,512]{1,0:T(8,128)(2,1)S(1)}, bf16[288,512]{1,0:T(8,128)(2,1)S(1)}, u32[]{:S(2)}, u32[]{:S(2)}) collective-permute-start(bf16[288,512]{1,0:T(8,128)(2,1)S(1)} %get-tuple-element.81), channel_id=1, source_target_pairs={{0,2},{1,3},{2,0},{3,1},{4,6},{5,7},{6,4},{7,5},{8,10},{9,11},{10,... | collective-permute-start | bytes 884744 | tf_op jit(solution)/shard_map/ppermute | solution.py:90
  63.9 14.2 %collective-permute-start.22 = (bf16[288,512]{1,0:T(8,128)(2,1)S(1)}, bf16[288,512]{1,0:T(8,128)(2,1)S(1)}, u32[]{:S(2)}, u32[]{:S(2)}) collective-permute-start(bf16[288,512]{1,0:T(8,128)(2,1)S(1)} %get-tuple-element.82), channel_id=1, source_target_pairs={{0,3},{1,2},{2,1},{3,0},{4,7},{5,6},{6,5},{7,4},{8,11},{9,10},{10,... | collective-permute-start | bytes 884744 | tf_op jit(solution)/shard_map/ppermute | solution.py:90
  71.3 7.9 %collective-permute-start.16 = (bf16[72,288]{1,0:T(8,128)(2,1)S(1)}, bf16[72,288]{1,0:T(8,128)(2,1)S(1)}, u32[]{:S(2)}, u32[]{:S(2)}) collective-permute-start(bf16[72,288]{1,0:T(8,128)(2,1)S(1)} %get-tuple-element.74), channel_id=1, source_target_pairs={{0,4},{4,0},{8,12},{12,8},{16,20},{20,16},{24,28},{28,24},{1,5},{5... | collective-permute-start | bytes 124424 | tf_op jit(solution)/shard_map/ppermute | solution.py:380
  72.5 7.8 %collective-permute-start.23 = (bf16[72,288]{1,0:T(8,128)(2,1)S(1)}, bf16[72,288]{1,0:T(8,128)(2,1)S(1)}, u32[]{:S(2)}, u32[]{:S(2)}) collective-permute-start(bf16[72,288]{1,0:T(8,128)(2,1)S(1)} %get-tuple-element.84), channel_id=1, source_target_pairs={{0,1},{1,0},{2,3},{3,2},{4,5},{5,4},{6,7},{7,6},{8,9},{9,8},{10,11... | collective-permute-start | bytes 124424 | tf_op jit(solution)/shard_map/ppermute | solution.py:90
  72.5 8.6 %collective-permute-start.24 = (bf16[72,288]{1,0:T(8,128)(2,1)S(1)}, bf16[72,288]{1,0:T(8,128)(2,1)S(1)}, u32[]{:S(2)}, u32[]{:S(2)}) collective-permute-start(bf16[72,288]{1,0:T(8,128)(2,1)S(1)} %get-tuple-element.85), channel_id=1, source_target_pairs={{0,2},{1,3},{2,0},{3,1},{4,6},{5,7},{6,4},{7,5},{8,10},{9,11},{10,... | collective-permute-start | bytes 124424 | tf_op jit(solution)/shard_map/ppermute | solution.py:90
  73.4 34.1 %collective-permute-start.29 = (bf16[288,512]{1,0:T(8,128)(2,1)S(1)}, bf16[288,512]{1,0:T(8,128)(2,1)S(1)}, u32[]{:S(2)}, u32[]{:S(2)}) collective-permute-start(bf16[288,512]{1,0:T(8,128)(2,1)S(1)} %get-tuple-element.96), channel_id=1, source_target_pairs={{0,1},{1,0},{2,3},{3,2},{4,5},{5,4},{6,7},{7,6},{8,9},{9,8},{10,11... | collective-permute-start | bytes 884744 | tf_op jit(solution)/shard_map/ppermute | solution.py:90
  78.1 30.5 %collective-permute-start.30 = (bf16[288,512]{1,0:T(8,128)(2,1)S(1)}, bf16[288,512]{1,0:T(8,128)(2,1)S(1)}, u32[]{:S(2)}, u32[]{:S(2)}) collective-permute-start(bf16[288,512]{1,0:T(8,128)(2,1)S(1)} %get-tuple-element.97), channel_id=1, source_target_pairs={{0,2},{1,3},{2,0},{3,1},{4,6},{5,7},{6,4},{7,5},{8,10},{9,11},{10,... | collective-permute-start | bytes 884744 | tf_op jit(solution)/shard_map/ppermute | solution.py:90
  79.2 29.4 %collective-permute-start.31 = (bf16[288,512]{1,0:T(8,128)(2,1)S(1)}, bf16[288,512]{1,0:T(8,128)(2,1)S(1)}, u32[]{:S(2)}, u32[]{:S(2)}) collective-permute-start(bf16[288,512]{1,0:T(8,128)(2,1)S(1)} %get-tuple-element.98), channel_id=1, source_target_pairs={{0,3},{1,2},{2,1},{3,0},{4,7},{5,6},{6,5},{7,4},{8,11},{9,10},{10,... | collective-permute-start | bytes 884744 | tf_op jit(solution)/shard_map/ppermute | solution.py:90
  80.3 14.8 %collective-permute-start.25 = (bf16[72,288]{1,0:T(8,128)(2,1)S(1)}, bf16[72,288]{1,0:T(8,128)(2,1)S(1)}, u32[]{:S(2)}, u32[]{:S(2)}) collective-permute-start(bf16[72,288]{1,0:T(8,128)(2,1)S(1)} %get-tuple-element.86), channel_id=1, source_target_pairs={{0,3},{1,2},{2,1},{3,0},{4,7},{5,6},{6,5},{7,4},{8,11},{9,10},{10,... | collective-permute-start | bytes 124424 | tf_op jit(solution)/shard_map/ppermute | solution.py:90
  81.0 17.5 %collective-permute-start.17 = (bf16[72,288]{1,0:T(8,128)(2,1)S(1)}, bf16[72,288]{1,0:T(8,128)(2,1)S(1)}, u32[]{:S(2)}, u32[]{:S(2)}) collective-permute-start(bf16[72,288]{1,0:T(8,128)(2,1)S(1)} %fusion), channel_id=1, source_target_pairs={{0,8},{4,12},{8,0},{12,4},{16,24},{20,28},{24,16},{28,20},{1,9},{5... | collective-permute-start | bytes 124424 | tf_op jit(solution)/shard_map/ppermute | solution.py:380
  95.1 10.1 %collective-permute-start.18 = (bf16[72,288]{1,0:T(8,128)(2,1)S(1)}, bf16[72,288]{1,0:T(8,128)(2,1)S(1)}, u32[]{:S(2)}, u32[]{:S(2)}) collective-permute-start(bf16[72,288]{1,0:T(8,128)(2,1)S(1)} %fusion), channel_id=1, source_target_pairs={{0,16},{4,20},{8,24},{12,28},{16,0},{20,4},{24,8},{28,12},{1,17},{... | collective-permute-start | bytes 124424 | tf_op jit(solution)/shard_map/ppermute | solution.py:380
  98.6 6.6 %collective-permute-start.19 = (bf16[72,288]{1,0:T(8,128)(2,1)S(1)}, bf16[72,288]{1,0:T(8,128)(2,1)S(1)}, u32[]{:S(2)}, u32[]{:S(2)}) collective-permute-start(bf16[72,288]{1,0:T(8,128)(2,1)S(1)} %fusion), channel_id=1, source_target_pairs={{0,24},{4,28},{8,16},{12,20},{16,8},{20,12},{24,0},{28,4},{1,25},{... | collective-permute-start | bytes 124424 | tf_op jit(solution)/shard_map/ppermute | solution.py:380
  106.7 3.7 %collective-permute-start.26 = (bf16[2,72,288]{2,1,0:T(8,128)(2,1)S(1)}, bf16[2,72,288]{2,1,0:T(8,128)(2,1)S(1)}, u32[]{:S(2)}, u32[]{:S(2)}) collective-permute-start(bf16[2,72,288]{2,1,0:T(8,128)(2,1)S(1)} %get-tuple-element.91), channel_id=1, source_target_pairs={{0,1},{1,0},{2,3},{3,2},{4,5},{5,4},{6,7},{7,6},{8,9},{9,8},{10,11... | collective-permute-start | bytes 248840 | tf_op jit(solution)/shard_map/ppermute | solution.py:90
  106.7 5.9 %collective-permute-start.27 = (bf16[2,72,288]{2,1,0:T(8,128)(2,1)S(1)}, bf16[2,72,288]{2,1,0:T(8,128)(2,1)S(1)}, u32[]{:S(2)}, u32[]{:S(2)}) collective-permute-start(bf16[2,72,288]{2,1,0:T(8,128)(2,1)S(1)} %get-tuple-element.92), channel_id=1, source_target_pairs={{0,2},{1,3},{2,0},{3,1},{4,6},{5,7},{6,4},{7,5},{8,10},{9,11},{10,... | collective-permute-start | bytes 248840 | tf_op jit(solution)/shard_map/ppermute | solution.py:90
  107.5 6.6 %collective-permute-start.28 = (bf16[2,72,288]{2,1,0:T(8,128)(2,1)S(1)}, bf16[2,72,288]{2,1,0:T(8,128)(2,1)S(1)}, u32[]{:S(2)}, u32[]{:S(2)}) collective-permute-start(bf16[2,72,288]{2,1,0:T(8,128)(2,1)S(1)} %get-tuple-element.93), channel_id=1, source_target_pairs={{0,3},{1,2},{2,1},{3,0},{4,7},{5,6},{6,5},{7,4},{8,11},{9,10},{10,... | collective-permute-start | bytes 248840 | tf_op jit(solution)/shard_map/ppermute | solution.py:90

commit v3 on v2

--- a/solution.py
+++ b/solution.py
@@ -95,12 +95,15 @@
     held[...] = project(x, w_ref[...]).reshape(held.shape)
 
 
-def probe_body(x_hbm, w_hbm, taps_hbm, *rest):
-    *outs, x_out, w_ref, taps_ref, x_ref, held, sems = rest
+def probe_body(x_hbm, w_hbm, k_hbm, taps_hbm, *rest):
+    *outs, x_out, w_ref, k_ref, key_ref, taps_ref, x_ref, held, sems = rest
     copies = [
         pltpu.make_async_copy(source, target, sems.at[i])
         for i, (source, target) in enumerate(
-            ((x_hbm, x_ref), (w_hbm, w_ref), (taps_hbm.at[pl.ds(0, 2)], taps_ref))
+            (
+                (x_hbm, x_ref), (w_hbm, w_ref), (k_hbm, k_ref),
+                (taps_hbm.at[pl.ds(0, 2)], taps_ref),
+            )
         )
     ]
     copies[0].start()
@@ -109,9 +112,12 @@
     x_out[...] = x_ref[...].astype(F32).astype(BF16)
     copies[1].wait()
     copies[2].start()
+    copies[3].start()
     project_groups(x_out[...], w_ref, held)
     hand_out(held, outs)
     copies[2].wait()
+    key_ref[...] = project(x_out[...], k_ref[...])
+    copies[3].wait()
 
 
 def query_body(x_ref, w_ref, *rest):
@@ -120,11 +126,10 @@
     hand_out(held, outs)
 
 
-def probe_pair_body(taps_hbm, x_ref, k_ref, v_ref, out_ref, taps_ref, sem):
+def probe_pair_body(taps_hbm, x_ref, v_ref, out_ref, taps_ref, sem):
     copy = pltpu.make_async_copy(taps_hbm.at[2], taps_ref, sem)
     copy.start()
-    out_ref[0] = project(x_ref[...], k_ref[...])
-    out_ref[1] = project(x_ref[...], v_ref[...])
+    out_ref[...] = project(x_ref[...], v_ref[...])
     copy.wait()
 
 
@@ -164,7 +169,7 @@
         out_ref[f * tokens : (f + 1) * tokens, :] = part.astype(out_ref.dtype)
 
 
-def state_body(near_ref, far_ref, embed_ref, dots, k_ref, v_ref, latent, both, *rest):
+def state_body(near_ref, far_ref, embed_ref, key_dots, value_dots, k_ref, v_ref, latent, both, *rest):
     *outs, state_ref, first_ref = rest
     groups = state_ref.shape[0]
     u = near_ref[...] + far_ref[...].astype(F32)
@@ -182,7 +187,7 @@
                 at = slice(f * SPAN, (f + 1) * SPAN)
                 kt, vt = both[0, rows, at], both[1, rows, at]
                 state = dot_nt(vt, kt)
-                moved = dot_nt(vt, dots[0, rows, at]) + dot_nt(dots[1, rows, at], kt)
+                moved = dot_nt(vt, key_dots[rows, at]) + dot_nt(value_dots[rows, at], kt)
                 blocks.append((packed_of(state), packed_of(moved)))
             for kind in range(2):
                 to = kind * share + half * PAIR
@@ -416,21 +421,21 @@
     grouped = (groups, share, tokens)
     held = pltpu.VMEM(grouped, BF16)
 
-    *query_dot, direction, q_near, two_taps = call(
+    *query_dot, direction, q_near, k_near, key_dot, two_taps = call(
         probe_body,
         [part] * groups
-        + [struct((tokens, D), BF16), struct(q_weight.shape, BF16), struct((2,) + taps.shape[1:], BF16)],
-        (probe_in.reshape(tokens, D), q_weight, taps), far=3,
-        scratch=[pltpu.VMEM((tokens, D), jnp.int32), held, pltpu.SemaphoreType.DMA((3,))],
+        + [struct((tokens, D), BF16), struct(q_weight.shape, BF16), struct(k_weight.shape, BF16), struct((D, tokens), BF16), struct((2,) + taps.shape[1:], BF16)],
+        (probe_in.reshape(tokens, D), q_weight, k_weight, taps), far=4,
+        scratch=[pltpu.VMEM((tokens, D), jnp.int32), held, pltpu.SemaphoreType.DMA((4,))],
         flops=2 * tokens * D * D, moved=weight_bytes + 8 * tokens * D,
     )
     query_dot = exchange(query_dot)
 
     far = conv(1, 0, two_taps, BF16)
     far = lax.ppermute(far, "tm", [(t, t + 1) for t in range(tms - 1)])
-    dots, last_tap = call(
-        probe_pair_body, [struct(two_tall, BF16), struct(taps.shape[1:], BF16)],
-        (taps, direction, k_weight, v_weight), far=1, scratch=[pltpu.SemaphoreType.DMA],
+    value_dot, last_tap = call(
+        probe_pair_body, [struct((D, tokens), BF16), struct(taps.shape[1:], BF16)],
+        (taps, direction, v_weight), far=1, scratch=[pltpu.SemaphoreType.DMA],
         flops=4 * tokens * D * D, moved=2 * weight_bytes + 6 * tokens * D,
     )
     near = conv(0, 1, last_tap, F32)
@@ -441,7 +446,7 @@
         state_body,
         [struct((tokens, D), BF16), struct(two_tall, BF16)] + [state_part] * groups
         + [struct((HEAD, share), BF16)] * (2 * groups),
-        (near, far, embed_weight, dots, k_weight, v_weight),
+        (near, far, embed_weight, key_dot, value_dot, k_near, v_weight),
         scratch=[
             pltpu.VMEM((groups,) + state_part.shape, BF16),
             pltpu.VMEM((2, groups, HEAD, share), BF16),
@@ -516,7 +521,7 @@
     )[0]
     adjoint = call(
         functools.partial(adjoint_body, groups), [struct((tokens, D), BF16)],
-        (*state_back, both, query_part, k_weight, v_weight),
+        (*state_back, both, query_part, k_near, v_weight),
         scratch=[pltpu.VMEM(two_tall, BF16), pltpu.VMEM((groups, frames, HEAD, share), BF16)],
         flops=4 * tokens * D * D, moved=2 * weight_bytes + 10 * tokens * D,
     )[0]

time: 120 us -> 122 us (1.017)
  waiting for transfers between devices: 34.7 us -> 36.3 us
    ppermute x1, waiting for transfers between devices: 1.17 us -> 2.83 us  [on_device(): far = lax.ppermute(far, 'tm', [(t, t + 1) for t in range(tms - 1)])]
where the time goes in v3:
time: 122 us
  Pallas kernels  45.5 us (37%)
  starting transfers between devices  38.6 us (32%)
  waiting for transfers between devices  36.3 us (30%)
    pallas_call x15, Pallas kernels, call(): pl.pallas_call(body, in_specs=[anywhere] * far + [vmem] * (len(args) - fa...  45.5 us
    ppermute x21, waiting for transfers between devices, exchange(): lax.ppermute(parts[k], 'space', [(i, i ^ k) for i in range(size)])  27 us
    ppermute x21, starting transfers between devices, exchange(): lax.ppermute(parts[k], 'space', [(i, i ^ k) for i in range(size)])  15.9 us
    ppermute x8, starting transfers between devices, scan_over(): gots.append(lax.ppermute(sent, axis, [(i, i ^ by) for i in range(size)]))  14.5 us
    ppermute x8, waiting for transfers between devices, scan_over(): gots.append(lax.ppermute(sent, axis, [(i, i ^ by) for i in range(size)]))  6.46 us
    ppermute x1, starting transfers between devices, on_device(): far = lax.ppermute(far, 'tm', [(t, t + 1) for t in range(tms - 1)])  4.42 us
    ppermute x1, waiting for transfers between devices, on_device(): far = lax.ppermute(far, 'tm', [(t, t + 1) for t in range(tms - 1)])  2.83 us
  transfers between devices with their start and end apart: 32, of which 10 were waited for; matrix products, arithmetic and copies ran while one was open for 0% of the time, Pallas kernels for 25%

profile of v3, /device:TPU:0, one launch (start us, length us, event | category | flops | bytes accessed | tf_op | source)
XLA Modules:
  0.0 122.1 jit_solution(271098029131312076)
XLA Ops:
  0.6 0.8 fusion.1
  1.5 2.4 %collective-permute-start = (bf16[2,1,32,384]{3,2,1,0:T(8,128)(2,1)S(1)}, bf16[2,1,32,384]{3,2,1,0:T(8,128)(2,1)S(1)}, u32[]{:S(2)}, u32[]{:S(2)}) collective-permute-start(bf16[2,1,32,384]{3,2,1,0:T(8,128)(2,1)S(1)} %get-tuple-element.105), channel_id=1, source_target_pairs={{0,1},{1,2},{2,3},{4,5},{5,6},{6,7},{8,9},{9,10},{10,11},{12,13},{... | collective-permute-start | bytes 147464 | tf_op jit(solution)/shard_map/ppermute | solution.py:405
  3.9 1.3 %collective-permute-start.1 = (bf16[2,1,32,384]{3,2,1,0:T(8,128)(2,1)S(1)}, bf16[2,1,32,384]{3,2,1,0:T(8,128)(2,1)S(1)}, u32[]{:S(2)}, u32[]{:S(2)}) collective-permute-start(bf16[2,1,32,384]{3,2,1,0:T(8,128)(2,1)S(1)} %get-tuple-element.104), channel_id=1, source_target_pairs={{1,0},{2,1},{3,2},{5,4},{6,5},{7,6},{9,8},{10,9},{11,10},{13,12},{... | collective-permute-start | bytes 147464 | tf_op jit(solution)/shard_map/ppermute | solution.py:406
  5.2 6.9 %shard_map.120 = (bf16[288,512]{1,0:T(8,128)(2,1)S(1)}, bf16[288,512]{1,0:T(8,128)(2,1)S(1)}, bf16[288,512]{1,0:T(8,128)(2,1)S(1)}, bf16[288,512]{1,0:T(8,128)(2...) custom-call(s32[512,1152]{1,0:T(8,128)} %bitcast.13, ...), custom_call_target="tpu_custom_call" | custom-call | flops 1358954496 | bytes 7372800 | tf_op jit(solution)/shard_map/pallas_call | solution.py:25
  12.2 3.0 %shard_map.123 = bf16[512,384]{1,0:T(8,128)(2,1)S(1)} custom-call(bf16[2,8,32,384]{3,2,1,0:T(8,128)(2,1)S(1)} %copy-done.2, bf16[2,1,32,384]{3,2,1,0:T(8,128)(2,1)S(1)} %collective-permute-done.up_ref, bf16[2,1,32,384]{3,2,1,0:T(8,128)(2,1)S(1)} %collective-permute-done.1.down_ref, bf16[2,3456,384]{2,1,0:T(8,128)(2,1)S(1)} %get-tuple-element.56.mid_ref.main_ref, ...), custom_call_target="tpu_custom_call" | custom-call | flops 2038431744 | bytes 5160960 | tf_op jit(solution)/shard_map/pallas_call | solution.py:25
  15.2 4.4 %collective-permute-start.2 = (bf16[512,384]{1,0:T(8,128)(2,1)S(1)}, bf16[512,384]{1,0:T(8,128)(2,1)S(1)}, u32[]{:S(2)}, u32[]{:S(2)}) collective-permute-start(bf16[512,384]{1,0:T(8,128)(2,1)S(1)} %shard_map.123), channel_id=1, source_target_pairs={{0,4},{4,8},{8,12},{12,16},{16,20},{20,24},{24,28},{1,5},{5,9},{9,... | collective-permute-start | bytes 1179656 | tf_op jit(solution)/shard_map/ppermute | solution.py:435
  19.6 2.0 %shard_map.121 = (bf16[1152,512]{1,0:T(8,128)(2,1)S(1)}, bf16[3456,384]{1,0:T(8,128)(2,1)S(1)}) custom-call(bf16[3,3456,384]{2,1,0:T(8,128)(2,1)} %bitcast.12, bf16[512,1152]{1,0:T(8,128)(2,1)S(1)} %get-tuple-element.54.x_ref, bf16[1152,1152]{1,0:T(8,128)(2,1)S(1)} %copy-done), custom_call_target="tpu_custom_call" | custom-call | flops 2717908992 | bytes 8847360 | tf_op jit(solution)/shard_map/pallas_call | solution.py:25
  21.6 3.0 %shard_map.122.near_ref = f32[512,384]{1,0:T(8,128)S(1)} custom-call(bf16[2,8,32,384]{3,2,1,0:T(8,128)(2,1)S(1)} %copy-done.2, bf16[2,1,32,384]{3,2,1,0:T(8,128)(2,1)S(1)} %collective-permute-done.up_ref, bf16[2,1,32,384]{3,2,1,0:T(8,128)(2,1)S(1)} %collective-permute-done.1.down_ref, bf16[3456,384]{1,0:T(8,128)(2,1)S(1)} %get-tuple-element.55.main_ref, ...), custom_call_target="tpu_custom_call" | custom-call | flops 2038431744 | bytes 5160960 | tf_op jit(solution)/shard_map/pallas_call | solution.py:25
  24.6 2.8 %collective-permute-done.2.far_ref = bf16[512,384]{1,0:T(8,128)(2,1)S(1)} collective-permute-done((bf16[512,384]{1,0:T(8,128)(2,1)S(1)}, bf16[512,384]{1,0:T(8,128)(2,1)S(1)}, u32[]{:S(2)}, u32[]{:S(2)}) %collective-permute-start.2) | collective-permute-done | bytes 393248 | tf_op jit(solution)/shard_map/ppermute | solution.py:435
  27.4 6.5 %shard_map.124 = (bf16[512,1152]{1,0:T(8,128)(2,1)S(1)}, bf16[2,1152,512]{2,1,0:T(8,128)(2,1)S(1)}, bf16[72,576]{1,0:T(8,128)(2,1)S(1)}, bf16[72,576]{1,0:T(8,12...) custom-call(f32[512,384]{1,0:T(8,128)S(1)} %shard_map.122.near_ref, ...), custom_call_target="tpu_custom_call" | custom-call | flops 2717908992 | bytes 13565952 | tf_op jit(solution)/shard_map/pallas_call | solution.py:25
  33.9 1.6 %collective-permute-start.6 = (bf16[72,576]{1,0:T(8,128)(2,1)S(1)}, bf16[72,576]{1,0:T(8,128)(2,1)S(1)}, u32[]{:S(2)}, u32[]{:S(2)}) collective-permute-start(bf16[72,576]{1,0:T(8,128)(2,1)S(1)} %get-tuple-element.67), channel_id=1, source_target_pairs={{0,1},{1,0},{2,3},{3,2},{4,5},{5,4},{6,7},{7,6},{8,9},{9,8},{10,11... | collective-permute-start | bytes 248840 | tf_op jit(solution)/shard_map/ppermute | solution.py:90
  35.5 1.8 %collective-permute-start.7 = (bf16[72,576]{1,0:T(8,128)(2,1)S(1)}, bf16[72,576]{1,0:T(8,128)(2,1)S(1)}, u32[]{:S(2)}, u32[]{:S(2)}) collective-permute-start(bf16[72,576]{1,0:T(8,128)(2,1)S(1)} %get-tuple-element.68), channel_id=1, source_target_pairs={{0,2},{1,3},{2,0},{3,1},{4,6},{5,7},{6,4},{7,5},{8,10},{9,11},{10,... | collective-permute-start | bytes 248840 | tf_op jit(solution)/shard_map/ppermute | solution.py:90
  37.4 3.5 %collective-permute-done.7.refs_2_.refs_6_.refs_10_ = bf16[72,576]{1,0:T(8,128)(2,1)S(1)} collective-permute-done((bf16[72,576]{1,0:T(8,128)(2,1)S(1)}, bf16[72,576]{1,0:T(8,128)(2,1)S(1)}, u32[]{:S(2)}, u32[]{:S(2)}) %collective-permute-start.7) | collective-permute-done | bytes 82976 | tf_op jit(solution)/shard_map/ppermute | solution.py:90
  40.9 1.4 %collective-permute-done.8.refs_3_.refs_7_.refs_11_ = bf16[72,576]{1,0:T(8,128)(2,1)S(1)} collective-permute-done((bf16[72,576]{1,0:T(8,128)(2,1)S(1)}, bf16[72,576]{1,0:T(8,128)(2,1)S(1)}, u32[]{:S(2)}, u32[]{:S(2)}) %collective-permute-start.8) | collective-permute-done | bytes 82976 | tf_op jit(solution)/shard_map/ppermute | solution.py:90
  42.4 2.6 %collective-permute-start.12 = (bf16[72,576]{1,0:T(8,128)(2,1)S(1)}, bf16[72,576]{1,0:T(8,128)(2,1)S(1)}, u32[]{:S(2)}, u32[]{:S(2)}) collective-permute-start(bf16[72,576]{1,0:T(8,128)(2,1)S(1)} %get-tuple-element.74.tie_ref), channel_id=1, source_target_pairs={{0,4},{4,0},{8,12},{12,8},{16,20},{20,16},{24,28},{28,24},{1,5},{5... | collective-permute-start | bytes 248840 | tf_op jit(solution)/shard_map/ppermute | solution.py:385
  44.9 2.1 %shard_map.125 = (bf16[288,512]{1,0:T(8,128)(2,1)S(1)}, bf16[288,512]{1,0:T(8,128)(2,1)S(1)}, bf16[288,512]{1,0:T(8,128)(2,1)S(1)}, bf16[288,512]{1,0:T(8,128)(2,1)S(1)}) custom-call(bf16[512,1152]{1,0:T(8,128)(2,1)S(1)} %get-tuple-element.60.x_ref, bf16[1152,1152]{1,0:T(8,128)(2,1)S(1)} %get-tuple-element.61.w_ref), custom_call_target="tpu_custom_call" | custom-call | flops 1358954496 | bytes 5013504 | tf_op jit(solution)/shard_map/pallas_call | solution.py:25
  47.1 1.5 %collective-permute-start.10 = (bf16[72,288]{1,0:T(8,128)(2,1)S(1)}, bf16[72,288]{1,0:T(8,128)(2,1)S(1)}, u32[]{:S(2)}, u32[]{:S(2)}) collective-permute-start(bf16[72,288]{1,0:T(8,128)(2,1)S(1)} %get-tuple-element.72), channel_id=1, source_target_pairs={{0,2},{1,3},{2,0},{3,1},{4,6},{5,7},{6,4},{7,5},{8,10},{9,11},{10,... | collective-permute-start | bytes 124424 | tf_op jit(solution)/shard_map/ppermute | solution.py:90
  48.6 0.3 collective-permute-start.11
  49.0 1.7 %collective-permute-start.13 = (bf16[72,576]{1,0:T(8,128)(2,1)S(1)}, bf16[72,576]{1,0:T(8,128)(2,1)S(1)}, u32[]{:S(2)}, u32[]{:S(2)}) collective-permute-start(bf16[72,576]{1,0:T(8,128)(2,1)S(1)} %add_convert_fusion), channel_id=1, source_target_pairs={{0,8},{4,12},{8,0},{12,4},{16,24},{20,28},{24,16},{28,20},{1,9},{5... | collective-permute-start | bytes 248840 | tf_op jit(solution)/shard_map/ppermute | solution.py:385
  50.7 1.7 %collective-permute-start.4 = (bf16[288,512]{1,0:T(8,128)(2,1)S(1)}, bf16[288,512]{1,0:T(8,128)(2,1)S(1)}, u32[]{:S(2)}, u32[]{:S(2)}) collective-permute-start(bf16[288,512]{1,0:T(8,128)(2,1)S(1)} %get-tuple-element.64), channel_id=1, source_target_pairs={{0,2},{1,3},{2,0},{3,1},{4,6},{5,7},{6,4},{7,5},{8,10},{9,11},{10,... | collective-permute-start | bytes 884744 | tf_op jit(solution)/shard_map/ppermute | solution.py:90
  52.5 1.0 collective-permute-start.9
  53.5 0.9 collective-permute-done.9.refs_9_
  54.4 2.6 %collective-permute-start.14 = (bf16[72,576]{1,0:T(8,128)(2,1)S(1)}, bf16[72,576]{1,0:T(8,128)(2,1)S(1)}, u32[]{:S(2)}, u32[]{:S(2)}) collective-permute-start(bf16[72,576]{1,0:T(8,128)(2,1)S(1)} %add_convert_fusion), channel_id=1, source_target_pairs={{0,16},{4,20},{8,24},{12,28},{16,0},{20,4},{24,8},{28,12},{1,17},{... | collective-permute-start | bytes 248840 | tf_op jit(solution)/shard_map/ppermute | solution.py:385
  57.0 1.3 %collective-permute-start.15 = (bf16[72,576]{1,0:T(8,128)(2,1)S(1)}, bf16[72,576]{1,0:T(8,128)(2,1)S(1)}, u32[]{:S(2)}, u32[]{:S(2)}) collective-permute-start(bf16[72,576]{1,0:T(8,128)(2,1)S(1)} %add_convert_fusion), channel_id=1, source_target_pairs={{0,24},{4,28},{8,16},{12,20},{16,8},{20,12},{24,0},{28,4},{1,25},{... | collective-permute-start | bytes 248840 | tf_op jit(solution)/shard_map/ppermute | solution.py:385
  58.3 6.4 %collective-permute-done.14.refs_14_.refs_18_ = bf16[72,576]{1,0:T(8,128)(2,1)S(1)} collective-permute-done((bf16[72,576]{1,0:T(8,128)(2,1)S(1)}, bf16[72,576]{1,0:T(8,128)(2,1)S(1)}, u32[]{:S(2)}, u32[]{:S(2)}) %collective-permute-start.14) | collective-permute-done | bytes 82976 | tf_op jit(solution)/shard_map/ppermute | solution.py:385
  64.8 1.1 collective-permute-start.21
  65.9 0.8 collective-permute-start.22
  66.7 1.1 shard_map.127.refs_17_
  67.8 5.4 %shard_map.128 = (bf16[288,512]{1,0:T(8,128)(2,1)S(1)}, bf16[288,512]{1,0:T(8,128)(2,1)S(1)}, bf16[288,512]{1,0:T(8,128)(2,1)S(1)}, bf16[288,512]{1,0:T(8,128)(2...) custom-call(bf16[288,512]{1,0:T(8,128)(2,1)S(1)} %get-tuple-element., ...), custom_call_target="tpu_custom_call" | custom-call | flops 1019215872 | bytes 5898240 | tf_op jit(solution)/shard_map/pallas_call | solution.py:25
  73.2 1.2 collective-permute-start.16
  74.4 0.9 collective-permute-start.24
  75.6 4.5 %collective-permute-done.22.refs_3_ = bf16[288,512]{1,0:T(8,128)(2,1)S(1)} collective-permute-done((bf16[288,512]{1,0:T(8,128)(2,1)S(1)}, bf16[288,512]{1,0:T(8,128)(2,1)S(1)}, u32[]{:S(2)}, u32[]{:S(2)}) %collective-permute-start.22) | collective-permute-done | bytes 294944 | tf_op jit(solution)/shard_map/ppermute | solution.py:90
  80.1 1.1 collective-permute-start.30
  81.1 1.0 collective-permute-start.31
  82.2 0.8 collective-permute-start.25
  83.0 1.1 collective-permute-start.17
  84.1 12.9 %collective-permute-done.25.refs_15_ = bf16[72,288]{1,0:T(8,128)(2,1)S(1)} collective-permute-done((bf16[72,288]{1,0:T(8,128)(2,1)S(1)}, bf16[72,288]{1,0:T(8,128)(2,1)S(1)}, u32[]{:S(2)}, u32[]{:S(2)}) %collective-permute-start.25) | collective-permute-done | bytes 41504 | tf_op jit(solution)/shard_map/ppermute | solution.py:90
  97.0 3.6 %collective-permute-start.18 = (bf16[72,288]{1,0:T(8,128)(2,1)S(1)}, bf16[72,288]{1,0:T(8,128)(2,1)S(1)}, u32[]{:S(2)}, u32[]{:S(2)}) collective-permute-start(bf16[72,288]{1,0:T(8,128)(2,1)S(1)} %fusion), channel_id=1, source_target_pairs={{0,16},{4,20},{8,24},{12,28},{16,0},{20,4},{24,8},{28,12},{1,17},{... | collective-permute-start | bytes 124424 | tf_op jit(solution)/shard_map/ppermute | solution.py:385
  100.6 0.4 collective-permute-start.19
  101.0 3.9 %shard_map.131 = bf16[2,4,256,288]{3,2,1,0:T(8,128)(2,1)} custom-call(bf16[288,512]{1,0:T(8,128)(2,1)S(1)} %get-tuple-element.83.refs_0_, bf16[288,512]{1,0:T(8,128)(2,1)S(1)} %collective-permute-done.20.refs_1_, bf16[288,512]{1,0:T(8,128)(2,1)S(1)} %collective-permute-done.21.refs_2_, bf16[288,512]{1,0:T(8,128)(2,1)S(1)} %collective-permute-done.22.refs_3_, ...), custom_call_target="tpu_custom_call" | custom-call | flops 1019215872 | bytes 5898240 | tf_op jit(solution)/shard_map/pallas_call | solution.py:25
  104.9 2.3 %shard_map.129 = bf16[2,4,256,288]{3,2,1,0:T(8,128)(2,1)} custom-call(bf16[2,4,288,256]{3,2,1,0:T(8,128)(2,1)S(1)} %get-tuple-element.76.unit_ref.refs_21_), custom_call_target="tpu_custom_call" | custom-call | bytes 2359296 | tf_op jit(solution)/shard_map/pallas_call | solution.py:25
  107.3 1.5 %shard_map.134 = f32[8,4,72,72]{3,2,1,0:T(8,128)} custom-call(f32[4,2,72,288]{3,2,1,0:T(8,128)S(1)} %get-tuple-element.77.suffix_ref, f32[72,288]{1,0:T(8,128)S(1)} %get-tuple-element.103.after_ref), custom_call_target="tpu_custom_call" | custom-call | bytes 1658880 | tf_op jit(solution)/shard_map/pallas_call | solution.py:25
  108.8 1.0 collective-permute-start.27
  109.7 0.9 collective-permute-start.28
  110.6 1.8 %shard_map.132.refs_5_ = f32[1152,512]{1,0:T(8,128)S(1)} custom-call(bf16[1152,1152]{1,0:T(8,128)(2,1)S(1)} %get-tuple-element.61.w_ref, bf16[288,512]{1,0:T(8,128)(2,1)S(1)} %get-tuple-element.99.refs_0_, bf16[288,512]{1,0:T(8,128)(2,1)S(1)} %collective-permute-done.29.refs_1_, bf16[288,512]{1,0:T(8,128)(2,1)S(1)} %collective-permute-done.30.refs_2_, ...), custom_call_target="tpu_custom_call" | custom-call | flops 1358954496 | bytes 6193152 | tf_op jit(solution)/shard_map/pallas_call | solution.py:25
  112.4 2.3 %collective-permute-done.27.refs_2_ = bf16[2,72,288]{2,1,0:T(8,128)(2,1)S(1)} collective-permute-done((bf16[2,72,288]{2,1,0:T(8,128)(2,1)S(1)}, bf16[2,72,288]{2,1,0:T(8,128)(2,1)S(1)}, u32[]{:S(2)}, u32[]{:S(2)}) %collective-permute-start.27) | collective-permute-done | bytes 82976 | tf_op jit(solution)/shard_map/ppermute | solution.py:90
  114.7 1.4 %collective-permute-done.28.refs_3_ = bf16[2,72,288]{2,1,0:T(8,128)(2,1)S(1)} collective-permute-done((bf16[2,72,288]{2,1,0:T(8,128)(2,1)S(1)}, bf16[2,72,288]{2,1,0:T(8,128)(2,1)S(1)}, u32[]{:S(2)}, u32[]{:S(2)}) %collective-permute-start.28) | collective-permute-done | bytes 82976 | tf_op jit(solution)/shard_map/ppermute | solution.py:90
  116.1 6.0 %shard_map.133 = bf16[512,1152]{1,0:T(8,128)(2,1)} custom-call(bf16[2,72,288]{2,1,0:T(8,128)(2,1)S(1)} %get-tuple-element.94.refs_0_, bf16[2,72,288]{2,1,0:T(8,128)(2,1)S(1)} %collective-permute-done.26.refs_1_, bf16[2,72,288]{2,1,0:T(8,128)(2,1)S(1)} %collective-permute-done.27.refs_2_, bf16[2,72,288]{2,1,0:T(8,128)(2,1)S(1)} %collective-permute-done.28.refs_3_, ...), custom_call_target="tpu_custom_call" | custom-call | flops 2717908992 | bytes 11206656 | tf_op jit(solution)/shard_map/pallas_call | solution.py:25
  (44 shorter events, 0.7 us)
Async XLA Ops:
  1.5 10.7 %collective-permute-start = (bf16[2,1,32,384]{3,2,1,0:T(8,128)(2,1)S(1)}, bf16[2,1,32,384]{3,2,1,0:T(8,128)(2,1)S(1)}, u32[]{:S(2)}, u32[]{:S(2)}) collective-permute-start(bf16[2,1,32,384]{3,2,1,0:T(8,128)(2,1)S(1)} %get-tuple-element.105), channel_id=1, source_target_pairs={{0,1},{1,2},{2,3},{4,5},{5,6},{6,7},{8,9},{9,10},{10,11},{12,13},{... | collective-permute-start | bytes 147464 | tf_op jit(solution)/shard_map/ppermute | solution.py:405
  3.9 8.3 %collective-permute-start.1 = (bf16[2,1,32,384]{3,2,1,0:T(8,128)(2,1)S(1)}, bf16[2,1,32,384]{3,2,1,0:T(8,128)(2,1)S(1)}, u32[]{:S(2)}, u32[]{:S(2)}) collective-permute-start(bf16[2,1,32,384]{3,2,1,0:T(8,128)(2,1)S(1)} %get-tuple-element.104), channel_id=1, source_target_pairs={{1,0},{2,1},{3,2},{5,4},{6,5},{7,6},{9,8},{10,9},{11,10},{13,12},{... | collective-permute-start | bytes 147464 | tf_op jit(solution)/shard_map/ppermute | solution.py:406
  5.2 7.0 %copy-start.2 = (bf16[2,8,32,384]{3,2,1,0:T(8,128)(2,1)S(1)}, bf16[2,8,32,384]{3,2,1,0:T(8,128)(2,1)}, u32[]{:S(2)}) copy-start(bf16[2,8,32,384]{3,2,1,0:T(8,128)(2,1)} %own_ref.3) | copy-start | bytes 1179652
  12.2 7.4 %copy-start = (bf16[1152,1152]{1,0:T(8,128)(2,1)S(1)}, bf16[1152,1152]{1,0:T(8,128)(2,1)}, u32[]{:S(2)}) copy-start(bf16[1152,1152]{1,0:T(8,128)(2,1)} %refs_7_.1) | copy-start | bytes 7962628
  15.2 12.2 %collective-permute-start.2 = (bf16[512,384]{1,0:T(8,128)(2,1)S(1)}, bf16[512,384]{1,0:T(8,128)(2,1)S(1)}, u32[]{:S(2)}, u32[]{:S(2)}) collective-permute-start(bf16[512,384]{1,0:T(8,128)(2,1)S(1)} %shard_map.123), channel_id=1, source_target_pairs={{0,4},{4,8},{8,12},{12,16},{16,20},{20,24},{24,28},{1,5},{5,9},{9,... | collective-permute-start | bytes 1179656 | tf_op jit(solution)/shard_map/ppermute | solution.py:435
  21.6 5.9 %copy-start.3 = (bf16[384,1152]{1,0:T(8,128)(2,1)S(1)}, bf16[384,1152]{1,0:T(8,128)(2,1)}, u32[]{:S(2)}) copy-start(bf16[384,1152]{1,0:T(8,128)(2,1)} %embed_ref.1) | copy-start | bytes 2654212
  33.9 3.5 %collective-permute-start.6 = (bf16[72,576]{1,0:T(8,128)(2,1)S(1)}, bf16[72,576]{1,0:T(8,128)(2,1)S(1)}, u32[]{:S(2)}, u32[]{:S(2)}) collective-permute-start(bf16[72,576]{1,0:T(8,128)(2,1)S(1)} %get-tuple-element.67), channel_id=1, source_target_pairs={{0,1},{1,0},{2,3},{3,2},{4,5},{5,4},{6,7},{7,6},{8,9},{9,8},{10,11... | collective-permute-start | bytes 248840 | tf_op jit(solution)/shard_map/ppermute | solution.py:90
  35.5 5.3 %collective-permute-start.7 = (bf16[72,576]{1,0:T(8,128)(2,1)S(1)}, bf16[72,576]{1,0:T(8,128)(2,1)S(1)}, u32[]{:S(2)}, u32[]{:S(2)}) collective-permute-start(bf16[72,576]{1,0:T(8,128)(2,1)S(1)} %get-tuple-element.68), channel_id=1, source_target_pairs={{0,2},{1,3},{2,0},{3,1},{4,6},{5,7},{6,4},{7,5},{8,10},{9,11},{10,... | collective-permute-start | bytes 248840 | tf_op jit(solution)/shard_map/ppermute | solution.py:90
  37.4 5.0 %collective-permute-start.8 = (bf16[72,576]{1,0:T(8,128)(2,1)S(1)}, bf16[72,576]{1,0:T(8,128)(2,1)S(1)}, u32[]{:S(2)}, u32[]{:S(2)}) collective-permute-start(bf16[72,576]{1,0:T(8,128)(2,1)S(1)} %get-tuple-element.69), channel_id=1, source_target_pairs={{0,3},{1,2},{2,1},{3,0},{4,7},{5,6},{6,5},{7,4},{8,11},{9,10},{10,... | collective-permute-start | bytes 248840 | tf_op jit(solution)/shard_map/ppermute | solution.py:90
  42.4 6.6 %collective-permute-start.12 = (bf16[72,576]{1,0:T(8,128)(2,1)S(1)}, bf16[72,576]{1,0:T(8,128)(2,1)S(1)}, u32[]{:S(2)}, u32[]{:S(2)}) collective-permute-start(bf16[72,576]{1,0:T(8,128)(2,1)S(1)} %get-tuple-element.74.tie_ref), channel_id=1, source_target_pairs={{0,4},{4,0},{8,12},{12,8},{16,20},{20,16},{24,28},{28,24},{1,5},{5... | collective-permute-start | bytes 248840 | tf_op jit(solution)/shard_map/ppermute | solution.py:385
  44.9 21.7 %copy-start.1 = (s32[2,32,32,288]{3,2,1,0:T(8,128)S(1)}, s32[2,32,32,288]{3,2,1,0:T(8,128)}, u32[]{:S(2)}) copy-start(s32[2,32,32,288]{3,2,1,0:T(8,128)} %param.17) | copy-start | bytes 7077892
  47.0 18.8 %collective-permute-start.3 = (bf16[288,512]{1,0:T(8,128)(2,1)S(1)}, bf16[288,512]{1,0:T(8,128)(2,1)S(1)}, u32[]{:S(2)}, u32[]{:S(2)}) collective-permute-start(bf16[288,512]{1,0:T(8,128)(2,1)S(1)} %get-tuple-element.63), channel_id=1, source_target_pairs={{0,1},{1,0},{2,3},{3,2},{4,5},{5,4},{6,7},{7,6},{8,9},{9,8},{10,11... | collective-permute-start | bytes 884744 | tf_op jit(solution)/shard_map/ppermute | solution.py:90
  47.1 5.3 %collective-permute-start.10 = (bf16[72,288]{1,0:T(8,128)(2,1)S(1)}, bf16[72,288]{1,0:T(8,128)(2,1)S(1)}, u32[]{:S(2)}, u32[]{:S(2)}) collective-permute-start(bf16[72,288]{1,0:T(8,128)(2,1)S(1)} %get-tuple-element.72), channel_id=1, source_target_pairs={{0,2},{1,3},{2,0},{3,1},{4,6},{5,7},{6,4},{7,5},{8,10},{9,11},{10,... | collective-permute-start | bytes 124424 | tf_op jit(solution)/shard_map/ppermute | solution.py:90
  48.6 3.9 %collective-permute-start.11 = (bf16[72,288]{1,0:T(8,128)(2,1)S(1)}, bf16[72,288]{1,0:T(8,128)(2,1)S(1)}, u32[]{:S(2)}, u32[]{:S(2)}) collective-permute-start(bf16[72,288]{1,0:T(8,128)(2,1)S(1)} %get-tuple-element.73), channel_id=1, source_target_pairs={{0,3},{1,2},{2,1},{3,0},{4,7},{5,6},{6,5},{7,4},{8,11},{9,10},{10,... | collective-permute-start | bytes 124424 | tf_op jit(solution)/shard_map/ppermute | solution.py:90
  49.0 18.8 %copy-start.4 = (f32[4,72,72]{2,1,0:T(8,128)S(1)}, f32[4,72,72]{2,1,0:T(8,128)}, u32[]{:S(2)}) copy-start(f32[4,72,72]{2,1,0:T(8,128)} %refs_16_.1) | copy-start | bytes 248836
  49.0 8.0 %collective-permute-start.13 = (bf16[72,576]{1,0:T(8,128)(2,1)S(1)}, bf16[72,576]{1,0:T(8,128)(2,1)S(1)}, u32[]{:S(2)}, u32[]{:S(2)}) collective-permute-start(bf16[72,576]{1,0:T(8,128)(2,1)S(1)} %add_convert_fusion), channel_id=1, source_target_pairs={{0,8},{4,12},{8,0},{12,4},{16,24},{20,28},{24,16},{28,20},{1,9},{5... | collective-permute-start | bytes 248840 | tf_op jit(solution)/shard_map/ppermute | solution.py:385
  50.7 17.1 %collective-permute-start.4 = (bf16[288,512]{1,0:T(8,128)(2,1)S(1)}, bf16[288,512]{1,0:T(8,128)(2,1)S(1)}, u32[]{:S(2)}, u32[]{:S(2)}) collective-permute-start(bf16[288,512]{1,0:T(8,128)(2,1)S(1)} %get-tuple-element.64), channel_id=1, source_target_pairs={{0,2},{1,3},{2,0},{3,1},{4,6},{5,7},{6,4},{7,5},{8,10},{9,11},{10,... | collective-permute-start | bytes 884744 | tf_op jit(solution)/shard_map/ppermute | solution.py:90
  52.4 15.4 %collective-permute-start.5 = (bf16[288,512]{1,0:T(8,128)(2,1)S(1)}, bf16[288,512]{1,0:T(8,128)(2,1)S(1)}, u32[]{:S(2)}, u32[]{:S(2)}) collective-permute-start(bf16[288,512]{1,0:T(8,128)(2,1)S(1)} %get-tuple-element.65), channel_id=1, source_target_pairs={{0,3},{1,2},{2,1},{3,0},{4,7},{5,6},{6,5},{7,4},{8,11},{9,10},{10,... | collective-permute-start | bytes 884744 | tf_op jit(solution)/shard_map/ppermute | solution.py:90
  52.5 1.9 %collective-permute-start.9 = (bf16[72,288]{1,0:T(8,128)(2,1)S(1)}, bf16[72,288]{1,0:T(8,128)(2,1)S(1)}, u32[]{:S(2)}, u32[]{:S(2)}) collective-permute-start(bf16[72,288]{1,0:T(8,128)(2,1)S(1)} %get-tuple-element.71), channel_id=1, source_target_pairs={{0,1},{1,0},{2,3},{3,2},{4,5},{5,4},{6,7},{7,6},{8,9},{9,8},{10,11... | collective-permute-start | bytes 124424 | tf_op jit(solution)/shard_map/ppermute | solution.py:90
  54.4 10.4 %collective-permute-start.14 = (bf16[72,576]{1,0:T(8,128)(2,1)S(1)}, bf16[72,576]{1,0:T(8,128)(2,1)S(1)}, u32[]{:S(2)}, u32[]{:S(2)}) collective-permute-start(bf16[72,576]{1,0:T(8,128)(2,1)S(1)} %add_convert_fusion), channel_id=1, source_target_pairs={{0,16},{4,20},{8,24},{12,28},{16,0},{20,4},{24,8},{28,12},{1,17},{... | collective-permute-start | bytes 248840 | tf_op jit(solution)/shard_map/ppermute | solution.py:385
  57.0 7.8 %collective-permute-start.15 = (bf16[72,576]{1,0:T(8,128)(2,1)S(1)}, bf16[72,576]{1,0:T(8,128)(2,1)S(1)}, u32[]{:S(2)}, u32[]{:S(2)}) collective-permute-start(bf16[72,576]{1,0:T(8,128)(2,1)S(1)} %add_convert_fusion), channel_id=1, source_target_pairs={{0,24},{4,28},{8,16},{12,20},{16,8},{20,12},{24,0},{28,4},{1,25},{... | collective-permute-start | bytes 248840 | tf_op jit(solution)/shard_map/ppermute | solution.py:385
  64.8 9.6 %collective-permute-start.20 = (bf16[288,512]{1,0:T(8,128)(2,1)S(1)}, bf16[288,512]{1,0:T(8,128)(2,1)S(1)}, u32[]{:S(2)}, u32[]{:S(2)}) collective-permute-start(bf16[288,512]{1,0:T(8,128)(2,1)S(1)} %get-tuple-element.84), channel_id=1, source_target_pairs={{0,1},{1,0},{2,3},{3,2},{4,5},{5,4},{6,7},{7,6},{8,9},{9,8},{10,11... | collective-permute-start | bytes 884744 | tf_op jit(solution)/shard_map/ppermute | solution.py:90
  64.8 10.6 %collective-permute-start.21 = (bf16[288,512]{1,0:T(8,128)(2,1)S(1)}, bf16[288,512]{1,0:T(8,128)(2,1)S(1)}, u32[]{:S(2)}, u32[]{:S(2)}) collective-permute-start(bf16[288,512]{1,0:T(8,128)(2,1)S(1)} %get-tuple-element.85), channel_id=1, source_target_pairs={{0,2},{1,3},{2,0},{3,1},{4,6},{5,7},{6,4},{7,5},{8,10},{9,11},{10,... | collective-permute-start | bytes 884744 | tf_op jit(solution)/shard_map/ppermute | solution.py:90
  65.9 14.2 %collective-permute-start.22 = (bf16[288,512]{1,0:T(8,128)(2,1)S(1)}, bf16[288,512]{1,0:T(8,128)(2,1)S(1)}, u32[]{:S(2)}, u32[]{:S(2)}) collective-permute-start(bf16[288,512]{1,0:T(8,128)(2,1)S(1)} %get-tuple-element.86), channel_id=1, source_target_pairs={{0,3},{1,2},{2,1},{3,0},{4,7},{5,6},{6,5},{7,4},{8,11},{9,10},{10,... | collective-permute-start | bytes 884744 | tf_op jit(solution)/shard_map/ppermute | solution.py:90
  73.2 7.9 %collective-permute-start.16 = (bf16[72,288]{1,0:T(8,128)(2,1)S(1)}, bf16[72,288]{1,0:T(8,128)(2,1)S(1)}, u32[]{:S(2)}, u32[]{:S(2)}) collective-permute-start(bf16[72,288]{1,0:T(8,128)(2,1)S(1)} %get-tuple-element.78), channel_id=1, source_target_pairs={{0,4},{4,0},{8,12},{12,8},{16,20},{20,16},{24,28},{28,24},{1,5},{5... | collective-permute-start | bytes 124424 | tf_op jit(solution)/shard_map/ppermute | solution.py:385
  74.4 7.8 %collective-permute-start.23 = (bf16[72,288]{1,0:T(8,128)(2,1)S(1)}, bf16[72,288]{1,0:T(8,128)(2,1)S(1)}, u32[]{:S(2)}, u32[]{:S(2)}) collective-permute-start(bf16[72,288]{1,0:T(8,128)(2,1)S(1)} %get-tuple-element.88), channel_id=1, source_target_pairs={{0,1},{1,0},{2,3},{3,2},{4,5},{5,4},{6,7},{7,6},{8,9},{9,8},{10,11... | collective-permute-start | bytes 124424 | tf_op jit(solution)/shard_map/ppermute | solution.py:90
  74.4 8.6 %collective-permute-start.24 = (bf16[72,288]{1,0:T(8,128)(2,1)S(1)}, bf16[72,288]{1,0:T(8,128)(2,1)S(1)}, u32[]{:S(2)}, u32[]{:S(2)}) collective-permute-start(bf16[72,288]{1,0:T(8,128)(2,1)S(1)} %get-tuple-element.89), channel_id=1, source_target_pairs={{0,2},{1,3},{2,0},{3,1},{4,6},{5,7},{6,4},{7,5},{8,10},{9,11},{10,... | collective-permute-start | bytes 124424 | tf_op jit(solution)/shard_map/ppermute | solution.py:90
  75.4 34.4 %collective-permute-start.29 = (bf16[288,512]{1,0:T(8,128)(2,1)S(1)}, bf16[288,512]{1,0:T(8,128)(2,1)S(1)}, u32[]{:S(2)}, u32[]{:S(2)}) collective-permute-start(bf16[288,512]{1,0:T(8,128)(2,1)S(1)} %get-tuple-element.100), channel_id=1, source_target_pairs={{0,1},{1,0},{2,3},{3,2},{4,5},{5,4},{6,7},{7,6},{8,9},{9,8},{10,11... | collective-permute-start | bytes 884744 | tf_op jit(solution)/shard_map/ppermute | solution.py:90
  80.1 30.6 %collective-permute-start.30 = (bf16[288,512]{1,0:T(8,128)(2,1)S(1)}, bf16[288,512]{1,0:T(8,128)(2,1)S(1)}, u32[]{:S(2)}, u32[]{:S(2)}) collective-permute-start(bf16[288,512]{1,0:T(8,128)(2,1)S(1)} %get-tuple-element.101), channel_id=1, source_target_pairs={{0,2},{1,3},{2,0},{3,1},{4,6},{5,7},{6,4},{7,5},{8,10},{9,11},{10,... | collective-permute-start | bytes 884744 | tf_op jit(solution)/shard_map/ppermute | solution.py:90
  81.1 29.5 %collective-permute-start.31 = (bf16[288,512]{1,0:T(8,128)(2,1)S(1)}, bf16[288,512]{1,0:T(8,128)(2,1)S(1)}, u32[]{:S(2)}, u32[]{:S(2)}) collective-permute-start(bf16[288,512]{1,0:T(8,128)(2,1)S(1)} %get-tuple-element.102), channel_id=1, source_target_pairs={{0,3},{1,2},{2,1},{3,0},{4,7},{5,6},{6,5},{7,4},{8,11},{9,10},{10,... | collective-permute-start | bytes 884744 | tf_op jit(solution)/shard_map/ppermute | solution.py:90
  82.2 14.8 %collective-permute-start.25 = (bf16[72,288]{1,0:T(8,128)(2,1)S(1)}, bf16[72,288]{1,0:T(8,128)(2,1)S(1)}, u32[]{:S(2)}, u32[]{:S(2)}) collective-permute-start(bf16[72,288]{1,0:T(8,128)(2,1)S(1)} %get-tuple-element.90), channel_id=1, source_target_pairs={{0,3},{1,2},{2,1},{3,0},{4,7},{5,6},{6,5},{7,4},{8,11},{9,10},{10,... | collective-permute-start | bytes 124424 | tf_op jit(solution)/shard_map/ppermute | solution.py:90
  83.0 17.6 %collective-permute-start.17 = (bf16[72,288]{1,0:T(8,128)(2,1)S(1)}, bf16[72,288]{1,0:T(8,128)(2,1)S(1)}, u32[]{:S(2)}, u32[]{:S(2)}) collective-permute-start(bf16[72,288]{1,0:T(8,128)(2,1)S(1)} %fusion), channel_id=1, source_target_pairs={{0,8},{4,12},{8,0},{12,4},{16,24},{20,28},{24,16},{28,20},{1,9},{5... | collective-permute-start | bytes 124424 | tf_op jit(solution)/shard_map/ppermute | solution.py:385
  97.0 10.2 %collective-permute-start.18 = (bf16[72,288]{1,0:T(8,128)(2,1)S(1)}, bf16[72,288]{1,0:T(8,128)(2,1)S(1)}, u32[]{:S(2)}, u32[]{:S(2)}) collective-permute-start(bf16[72,288]{1,0:T(8,128)(2,1)S(1)} %fusion), channel_id=1, source_target_pairs={{0,16},{4,20},{8,24},{12,28},{16,0},{20,4},{24,8},{28,12},{1,17},{... | collective-permute-start | bytes 124424 | tf_op jit(solution)/shard_map/ppermute | solution.py:385
  100.6 6.6 %collective-permute-start.19 = (bf16[72,288]{1,0:T(8,128)(2,1)S(1)}, bf16[72,288]{1,0:T(8,128)(2,1)S(1)}, u32[]{:S(2)}, u32[]{:S(2)}) collective-permute-start(bf16[72,288]{1,0:T(8,128)(2,1)S(1)} %fusion), channel_id=1, source_target_pairs={{0,24},{4,28},{8,16},{12,20},{16,8},{20,12},{24,0},{28,4},{1,25},{... | collective-permute-start | bytes 124424 | tf_op jit(solution)/shard_map/ppermute | solution.py:385
  108.8 3.7 %collective-permute-start.26 = (bf16[2,72,288]{2,1,0:T(8,128)(2,1)S(1)}, bf16[2,72,288]{2,1,0:T(8,128)(2,1)S(1)}, u32[]{:S(2)}, u32[]{:S(2)}) collective-permute-start(bf16[2,72,288]{2,1,0:T(8,128)(2,1)S(1)} %get-tuple-element.95), channel_id=1, source_target_pairs={{0,1},{1,0},{2,3},{3,2},{4,5},{5,4},{6,7},{7,6},{8,9},{9,8},{10,11... | collective-permute-start | bytes 248840 | tf_op jit(solution)/shard_map/ppermute | solution.py:90
  108.8 5.9 %collective-permute-start.27 = (bf16[2,72,288]{2,1,0:T(8,128)(2,1)S(1)}, bf16[2,72,288]{2,1,0:T(8,128)(2,1)S(1)}, u32[]{:S(2)}, u32[]{:S(2)}) collective-permute-start(bf16[2,72,288]{2,1,0:T(8,128)(2,1)S(1)} %get-tuple-element.96), channel_id=1, source_target_pairs={{0,2},{1,3},{2,0},{3,1},{4,6},{5,7},{6,4},{7,5},{8,10},{9,11},{10,... | collective-permute-start | bytes 248840 | tf_op jit(solution)/shard_map/ppermute | solution.py:90
  109.7 6.4 %collective-permute-start.28 = (bf16[2,72,288]{2,1,0:T(8,128)(2,1)S(1)}, bf16[2,72,288]{2,1,0:T(8,128)(2,1)S(1)}, u32[]{:S(2)}, u32[]{:S(2)}) collective-permute-start(bf16[2,72,288]{2,1,0:T(8,128)(2,1)S(1)} %get-tuple-element.97), channel_id=1, source_target_pairs={{0,3},{1,2},{2,1},{3,0},{4,7},{5,6},{6,5},{7,4},{8,11},{9,10},{10,... | collective-permute-start | bytes 248840 | tf_op jit(solution)/shard_map/ppermute | solution.py:90
